TPU v7x, 512 devices: a whole 4x8x8 slice. The times are simulated.
512 devices in a mesh: dp: 16 (over y, core), seq: 32 (over z, x).
Axes of the slice: x: 4, y: 8, z: 8, core: 2. Of those that a mesh axis runs over, the one named last changes fastest.
Arguments:
- query: bfloat16 [65536, 1536], P(('dp', 'seq')), may hold values from -100 to 100
- key: bfloat16 [65536, 1536], P(('dp', 'seq')), may hold values from -5 to 5
- value: bfloat16 [65536, 1536], P(('dp', 'seq')), may hold values from -6 to 6
- text: bfloat16 [4096, 512], P(('dp', 'seq')), may hold values from -6 to 6
- cond_weight: bfloat16 [512, 1536], P(('dp', 'seq')), may hold values from -0.25 to 0.25
- cotangent: bfloat16 [65536, 1536], P(('dp', 'seq')), may hold values from -6 to 6
- dest: int32 [65536], P(('dp', 'seq')), may hold values from 0 to 8191, as said below
- segment: int32 [131072], P(('dp', 'seq')), may hold values from -1 to 8191, as said below
- align: int32 [65536], P(('dp', 'seq')), may hold values from 0 to 255
Outputs:
- attended: bfloat16 [65536, 1536], P(('dp', 'seq'))
- query_grad: bfloat16 [65536, 1536], P(('dp', 'seq'))
- key_grad: bfloat16 [65536, 1536], P(('dp', 'seq'))
- value_grad: bfloat16 [65536, 1536], P(('dp', 'seq'))
- text_grad: float32 [4096, 512], P(('dp', 'seq'))
- weight_grad: float32 [512, 1536], P(('dp', 'seq'))
Inputs may be any that keep to these rules, and one draw needn't show every extreme that they name: `dest`: within each batch the entries are distinct; every device sends exactly 8 frames to each of exactly 16 owners; an owner's used slots are 0 upwards without gaps, either none or 192 to 256 of them; some owner of every batch has all 256 slots used and some none. `segment`: -1 exactly on unused slots; an utterance's slots are consecutive and lie on one owner; ids are distinct across owners.
All inputs are finite; a program needn't handle non-finite values.
Results may differ from a plain program's by a relative error of at most 0.013.
Values may be sent and summed in bfloat16 or wider, within the bound.
No kernel may reach another device: no remote copies, remote signals or barrier semaphores. Data moves between devices by JAX's collectives and lax.ppermute only.
A program may use at most 64 MiB of HBM per device.

v0:
```python
import jax
import jax.numpy as jnp
from jax import lax
from jax.sharding import PartitionSpec as P

HEADS = 12


def attend(queries, keys, values, cotangents, labels):
    slots = queries.shape[0]
    width = queries.shape[1]
    size = width // HEADS
    scale = size ** (-0.5)
    qheads = queries.reshape(slots, HEADS, size)
    kheads = keys.reshape(slots, HEADS, size)
    vheads = values.reshape(slots, HEADS, size)
    gheads = cotangents.reshape(slots, HEADS, size)
    index = jnp.arange(slots)
    allowed = (labels[:, None] == labels[None, :]) & (labels[:, None] >= 0) | (
        index[:, None] == index[None, :]
    )
    scores = jnp.einsum("qhd,khd->hqk", qheads, kheads, preferred_element_type=jnp.float32) * scale
    scores = jnp.where(allowed[None], scores, -1e30)
    top = jnp.max(scores, axis=2, keepdims=True)
    expos = jnp.exp(scores - top)
    probs = expos / jnp.sum(expos, axis=2, keepdims=True)
    weights = probs.astype(jnp.bfloat16)
    outputs = jnp.einsum(
        "hqk,khd->qhd", weights, vheads, preferred_element_type=jnp.float32
    ).astype(jnp.bfloat16)
    value_part = jnp.einsum(
        "hqk,qhd->khd", weights, gheads, preferred_element_type=jnp.float32
    ).astype(jnp.bfloat16)
    prob_grad = jnp.einsum("qhd,khd->hqk", gheads, vheads, preferred_element_type=jnp.float32)
    centre = jnp.sum(probs * prob_grad, axis=2, keepdims=True)
    score_grad = (probs * (prob_grad - centre)).astype(jnp.bfloat16)
    query_part = (
        jnp.einsum("hqk,khd->qhd", score_grad, kheads, preferred_element_type=jnp.float32) * scale
    ).astype(jnp.bfloat16)
    key_part = (
        jnp.einsum("hqk,qhd->khd", score_grad, qheads, preferred_element_type=jnp.float32) * scale
    ).astype(jnp.bfloat16)
    return (
        outputs.reshape(slots, width),
        query_part.reshape(slots, width),
        key_part.reshape(slots, width),
        value_part.reshape(slots, width),
    )


def local(query, key, value, text, cond_weight, cotangent, dest, segment, align):
    slots = segment.shape[0]
    peers = lax.axis_size("seq")
    bucket = slots // peers
    group_text = lax.all_gather(text, "seq", axis=0, tiled=True)
    condition = jnp.take(group_text, align, axis=0)
    full_weight = lax.all_gather(cond_weight, ("dp", "seq"), axis=0, tiled=True)
    extra = jnp.dot(condition, full_weight, preferred_element_type=jnp.float32)
    valued = (value.astype(jnp.float32) + extra).astype(jnp.bfloat16)
    owner = dest // slots
    local_slot = dest % slots
    member = (owner[:, None] == jnp.arange(peers)[None, :]).astype(jnp.int32)
    rank = jnp.sum(jnp.cumsum(member, axis=0) * member, axis=1) - 1
    position = owner * bucket + rank
    send_slot = jnp.full((slots,), -1, jnp.int32).at[position].set(local_slot)

    def to_buckets(source):
        return jnp.zeros((slots, source.shape[1]), source.dtype).at[position].set(source)

    def settle(arrived, target):
        return (
            jnp.zeros((slots, arrived.shape[1]), arrived.dtype).at[target].set(arrived, mode="drop")
        )

    got_query, got_key, got_value, got_slot = (
        lax.all_to_all(to_buckets(query), "seq", split_axis=0, concat_axis=0, tiled=True),
        lax.all_to_all(to_buckets(key), "seq", split_axis=0, concat_axis=0, tiled=True),
        lax.all_to_all(to_buckets(valued), "seq", split_axis=0, concat_axis=0, tiled=True),
        lax.all_to_all(send_slot, "seq", split_axis=0, concat_axis=0, tiled=True),
    )
    got_cot = lax.all_to_all(to_buckets(cotangent), "seq", split_axis=0, concat_axis=0, tiled=True)
    target = jnp.where(got_slot >= 0, got_slot, slots)
    results = attend(
        settle(got_query, target),
        settle(got_key, target),
        settle(got_value, target),
        settle(got_cot, target),
        segment,
    )
    picker = jnp.maximum(got_slot, 0)
    back_out = lax.all_to_all(results[0][picker], "seq", split_axis=0, concat_axis=0, tiled=True)
    back_query, back_key, back_value = (
        lax.all_to_all(results[1][picker], "seq", split_axis=0, concat_axis=0, tiled=True),
        lax.all_to_all(results[2][picker], "seq", split_axis=0, concat_axis=0, tiled=True),
        lax.all_to_all(results[3][picker], "seq", split_axis=0, concat_axis=0, tiled=True),
    )
    attended = back_out[position]
    query_grad = back_query[position]
    key_grad = back_key[position]
    value_grad = back_value[position]
    cond_grad = lax.dot_general(
        value_grad, full_weight, (((1,), (1,)), ((), ())), preferred_element_type=jnp.float32
    )
    local_weight = lax.dot_general(
        condition, value_grad, (((0,), (0,)), ((), ())), preferred_element_type=jnp.float32
    )
    weight_grad = lax.psum_scatter(local_weight, ("dp", "seq"), scatter_dimension=0, tiled=True)
    local_text = (
        jnp.zeros((group_text.shape[0], condition.shape[1]), jnp.float32).at[align].add(cond_grad)
    )
    text_grad = lax.psum_scatter(
        local_text.astype(jnp.bfloat16), "seq", scatter_dimension=0, tiled=True
    ).astype(jnp.float32)
    return (attended, query_grad, key_grad, value_grad, text_grad, weight_grad)


def solution(mesh):
    in_specs = (
        P(("dp", "seq"), None),
        P(("dp", "seq"), None),
        P(("dp", "seq"), None),
        P(("dp", "seq"), None),
        P(("dp", "seq"), None),
        P(("dp", "seq"), None),
        P(("dp", "seq")),
        P(("dp", "seq")),
        P(("dp", "seq")),
    )
    out_specs = (
        P(("dp", "seq"), None),
        P(("dp", "seq"), None),
        P(("dp", "seq"), None),
        P(("dp", "seq"), None),
        P(("dp", "seq"), None),
        P(("dp", "seq"), None),
    )
    return jax.shard_map(local, mesh=mesh, in_specs=in_specs, out_specs=out_specs, check_vma=False)
```

profile of v0, /device:TPU:1, one launch (start us, length us, event | category | flops | bytes accessed | tf_op | source)
XLA Modules:
  0.0 789.5 jit_solution(11496362760274739348)
XLA Ops:
  10.0 13.7 %all-to-all-start = ((s32[32,8,1]{1,2,0:T(1,128)}), s32[32,8,1]{1,2,0:T(1,128)S(1)}, u32[]{:S(2)}, u32[]{:S(2)}) async-start(s32[32,8,1]{1,2,0:T(1,128)} %bitcast), calls=%async_computation | async-start | bytes 32768 | tf_op jit(solution)/shard_map/all_to_all | solution.py:79
  23.7 2.6 scatter_custom_fusion.5
  26.3 5.9 all-to-all-done
  32.2 4.0 all-to-all-start.3
  37.0 2.6 scatter_custom_fusion.3
  39.6 16.4 %all-to-all-done.3 = bf16[32,8,1536]{2,1,0:T(8,128)(2,1)S(1)} async-done(((bf16[32,8,1536]{2,1,0:T(8,128)(2,1)}), bf16[32,8,1536]{2,1,0:T(8,128)(2,1)S(1)}, u32[]{:S(2)}, u32[]{:S(2)}) %all-to-all-start.3) | async-done | bytes 786464 | tf_op jit(solution)/shard_map/all_to_all | solution.py:77
  56.0 6.8 all-to-all-start.2
  62.9 2.6 scatter_custom_fusion.7
  65.5 17.1 %all-to-all-done.2 = bf16[32,8,1536]{2,1,0:T(8,128)(2,1)S(1)} async-done(((bf16[32,8,1536]{2,1,0:T(8,128)(2,1)}), bf16[32,8,1536]{2,1,0:T(8,128)(2,1)S(1)}, u32[]{:S(2)}, u32[]{:S(2)}) %all-to-all-start.2) | async-done | bytes 786464 | tf_op jit(solution)/shard_map/all_to_all | solution.py:76
  82.6 6.8 all-to-all-start.5
  89.5 50.3 %all_gather.6 = bf16[256,512]{1,0:T(8,128)(2,1)S(1)} all-gather(bf16[8,512]{1,0:T(8,128)(2,1)S(1)} %copy-done.11), channel_id=1, replica_groups=mesh['dp'=16,'seq'=32] {'seq'}, dimensions={0}, use_global_device_ids=true | all-gather | bytes 270336 | tf_op jit(solution)/shard_map/all_gather | solution.py:55
  140.7 24.4 %all-gather.3.cloned.1.call-done = bf16[512,1,1536]{2,1,0:T(2,128)(2,1)} async-done(((bf16[1,1,1536]{2,1,0:T(2,128)(2,1)}), bf16[512,1,1536]{2,1,0:T(2,128)(2,1)}) %all-gather.3.cloned.1.call-update) | async-done | bytes 1572880 | tf_op jit(solution)/shard_map/all_gather | solution.py:57
  165.1 3.1 fusion.1
  168.2 2.6 scatter_custom_fusion.1
  171.7 7.0 all-to-all-start.1
  180.2 2.2 scatter_custom_fusion.6
  189.0 4.3 fusion.46
  193.3 2.5 convolution_convert_fusion
  200.1 7.4 all-to-all-start.8
  209.8 2.3 convolution_convert_fusion.1
  214.5 14.0 %all-to-all-done.8 = bf16[32,8,1536]{2,1,0:T(8,128)(2,1)S(1)} async-done(((bf16[32,8,1536]{2,1,0:T(8,128)(2,1)}), bf16[32,8,1536]{2,1,0:T(8,128)(2,1)S(1)}, u32[]{:S(2)}, u32[]{:S(2)}) %all-to-all-start.8) | async-done | bytes 786464 | tf_op jit(solution)/shard_map/all_to_all | solution.py:95
  228.5 6.1 all-to-all-start.4
  234.6 2.7 multiply_reduce_fusion
  243.7 10.7 %all-to-all-done.4 = bf16[32,8,1536]{2,1,0:T(8,128)(2,1)S(1)} async-done(((bf16[32,8,1536]{2,1,0:T(8,128)(2,1)}), bf16[32,8,1536]{2,1,0:T(8,128)(2,1)S(1)}, u32[]{:S(2)}, u32[]{:S(2)}) %all-to-all-start.4) | async-done | bytes 786464 | tf_op jit(solution)/shard_map/all_to_all | solution.py:91
  254.4 6.5 all-to-all-start.7
  261.9 2.7 fusion.3
  266.9 3.4 fusion.39
  270.2 2.5 multiply_convert_fusion.2
  276.2 4.4 all-to-all-done.7
  280.6 6.7 all-to-all-start.6
  287.3 197.6 %reduce-scatter.2.cloned.1.call-done = bf16[8,512]{1,0:T(8,128)(2,1)} async-done(((bf16[256,512]{1,0:T(8,128)(2,1)}), bf16[8,512]{1,0:T(8,128)(2,1)}) %reduce-scatter.2.cloned.1.call-update) | async-done | bytes 8208 | tf_op jit(solution)/shard_map/reduce_scatter | solution.py:111
  486.3 290.4 %all-reduce.3.cloned.1.call-done = f32[512,1536]{1,0:T(8,128)} async-done(((f32[512,1536]{1,0:T(8,128)}), f32[512,1536]{1,0:T(8,128)}) %all-reduce.3.cloned.1.call-update) | async-done | bytes 3145744
  (83 shorter events, 42.9 us)
Async XLA Ops:
  10.0 22.2 %all-to-all-start = ((s32[32,8,1]{1,2,0:T(1,128)}), s32[32,8,1]{1,2,0:T(1,128)S(1)}, u32[]{:S(2)}, u32[]{:S(2)}) async-start(s32[32,8,1]{1,2,0:T(1,128)} %bitcast), calls=%async_computation | async-start | bytes 32768 | tf_op jit(solution)/shard_map/all_to_all | solution.py:79
  32.2 57.2 %copy-start.11 = (bf16[8,512]{1,0:T(8,128)(2,1)S(1)}, bf16[8,512]{1,0:T(8,128)(2,1)}, u32[]{:S(2)}) copy-start(bf16[8,512]{1,0:T(8,128)(2,1)} %param.12) | copy-start | bytes 24580
  32.2 107.6 %copy-start.14 = (s32[128]{0:T(128)S(1)}, s32[128]{0:T(128)}, u32[]{:S(2)}) copy-start(s32[128]{0:T(128)} %param.17) | copy-start | bytes 1540
  32.2 23.8 %all-to-all-start.3 = ((bf16[32,8,1536]{2,1,0:T(8,128)(2,1)}), bf16[32,8,1536]{2,1,0:T(8,128)(2,1)S(1)}, u32[]{:S(2)}, u32[]{:S(2)}) async-start(bf16[32,8,1536]{2,1,0:T(8,128)(2,1)} %bitcast.9), calls=%async_computation.3 | async-start | bytes 1572864 | tf_op jit(solution)/shard_map/all_to_all | solution.py:77
  36.3 128.8 %copy-start.13 = (bf16[128,1536]{1,0:T(8,128)(2,1)S(1)}, bf16[128,1536]{1,0:T(8,128)(2,1)}, u32[]{:S(2)}) copy-start(bf16[128,1536]{1,0:T(8,128)(2,1)} %param.11) | copy-start | bytes 1179652
  36.3 128.8 %all-gather.3.cloned.1.call-start = ((), (), s32[]{:S(2)}) async-start(), calls=%async_computation.11 | async-start | bytes 3151872 | tf_op jit(solution)/shard_map/all_gather | solution.py:57
  56.0 26.6 %all-to-all-start.2 = ((bf16[32,8,1536]{2,1,0:T(8,128)(2,1)}), bf16[32,8,1536]{2,1,0:T(8,128)(2,1)S(1)}, u32[]{:S(2)}, u32[]{:S(2)}) async-start(bf16[32,8,1536]{2,1,0:T(8,128)(2,1)} %bitcast.6), calls=%async_computation.2 | async-start | bytes 1572864 | tf_op jit(solution)/shard_map/all_to_all | solution.py:76
  82.6 88.2 %all-to-all-start.5 = ((bf16[32,8,1536]{2,1,0:T(8,128)(2,1)}), bf16[32,8,1536]{2,1,0:T(8,128)(2,1)S(1)}, u32[]{:S(2)}, u32[]{:S(2)}) async-start(bf16[32,8,1536]{2,1,0:T(8,128)(2,1)} %bitcast.17), calls=%async_computation.5 | async-start | bytes 1572864 | tf_op jit(solution)/shard_map/all_to_all | solution.py:81
  139.8 38.9 %copy-start.12 = (s32[256]{0:T(256)S(1)}, s32[256]{0:T(256)}, u32[]{:S(2)}) copy-start(s32[256]{0:T(256)} %param.16) | copy-start | bytes 3076
  140.7 39.5 %copy-start.10 = (bf16[128,512]{1,0:T(8,128)(2,1)}, bf16[128,512]{1,0:T(8,128)(2,1)S(1)}, u32[]{:S(2)}) copy-start(bf16[128,512]{1,0:T(8,128)(2,1)S(1)} %gather_fusion) | copy-start | bytes 393220
  170.8 0.9 copy-start.2
  171.7 28.4 %all-to-all-start.1 = ((bf16[32,8,1536]{2,1,0:T(8,128)(2,1)}), bf16[32,8,1536]{2,1,0:T(8,128)(2,1)S(1)}, u32[]{:S(2)}, u32[]{:S(2)}) async-start(bf16[32,8,1536]{2,1,0:T(8,128)(2,1)} %bitcast.3), calls=%async_computation.1 | async-start | bytes 1572864 | tf_op jit(solution)/shard_map/all_to_all | solution.py:78
  182.4 4.3 copy-start.3
  186.7 2.3 copy-start.4
  189.0 4.3 copy-start.8
  200.1 28.5 %all-to-all-start.8 = ((bf16[32,8,1536]{2,1,0:T(8,128)(2,1)}), bf16[32,8,1536]{2,1,0:T(8,128)(2,1)S(1)}, u32[]{:S(2)}, u32[]{:S(2)}) async-start(bf16[32,8,1536]{2,1,0:T(8,128)(2,1)} %bitcast.30), calls=%async_computation.8 | async-start | bytes 1572864 | tf_op jit(solution)/shard_map/all_to_all | solution.py:95
  212.4 22.3 %copy-start.9 = (bf16[256,1536]{0,1:T(8,128)(2,1)S(1)}, bf16[256,1536]{0,1:T(8,128)(2,1)}, u32[]{:S(2)}) copy-start(bf16[256,1536]{0,1:T(8,128)(2,1)} %copy-done.8) | copy-start | bytes 2359300
  228.5 25.9 %all-to-all-start.4 = ((bf16[32,8,1536]{2,1,0:T(8,128)(2,1)}), bf16[32,8,1536]{2,1,0:T(8,128)(2,1)S(1)}, u32[]{:S(2)}, u32[]{:S(2)}) async-start(bf16[32,8,1536]{2,1,0:T(8,128)(2,1)} %bitcast.15), calls=%async_computation.4 | async-start | bytes 1572864 | tf_op jit(solution)/shard_map/all_to_all | solution.py:91
  234.6 2.8 copy-start.6
  237.5 1.1 copy-start.5
  238.6 1.5 copy-start
  254.4 26.2 %all-to-all-start.7 = ((bf16[32,8,1536]{2,1,0:T(8,128)(2,1)}), bf16[32,8,1536]{2,1,0:T(8,128)(2,1)S(1)}, u32[]{:S(2)}, u32[]{:S(2)}) async-start(bf16[32,8,1536]{2,1,0:T(8,128)(2,1)} %bitcast.26), calls=%async_computation.7 | async-start | bytes 1572864 | tf_op jit(solution)/shard_map/all_to_all | solution.py:94
  260.9 224.1 %reduce-scatter.2.cloned.1.call-start = ((), (), s32[]{:S(2)}) async-start(), calls=%async_computation.10 | async-start | bytes 270336 | tf_op jit(solution)/shard_map/reduce_scatter | solution.py:111
  261.9 8.4 %copy-start.7 = (bf16[128,1536]{1,0:T(8,128)(2,1)}, bf16[128,1536]{1,0:T(8,128)(2,1)S(1)}, u32[]{:S(2)}) copy-start(bf16[128,1536]{1,0:T(8,128)(2,1)S(1)} %gather_fusion.8) | copy-start | bytes 1179652
  266.8 3.4 copy-start.1
  266.8 509.8 %all-reduce.3.cloned.1.call-start = ((), (), s32[]{:S(2)}) async-start(), calls=%async_computation.12 | async-start | bytes 6291456
  280.6 500.7 %all-to-all-start.6 = ((bf16[32,8,1536]{2,1,0:T(8,128)(2,1)}), bf16[32,8,1536]{2,1,0:T(8,128)(2,1)S(1)}, u32[]{:S(2)}, u32[]{:S(2)}) async-start(bf16[32,8,1536]{2,1,0:T(8,128)(2,1)} %bitcast.22), calls=%async_computation.6 | async-start | bytes 1572864 | tf_op jit(solution)/shard_map/all_to_all | solution.py:93
Sparse Core Ops, SparseCore 0:
  41.3 123.7 all-gather.2
  266.9 217.9 reduce-scatter.1
  489.9 286.6 all-reduce.2
where the time goes:
time: 791 us; the launch traced here: 789 us
  waiting for transfers between devices  583 us (74%)
  starting transfers between devices  65.2 us (8%)
  blocking collectives  50.3 us (6%)
  local copies, waits for them, and re-layouts  45.3 us (6%)
  matrix products  24.9 us (3%)
  between operations  14.2 us (2%)
    unnamed x4, waiting for transfers between devices  291 us
    reduce_scatter x1, waiting for transfers between devices, local(): lax.psum_scatter(local_text.astype(jnp.bfloat16), 'seq', scatter_dimensio...  198 us
    all_gather x1, blocking collectives, local(): group_text = lax.all_gather(text, 'seq', axis=0, tiled=True)  50.3 us
    all_gather x1, waiting for transfers between devices, local(): full_weight = lax.all_gather(cond_weight, ('dp', 'seq'), axis=0, tiled=True)  24.4 us
    all_to_all x1, waiting for transfers between devices, local(): lax.all_to_all(to_buckets(query), 'seq', split_axis=0, concat_axis=0, til...  17.1 us
    all_to_all x1, waiting for transfers between devices, local(): lax.all_to_all(to_buckets(key), 'seq', split_axis=0, concat_axis=0, tiled...  16.4 us
  transfers between devices with their start and end apart: 12, of which 10 were waited for; matrix products, arithmetic and copies ran while one was open for 9% of the time, Pallas kernels for 0%

commit v1 on v0

v1 whole, which is shorter than its diff:
```python
import functools

import jax
import jax.numpy as jnp
from jax import lax
from jax.experimental import pallas as pl
from jax.experimental.pallas import tpu as pltpu
from jax.sharding import PartitionSpec as P

F32 = jnp.float32
BF16 = jnp.bfloat16

NZ, NX = 8, 4
PEERS = NZ * NX
ROWS = 128
SLOTS = 256
BUCKET = 8
OWN = 3
HPD = 3
COMPACT = NZ * OWN
LANES = 128
COLS = HPD * LANES
TEXT = 512
GTEXT = 256
BLOCK = 2 * HPD * 2 * BUCKET
TG_ROWS = 32
OUT_ROWS = OWN * BLOCK + TG_ROWS


def iota(shape, dim):
    return lax.broadcasted_iota(jnp.int32, shape, dim)


def dot(a, b):
    return jnp.dot(a, b, preferred_element_type=F32)


def dot_nt(a, b):
    return lax.dot_general(a, b, (((1,), (1,)), ((), ())), preferred_element_type=F32)


def dot_tn(a, b):
    return lax.dot_general(a, b, (((0,), (0,)), ((), ())), preferred_element_type=F32)


def upper(n):
    return (iota((n, n), 0) <= iota((n, n), 1)).astype(BF16)


def spread8(x):
    n = x.shape[0]
    return jnp.broadcast_to(x[:, None, :], (n, BUCKET, LANES)).reshape(n * BUCKET, LANES)


def bucket_select(match):
    n = match.shape[0]
    count = dot(match.astype(BF16), upper(ROWS))
    rank = ((iota((n * BUCKET, LANES), 0) & (BUCKET - 1)) + 1).astype(F32)
    hit = (spread8(count) == rank) & (spread8(match) > 0.5)
    return jnp.where(hit, 1.0, 0.0)


def compact_owners(seg_first):
    flag = jnp.where(jnp.broadcast_to(seg_first[:, 0:1], (PEERS, LANES)) >= 0.0, 1.0, 0.0)
    lower = (iota((PEERS, PEERS), 0) >= iota((PEERS, PEERS), 1)).astype(BF16)
    count = dot(lower, flag.astype(BF16))
    lane = (iota((PEERS, LANES), 1) + 1).astype(F32)
    hit = jnp.where((count == lane) & (flag > 0.5), 1.0, 0.0)
    ids = iota((PEERS, LANES), 0).astype(F32) + 1.0
    row = jnp.sum(hit * ids, axis=0, keepdims=True) - 1.0
    diag = iota((COMPACT, LANES), 0) == iota((COMPACT, LANES), 1)
    col = jnp.sum(jnp.where(diag, jnp.broadcast_to(row, (COMPACT, LANES)), 0.0), axis=1, keepdims=True)
    return jnp.broadcast_to(col, (COMPACT, LANES))


def prep_kernel(dest_ref, align_ref, seg_ref, w_ref, out_ref):
    sub = iota((8, LANES), 0)

    def row(v):
        return jnp.broadcast_to(v.astype(F32), (8, LANES))

    base = jnp.where(sub == 0, row(dest_ref[...]), 0.0)
    base = jnp.where(sub == 1, row(align_ref[...]), base)
    seg = seg_ref[...]
    base = jnp.where(sub == 2, row(seg[:, :LANES]), base)
    base = jnp.where(sub == 3, row(seg[:, LANES:]), base)
    w = w_ref[...].astype(F32)
    for x in range(NX):
        msg = base
        for h in range(HPD):
            start = (x * HPD + h) * LANES
            msg = jnp.where(sub == 4 + h, row(w[:, start : start + LANES]), msg)
        for z in range(NZ):
            out_ref[z, x] = msg


def prep(dest, align, seg, w):
    return pl.pallas_call(
        prep_kernel,
        out_shape=jax.ShapeDtypeStruct((NZ, NX, 8, LANES), F32),
        name="prep",
    )(dest, align, seg, w)


def owner_match(msg_ref, dest_ref):
    owners = compact_owners(msg_ref[pl.ds(2, PEERS, stride=8), :])
    mine = jnp.broadcast_to(dest_ref[...] >> 8, (COMPACT, LANES)).astype(F32)
    return owners, jnp.where(mine == owners, 1.0, 0.0)


def pack_kernel(msg_ref, dest_ref, q_ref, k_ref, v_ref, g_ref, out_ref, own_ref, sel_ref):
    @pl.when(pl.program_id(0) == 0)
    def _():
        owners, match = owner_match(msg_ref, dest_ref)
        own_ref[...] = owners
        sel_ref[...] = bucket_select(match).astype(BF16)

    sel = sel_ref[...]
    for pair, (a_ref, b_ref) in enumerate(((q_ref, k_ref), (v_ref, g_ref))):
        a = dot(sel, a_ref[...]).reshape(COMPACT, BUCKET, COLS)
        b = dot(sel, b_ref[...]).reshape(COMPACT, BUCKET, COLS)
        both = jnp.concatenate([a, b], axis=1).astype(BF16).reshape(NZ, OWN, 2 * BUCKET, COLS)
        for i in range(OWN):
            for h in range(HPD):
                off = i * BLOCK + (pair * HPD + h) * 2 * BUCKET
                out_ref[:, 0, off : off + 2 * BUCKET, :] = both[:, i, :, h * LANES : (h + 1) * LANES]


def pack(msg, dest, q, k, v, g):
    full = lambda shape: pl.BlockSpec(shape, lambda x: (0,) * len(shape))
    cols = pl.BlockSpec((ROWS, COLS), lambda x: (0, x))
    return pl.pallas_call(
        pack_kernel,
        grid=(NX,),
        in_specs=[full((PEERS * 8, LANES)), full((1, LANES)), cols, cols, cols, cols],
        out_specs=[
            pl.BlockSpec((NZ, 1, OWN * BLOCK, LANES), lambda x: (0, x, 0, 0)),
            full((COMPACT, LANES)),
        ],
        out_shape=[
            jax.ShapeDtypeStruct((NZ, NX, OWN * BLOCK, LANES), BF16),
            jax.ShapeDtypeStruct((COMPACT, LANES), F32),
        ],
        scratch_shapes=[pltpu.VMEM((COMPACT * BUCKET, LANES), BF16)],
        name="pack",
    )(msg, dest, q, k, v, g)


def attend_kernel(z_ref, msg_ref, own_ref, in_ref, text_ref, w_ref, out_ref, wg_ref, acc_ref):
    i = pl.program_id(0)
    n = SLOTS

    owner = jnp.broadcast_to(own_ref[pl.ds(z_ref[0] * OWN + i, 1), :], (PEERS, LANES))
    dest = msg_ref[pl.ds(0, PEERS, stride=8), :].astype(jnp.int32)
    match = jnp.where((dest >> 8).astype(F32) == owner, 1.0, 0.0)
    sel = bucket_select(match)
    valid = jnp.sum(sel, axis=1, keepdims=True)
    slot = jnp.sum(sel * spread8((dest & (SLOTS - 1)).astype(F32)), axis=1, keepdims=True)
    slot = jnp.where(valid > 0.5, slot, -1.0)
    align = jnp.sum(sel * spread8(msg_ref[pl.ds(1, PEERS, stride=8), :]), axis=1, keepdims=True)
    align = jnp.where(valid > 0.5, align, -1.0)

    mine = iota((PEERS, LANES), 0).astype(F32) == owner
    seg_lo = jnp.sum(jnp.where(mine, msg_ref[pl.ds(2, PEERS, stride=8), :], 0.0), axis=0, keepdims=True)
    seg_hi = jnp.sum(jnp.where(mine, msg_ref[pl.ds(3, PEERS, stride=8), :], 0.0), axis=0, keepdims=True)
    seg = jnp.concatenate([seg_lo, seg_hi], axis=1)
    lane = iota((n, n), 1)
    lanef = lane.astype(F32)
    diag = iota((n, n), 0) == lane
    label = jnp.sum(jnp.where(lanef == slot, jnp.broadcast_to(seg, (n, n)), 0.0), axis=1, keepdims=True)
    label = jnp.where(valid > 0.5, label, -1.0)
    label_b = jnp.broadcast_to(label, (n, n))
    label_row = jnp.sum(jnp.where(diag, label_b, 0.0), axis=0, keepdims=True)
    allowed = ((label_b == jnp.broadcast_to(label_row, (n, n))) & (label_b >= 0.0)) | diag
    bias = jnp.where(allowed, 0.0, -1e30)

    pick = jnp.where(lanef == align, 1.0, 0.0).astype(BF16)
    cond = dot(pick, text_ref[...]).astype(BF16)
    extra = dot(cond, w_ref[...])

    scale = LANES ** (-0.5)

    def pair_of(pair, h):
        off = (pair * HPD + h) * 2 * BUCKET
        both = in_ref[:, off : off + 2 * BUCKET, :].astype(F32).reshape(PEERS, 2, BUCKET, LANES)
        return both[:, 0].reshape(n, LANES), both[:, 1].reshape(n, LANES)

    def put(pair, h, a, b):
        off = (pair * HPD + h) * 2 * BUCKET
        both = jnp.concatenate(
            [a.reshape(PEERS, BUCKET, LANES), b.reshape(PEERS, BUCKET, LANES)], axis=1
        ).astype(BF16)
        out_ref[:, pl.ds(pl.multiple_of(i * BLOCK + off, 16), 2 * BUCKET), :] = both

    value_grads = []
    for h in range(HPD):
        q, k = pair_of(0, h)
        v, g = pair_of(1, h)
        q, k, g = q.astype(BF16), k.astype(BF16), g.astype(BF16)
        v = (v + extra[:, h * LANES : (h + 1) * LANES]).astype(BF16)
        s = dot_nt(q, k) * scale + bias
        e = jnp.exp(s - jnp.max(s, axis=1, keepdims=True))
        p = e * (1.0 / jnp.sum(e, axis=1, keepdims=True))
        w = p.astype(BF16)
        out = dot(w, v)
        value_grad = dot_tn(w, g)
        pg = dot_nt(g, v)
        centre = jnp.sum(p * pg, axis=1, keepdims=True)
        sg = (p * (pg - centre)).astype(BF16)
        query_grad = dot(sg, k) * scale
        key_grad = dot_tn(sg, q) * scale
        put(0, h, out, query_grad)
        put(1, h, key_grad, value_grad)
        value_grads.append(value_grad.astype(BF16))

    part = dot_tn(pick, jnp.concatenate(value_grads, axis=1))

    @pl.when(i == 0)
    def _():
        acc_ref[...] = part

    @pl.when(i > 0)
    def _():
        acc_ref[...] += part

    @pl.when(i == OWN - 1)
    def _():
        acc = acc_ref[...]
        high = acc.astype(BF16)
        low = (acc - high.astype(F32)).astype(BF16)
        weight = w_ref[...]
        tg = dot_nt(high, weight) + dot_nt(low, weight)
        tg = tg.reshape(PEERS, BUCKET, TEXT)
        for c in range(2):
            both = jnp.concatenate(
                [tg[:, :, 2 * c * LANES : (2 * c + 1) * LANES], tg[:, :, (2 * c + 1) * LANES : (2 * c + 2) * LANES]],
                axis=1,
            ).astype(BF16)
            off = OWN * BLOCK + c * 2 * BUCKET
            out_ref[:, off : off + 2 * BUCKET, :] = both
        text = text_ref[...]
        wg_ref[...] = dot_tn(text, high) + dot_tn(text, low)


def attend(zi, msg, own, got, text, w):
    full = lambda shape: pl.BlockSpec(shape, lambda i, z: (0,) * len(shape))
    return pl.pallas_call(
        attend_kernel,
        grid_spec=pltpu.PrefetchScalarGridSpec(
            num_scalar_prefetch=1,
            grid=(OWN,),
            in_specs=[
                full((PEERS * 8, LANES)),
                full((COMPACT, LANES)),
                pl.BlockSpec((PEERS, BLOCK, LANES), lambda i, z: (0, i, 0)),
                full((GTEXT, TEXT)),
                full((TEXT, COLS)),
            ],
            out_specs=[full((PEERS, OUT_ROWS, LANES)), full((TEXT, COLS))],
            scratch_shapes=[pltpu.VMEM((GTEXT, COLS), F32)],
        ),
        out_shape=[
            jax.ShapeDtypeStruct((PEERS, OUT_ROWS, LANES), BF16),
            jax.ShapeDtypeStruct((TEXT, COLS), F32),
        ],
        name="attend",
    )(zi, msg, own, got, text, w)


def unpack_kernel(msg_ref, dest_ref, in_ref, o_ref, q_ref, k_ref, v_ref, tg_ref, sel_ref):
    x = pl.program_id(0)

    @pl.when(x == 0)
    def _():
        _, match = owner_match(msg_ref, dest_ref)
        sel_ref[...] = jnp.transpose(bucket_select(match)).astype(BF16)

    sel = sel_ref[...]
    for pair, (a_ref, b_ref) in enumerate(((o_ref, q_ref), (k_ref, v_ref))):
        for h in range(HPD):
            parts = []
            for i in range(OWN):
                off = i * BLOCK + (pair * HPD + h) * 2 * BUCKET
                parts.append(
                    in_ref[:, 0, off : off + 2 * BUCKET, :].astype(F32).reshape(NZ, 1, 2, BUCKET, LANES)
                )
            both = jnp.concatenate(parts, axis=1)
            a = both[:, :, 0].reshape(COMPACT * BUCKET, LANES).astype(BF16)
            b = both[:, :, 1].reshape(COMPACT * BUCKET, LANES).astype(BF16)
            span = slice(h * LANES, (h + 1) * LANES)
            a_ref[:, span] = dot(sel, a).astype(BF16)
            b_ref[:, span] = dot(sel, b).astype(BF16)

    for c in range(2):
        off = OWN * BLOCK + c * 2 * BUCKET
        total = jnp.sum(in_ref[:, 0, off : off + 2 * BUCKET, :].astype(F32), axis=0)
        for half in range(2):
            span = slice((2 * c + half) * LANES, (2 * c + half + 1) * LANES)
            piece = total[half * BUCKET : (half + 1) * BUCKET]

            @pl.when(x == 0)
            def _():
                tg_ref[:, span] = piece

            @pl.when(x > 0)
            def _():
                tg_ref[:, span] += piece


def unpack(msg, dest, got):
    full = lambda shape: pl.BlockSpec(shape, lambda x: (0,) * len(shape))
    cols = pl.BlockSpec((ROWS, COLS), lambda x: (0, x))
    rows = jax.ShapeDtypeStruct((ROWS, NX * COLS), BF16)
    return pl.pallas_call(
        unpack_kernel,
        grid=(NX,),
        in_specs=[
            full((PEERS * 8, LANES)),
            full((1, LANES)),
            pl.BlockSpec((NZ, 1, OUT_ROWS, LANES), lambda x: (0, x, 0, 0)),
        ],
        out_specs=[cols, cols, cols, cols, full((BUCKET, TEXT))],
        out_shape=[rows, rows, rows, rows, jax.ShapeDtypeStruct((BUCKET, TEXT), F32)],
        scratch_shapes=[pltpu.VMEM((ROWS, COMPACT * BUCKET), BF16)],
        name="unpack",
    )(msg, dest, got)


def exchange(x):
    return lax.all_to_all(x, "seq", split_axis=0, concat_axis=0, tiled=True)


def swap(x, axis, bit):
    size = lax.axis_size(axis)
    return lax.ppermute(x, axis, [(j, j ^ bit) for j in range(size)])


def gather_bits(x, axis, bits):
    index = lax.axis_index(axis)
    for depth, bit in enumerate(bits):
        other = swap(x, axis, bit)
        up = (index & bit) != 0
        first = jnp.where(up, other, x)
        second = jnp.where(up, x, other)
        x = jnp.stack([first, second], axis=depth)
    return x


def halve(x, axis, bit, dim):
    up = (lax.axis_index(axis) & bit) != 0
    zero, one = lax.index_in_dim(x, 0, dim, False), lax.index_in_dim(x, 1, dim, False)
    return jnp.where(up, one, zero) + swap(jnp.where(up, zero, one), axis, bit)


def local(query, key, value, text, cond_weight, cotangent, dest, segment, align):
    seq = lax.axis_index("seq")
    zi = (seq // NX).astype(jnp.int32).reshape(1)
    xi = seq % NX
    dest_row = dest.reshape(1, ROWS)
    first = prep(dest_row, align.reshape(1, ROWS), segment.reshape(1, SLOTS), cond_weight)
    msg3 = exchange(first.reshape(PEERS, 8, LANES))
    msg = msg3.reshape(PEERS * 8, LANES)
    packed, own = pack(msg, dest_row, query, key, value, cotangent)
    got = exchange(packed.reshape(PEERS, OWN * BLOCK, LANES))
    my_w = msg3[:, 4 : 4 + HPD, :].astype(BF16).reshape(PEERS, COLS)
    full_w = gather_bits(my_w, "dp", (8, 4, 2, 1)).reshape(TEXT, COLS)
    full_text = gather_bits(text, "seq", (16, 8, 4, 2, 1)).reshape(GTEXT, TEXT)
    back, wg = attend(zi, msg, own, got, full_text, full_w)
    returned = exchange(back)
    wg = wg.reshape(2, 2, 2, 2, PEERS, COLS)
    for bit, dim in ((1, 3), (2, 2), (4, 1), (8, 0)):
        wg = halve(wg, "dp", bit, dim)
    wg = wg.reshape(2, 2, 2, NX, COLS)
    for bit, dim in ((4, 2), (8, 1), (16, 0)):
        wg = halve(wg, "seq", bit, dim)
    pieces = [lax.dynamic_index_in_dim(wg, xi, 0, True)]
    for flip in (1, 2, 3):
        row = lax.dynamic_index_in_dim(wg, xi ^ flip, 0, True)
        pieces.append(swap(row, "seq", flip))
    out_cols = []
    for c in range(NX):
        flip = xi ^ c
        col = pieces[0]
        for m in (1, 2, 3):
            col = jnp.where(flip == m, pieces[m], col)
        out_cols.append(col)
    weight_grad = jnp.concatenate(out_cols, axis=1)
    attended, query_grad, key_grad, value_grad, text_grad = unpack(
        msg, dest_row, returned.reshape(NZ, NX, OUT_ROWS, LANES)
    )
    return attended, query_grad, key_grad, value_grad, text_grad, weight_grad


def solution(mesh):
    rows = P(("dp", "seq"), None)
    flat = P(("dp", "seq"))
    return jax.shard_map(
        local,
        mesh=mesh,
        in_specs=(rows, rows, rows, rows, rows, rows, flat, flat, flat),
        out_specs=(rows,) * 6,
        check_vma=False,
    )
```

time: 791 us -> 249 us (0.31)
  the two profiles are of different devices: /device:TPU:1 before, /device:TPU:4 now
where the time goes in v1:
time: 249 us; the launch traced here: 248 us
  waiting for transfers between devices  112 us (45%)
  starting transfers between devices  82.6 us (33%)
  Pallas kernels  23.9 us (10%)
  blocking collectives  22 us (9%)
  local copies, waits for them, and re-layouts  5.51 us (2%)
    ppermute x19, waiting for transfers between devices, swap(): return lax.ppermute(x, axis, [(j, j ^ bit) for j in range(size)])  112 us
    ppermute x19, starting transfers between devices, swap(): return lax.ppermute(x, axis, [(j, j ^ bit) for j in range(size)])  70.5 us
    all_to_all x1, blocking collectives, exchange(): return lax.all_to_all(x, 'seq', split_axis=0, concat_axis=0, tiled=True)  22 us
    pallas_call x1, Pallas kernels, attend(): pl.pallas_call(attend_kernel, grid_spec=pltpu.PrefetchScalarGridSpec(num_...  12.5 us
    all_to_all x2, starting transfers between devices, exchange(): return lax.all_to_all(x, 'seq', split_axis=0, concat_axis=0, tiled=True)  12.1 us
    pallas_call x1, Pallas kernels, unpack(): pl.pallas_call(unpack_kernel, grid=(NX,), in_specs=[full((PEERS * 8, LANE...  5 us
  transfers between devices with their start and end apart: 21, of which 15 were waited for; matrix products, arithmetic and copies ran while one was open for 2% of the time, Pallas kernels for 0%

profile of v1, /device:TPU:4, one launch (start us, length us, event | category | flops | bytes accessed | tf_op | source)
XLA Modules:
  0.0 248.1 jit_solution(1900794964043183442)
XLA Ops:
  2.0 22.0 %all_to_all.15 = f32[32,8,128]{2,1,0:T(8,128)} all-to-all(f32[32,8,128]{2,1,0:T(8,128)} %bitcast.117), channel_id=1, replica_groups=mesh['dp'=16,'seq'=32] {'seq'}, dimensions={0} | all-to-all | bytes 262144 | tf_op jit(solution)/shard_map/all_to_all | solution.py:330
  24.0 5.0 %pack.1 = (bf16[8,4,288,128]{3,2,1,0:T(8,128)(2,1)}, f32[24,128]{1,0:T(8,128)}) custom-call(f32[256,128]{1,0:T(8,128)} %bitcast.110, s32[1,128]{1,0:T(1,128)} %bitcast.122, bf16[128,1536]{1,0:T(8,128)(2,1)} %q_ref.1, bf16[128,1536]{1,0:T(8,128)(2,1)} %k_ref.1, bf16[128,1536]{1,0:T(8,128)(2,1)} %v_ref.1, bf16[128,1536]{1,0:T(8,128)(2,1)} %g_ref.1), custom_call_target="tpu_custom_call" | custom-call | tf_op jit(solution)/shard_map/pack/pallas_call | solution.py:132
  29.0 6.1 %all-to-all-start.1 = ((bf16[32,288,128]{2,1,0:T(8,128)(2,1)}), bf16[32,288,128]{2,1,0:T(8,128)(2,1)S(1)}, u32[]{:S(2)}, u32[]{:S(2)}) async-start(bf16[32,288,128]{2,1,0:T(8,128)(2,1)} %bitcast.113), calls=%async_computation.1 | async-start | bytes 4718592 | tf_op jit(solution)/shard_map/all_to_all | solution.py:330
  35.1 7.4 %collective-permute-start = (bf16[8,512]{1,0:T(8,128)(2,1)S(1)}, bf16[8,512]{1,0:T(8,128)(2,1)S(1)}, u32[]{:S(2)}, u32[]{:S(2)}) collective-permute-start(bf16[8,512]{1,0:T(8,128)(2,1)S(1)} %copy-done.3), channel_id=1, source_target_pairs={{0,16},{1,17},{2,18},{3,19},{4,20},{5,21},{6,22},{7,23},{8,24},{9,... | collective-permute-start | bytes 24584 | tf_op jit(solution)/shard_map/ppermute | solution.py:335
  42.5 48.1 %collective-permute-done = bf16[8,512]{1,0:T(8,128)(2,1)S(1)} collective-permute-done((bf16[8,512]{1,0:T(8,128)(2,1)S(1)}, bf16[8,512]{1,0:T(8,128)(2,1)S(1)}, u32[]{:S(2)}, u32[]{:S(2)}) %collective-permute-start) | collective-permute-done | bytes 8224 | tf_op jit(solution)/shard_map/ppermute | solution.py:335
  92.5 4.8 %collective-permute-done.1 = bf16[2,8,512]{2,1,0:T(8,128)(2,1)S(1)} collective-permute-done((bf16[2,8,512]{2,1,0:T(8,128)(2,1)S(1)}, bf16[2,8,512]{2,1,0:T(8,128)(2,1)S(1)}, u32[]{:S(2)}, u32[]{:S(2)}) %collective-permute-start.1) | collective-permute-done | bytes 16416 | tf_op jit(solution)/shard_map/ppermute | solution.py:335
  97.3 2.4 collective-permute-start.2
  99.8 3.3 %collective-permute-done.2 = bf16[2,2,8,512]{3,2,0,1:T(8,128)(2,1)S(1)} collective-permute-done((bf16[2,2,8,512]{3,2,0,1:T(8,128)(2,1)S(1)}, bf16[2,2,8,512]{3,2,0,1:T(8,128)(2,1)S(1)}, u32[]{:S(2)}, u32[]{:S(2)}) %collective-permute-start.2) | collective-permute-done | bytes 32800 | tf_op jit(solution)/shard_map/ppermute | solution.py:335
  104.1 7.7 %collective-permute-start.5 = (bf16[32,384]{1,0:T(8,128)(2,1)S(1)}, bf16[32,384]{1,0:T(8,128)(2,1)S(1)}, u32[]{:S(2)}, u32[]{:S(2)}) collective-permute-start(bf16[32,384]{1,0:T(8,128)(2,1)S(1)} %bitcast.120), channel_id=1, source_target_pairs={{0,256},{32,288},{64,320},{96,352},{128,384},{160,416},{192,448},{... | collective-permute-start | bytes 73736 | tf_op jit(solution)/shard_map/ppermute | solution.py:335
  111.8 2.5 collective-permute-start.3
  114.4 4.0 %collective-permute-start.6 = (bf16[2,32,384]{2,1,0:T(8,128)(2,1)S(1)}, bf16[2,32,384]{2,1,0:T(8,128)(2,1)S(1)}, u32[]{:S(2)}, u32[]{:S(2)}) collective-permute-start(bf16[2,32,384]{2,1,0:T(8,128)(2,1)S(1)} %pad_maximum_fusion.6), channel_id=1, source_target_pairs={{0,128},{32,160},{64,192},{96,224},{128,0},{160,32},{192,64},{224,... | collective-permute-start | bytes 147464 | tf_op jit(solution)/shard_map/ppermute | solution.py:335
  121.4 3.5 %collective-permute-start.7 = (bf16[2,2,32,384]{3,2,0,1:T(8,128)(2,1)S(1)}, bf16[2,2,32,384]{3,2,0,1:T(8,128)(2,1)S(1)}, u32[]{:S(2)}, u32[]{:S(2)}) collective-permute-start(bf16[2,2,32,384]{3,2,0,1:T(8,128)(2,1)S(1)} %pad_maximum_fusion.4), channel_id=1, source_target_pairs={{0,64},{32,96},{64,0},{96,32},{128,192},{160,224},{192,128},{224,1... | collective-permute-start | bytes 294920 | tf_op jit(solution)/shard_map/ppermute | solution.py:335
  124.9 1.9 collective-permute-start.4
  135.0 12.5 %attend.1 = (bf16[32,320,128]{2,1,0:T(8,128)(2,1)}, f32[512,384]{1,0:T(8,128)}) custom-call(s32[1]{0:T(128)} %bitcast.5.z_ref, f32[256,128]{1,0:T(8,128)} %bitcast.111, f32[24,128]{1,0:T(8,128)} %get-tuple-element.15.own_ref, bf16[32,288,128]{2,1,0:T(8,128)(2,1)} %copy-done.1, bf16[256,512]{1,0:T(8,128)(2,1)} %bitcast.115, bf16[512,384]{1,0:T(8,128)(2,1)} %bitcast.114), custom_call_target="tpu_custom_call" | custom-call | tf_op jit(solution)/shard_map/attend/pallas_call | solution.py:247
  147.4 6.0 %all-to-all-start.2 = ((bf16[32,320,128]{2,1,0:T(8,128)(2,1)}), bf16[32,320,128]{2,1,0:T(8,128)(2,1)S(1)}, u32[]{:S(2)}, u32[]{:S(2)}) async-start(bf16[32,320,128]{2,1,0:T(8,128)(2,1)} %get-tuple-element.17), calls=%async_computation.2 | async-start | bytes 5242880 | tf_op jit(solution)/shard_map/all_to_all | solution.py:330
  157.3 3.6 %collective-permute-start.10 = (f32[2,2,32,384]{3,2,0,1:T(8,128)S(1)}, f32[2,2,32,384]{3,2,0,1:T(8,128)S(1)}, u32[]{:S(2)}, u32[]{:S(2)}) collective-permute-start(f32[2,2,32,384]{3,2,0,1:T(8,128)S(1)} %select_bitcast_fusion.1), channel_id=1, source_target_pairs={{0,64},{32,96},{64,0},{96,32},{128,192},{160,224},{192,128},{224,1... | collective-permute-start | bytes 589832 | tf_op jit(solution)/shard_map/ppermute | solution.py:335
  160.9 5.2 %collective-permute-done.10 = f32[2,2,32,384]{3,2,0,1:T(8,128)S(1)} collective-permute-done((f32[2,2,32,384]{3,2,0,1:T(8,128)S(1)}, f32[2,2,32,384]{3,2,0,1:T(8,128)S(1)}, u32[]{:S(2)}, u32[]{:S(2)}) %collective-permute-start.10) | collective-permute-done | bytes 196640 | tf_op jit(solution)/shard_map/ppermute | solution.py:335
  166.2 3.4 %collective-permute-start.11 = (f32[2,32,384]{2,1,0:T(8,128)S(1)}, f32[2,32,384]{2,1,0:T(8,128)S(1)}, u32[]{:S(2)}, u32[]{:S(2)}) collective-permute-start(f32[2,32,384]{2,1,0:T(8,128)S(1)} %select_bitcast_fusion.6), channel_id=1, source_target_pairs={{0,128},{32,160},{64,192},{96,224},{128,0},{160,32},{192,64},{224,... | collective-permute-start | bytes 294920 | tf_op jit(solution)/shard_map/ppermute | solution.py:335
  169.6 5.6 %collective-permute-done.11 = f32[2,32,384]{2,1,0:T(8,128)S(1)} collective-permute-done((f32[2,32,384]{2,1,0:T(8,128)S(1)}, f32[2,32,384]{2,1,0:T(8,128)S(1)}, u32[]{:S(2)}, u32[]{:S(2)}) %collective-permute-start.11) | collective-permute-done | bytes 98336 | tf_op jit(solution)/shard_map/ppermute | solution.py:335
  175.2 5.7 %collective-permute-start.12 = (f32[32,384]{1,0:T(8,128)S(1)}, f32[32,384]{1,0:T(8,128)S(1)}, u32[]{:S(2)}, u32[]{:S(2)}) collective-permute-start(f32[32,384]{1,0:T(8,128)S(1)} %select_bitcast_fusion.11), channel_id=1, source_target_pairs={{0,256},{32,288},{64,320},{96,352},{128,384},{160,416},{192,448},{... | collective-permute-start | bytes 147464 | tf_op jit(solution)/shard_map/ppermute | solution.py:335
  180.9 4.2 %collective-permute-done.12 = f32[32,384]{1,0:T(8,128)S(1)} collective-permute-done((f32[32,384]{1,0:T(8,128)S(1)}, f32[32,384]{1,0:T(8,128)S(1)}, u32[]{:S(2)}, u32[]{:S(2)}) %collective-permute-start.12) | collective-permute-done | bytes 49184 | tf_op jit(solution)/shard_map/ppermute | solution.py:335
  185.1 3.4 %collective-permute-start.13 = (f32[2,2,4,384]{3,2,1,0:T(4,128)S(1)}, f32[2,2,4,384]{3,2,1,0:T(4,128)S(1)}, u32[]{:S(2)}, u32[]{:S(2)}) collective-permute-start(f32[2,2,4,384]{3,2,1,0:T(4,128)S(1)} %select_bitcast_fusion.16), channel_id=1, source_target_pairs={{0,4},{1,5},{2,6},{3,7},{4,0},{5,1},{6,2},{7,3},{8,12},{9,13},{10,... | collective-permute-start | bytes 73736 | tf_op jit(solution)/shard_map/ppermute | solution.py:335
  188.5 23.9 %collective-permute-done.13 = f32[2,2,4,384]{3,2,1,0:T(4,128)S(1)} collective-permute-done((f32[2,2,4,384]{3,2,1,0:T(4,128)S(1)}, f32[2,2,4,384]{3,2,1,0:T(4,128)S(1)}, u32[]{:S(2)}, u32[]{:S(2)}) %collective-permute-start.13) | collective-permute-done | bytes 24608 | tf_op jit(solution)/shard_map/ppermute | solution.py:335
  212.5 2.8 %collective-permute-start.14 = (f32[2,4,384]{2,1,0:T(4,128)S(1)}, f32[2,4,384]{2,1,0:T(4,128)S(1)}, u32[]{:S(2)}, u32[]{:S(2)}) collective-permute-start(f32[2,4,384]{2,1,0:T(4,128)S(1)} %select_bitcast_fusion.21), channel_id=1, source_target_pairs={{0,8},{1,9},{2,10},{3,11},{4,12},{5,13},{6,14},{7,15},{8,0},{9,1},... | collective-permute-start | bytes 36872 | tf_op jit(solution)/shard_map/ppermute | solution.py:335
  215.3 3.7 %collective-permute-done.14 = f32[2,4,384]{2,1,0:T(4,128)S(1)} collective-permute-done((f32[2,4,384]{2,1,0:T(4,128)S(1)}, f32[2,4,384]{2,1,0:T(4,128)S(1)}, u32[]{:S(2)}, u32[]{:S(2)}) %collective-permute-start.14) | collective-permute-done | bytes 12320 | tf_op jit(solution)/shard_map/ppermute | solution.py:335
  219.0 6.6 %collective-permute-start.15 = (f32[4,384]{1,0:T(4,128)S(1)}, f32[4,384]{1,0:T(4,128)S(1)}, u32[]{:S(2)}, u32[]{:S(2)}) collective-permute-start(f32[4,384]{1,0:T(4,128)S(1)} %select_bitcast_fusion.24), channel_id=1, source_target_pairs={{0,16},{1,17},{2,18},{3,19},{4,20},{5,21},{6,22},{7,23},{8,24},{9,... | collective-permute-start | bytes 18440 | tf_op jit(solution)/shard_map/ppermute | solution.py:335
  225.6 2.8 %collective-permute-done.15 = f32[4,384]{1,0:T(4,128)S(1)} collective-permute-done((f32[4,384]{1,0:T(4,128)S(1)}, f32[4,384]{1,0:T(4,128)S(1)}, u32[]{:S(2)}, u32[]{:S(2)}) %collective-permute-start.15) | collective-permute-done | bytes 6176 | tf_op jit(solution)/shard_map/ppermute | solution.py:335
  228.4 2.5 collective-permute-start.16
  230.9 4.6 %collective-permute-start.17 = (f32[1,384]{1,0:T(1,128)S(1)}, f32[1,384]{1,0:T(1,128)S(1)}, u32[]{:S(2)}, u32[]{:S(2)}) collective-permute-start(f32[1,384]{1,0:T(1,128)S(1)} %get-tuple-element.49), channel_id=1, source_target_pairs={{0,2},{1,3},{2,0},{3,1},{4,6},{5,7},{6,4},{7,5},{8,10},{9,11},{10,... | collective-permute-start | bytes 4616 | tf_op jit(solution)/shard_map/ppermute | solution.py:335
  235.5 2.8 %collective-permute-start.18 = (f32[1,384]{1,0:T(1,128)S(1)}, f32[1,384]{1,0:T(1,128)S(1)}, u32[]{:S(2)}, u32[]{:S(2)}) collective-permute-start(f32[1,384]{1,0:T(1,128)S(1)} %get-tuple-element.48), channel_id=1, source_target_pairs={{0,1},{1,0},{2,3},{3,2},{4,5},{5,4},{6,7},{7,6},{8,9},{9,8},{10,11... | collective-permute-start | bytes 4616 | tf_op jit(solution)/shard_map/ppermute | solution.py:335
  238.3 2.7 %collective-permute-done.18 = f32[1,384]{1,0:T(1,128)S(1)} collective-permute-done((f32[1,384]{1,0:T(1,128)S(1)}, f32[1,384]{1,0:T(1,128)S(1)}, u32[]{:S(2)}, u32[]{:S(2)}) %collective-permute-start.18) | collective-permute-done | bytes 1568 | tf_op jit(solution)/shard_map/ppermute | solution.py:335
  243.1 5.0 %unpack.1 = (bf16[128,1536]{1,0:T(8,128)(2,1)}, bf16[128,1536]{1,0:T(8,128)(2,1)}, bf16[128,1536]{1,0:T(8,128)(2,1)}, bf16[128,1536]{1,0:T(8,128)(2,1)}, f32[8,512]{1,0:T(8,128)}) custom-call(f32[256,128]{1,0:T(8,128)} %bitcast.112, s32[1,128]{1,0:T(1,128)} %bitcast.123, bf16[8,4,320,128]{3,2,1,0:T(8,128)(2,1)} %bitcast.109), custom_call_target="tpu_custom_call" | custom-call | tf_op jit(solution)/shard_map/unpack/pallas_call | solution.py:314
  (64 shorter events, 21.5 us)
Async XLA Ops:
  29.0 6.1 %copy-start.3 = (bf16[8,512]{1,0:T(8,128)(2,1)S(1)}, bf16[8,512]{1,0:T(8,128)(2,1)}, u32[]{:S(2)}) copy-start(bf16[8,512]{1,0:T(8,128)(2,1)} %param.12) | copy-start | bytes 24580
  29.0 104.5 %all-to-all-start.1 = ((bf16[32,288,128]{2,1,0:T(8,128)(2,1)}), bf16[32,288,128]{2,1,0:T(8,128)(2,1)S(1)}, u32[]{:S(2)}, u32[]{:S(2)}) async-start(bf16[32,288,128]{2,1,0:T(8,128)(2,1)} %bitcast.113), calls=%async_computation.1 | async-start | bytes 4718592 | tf_op jit(solution)/shard_map/all_to_all | solution.py:330
  35.1 55.5 %collective-permute-start = (bf16[8,512]{1,0:T(8,128)(2,1)S(1)}, bf16[8,512]{1,0:T(8,128)(2,1)S(1)}, u32[]{:S(2)}, u32[]{:S(2)}) collective-permute-start(bf16[8,512]{1,0:T(8,128)(2,1)S(1)} %copy-done.3), channel_id=1, source_target_pairs={{0,16},{1,17},{2,18},{3,19},{4,20},{5,21},{6,22},{7,23},{8,24},{9,... | collective-permute-start | bytes 24584 | tf_op jit(solution)/shard_map/ppermute | solution.py:335
  90.6 6.7 %collective-permute-start.1 = (bf16[2,8,512]{2,1,0:T(8,128)(2,1)S(1)}, bf16[2,8,512]{2,1,0:T(8,128)(2,1)S(1)}, u32[]{:S(2)}, u32[]{:S(2)}) collective-permute-start(bf16[2,8,512]{2,1,0:T(8,128)(2,1)S(1)} %pad_maximum_fusion.8), channel_id=1, source_target_pairs={{0,8},{1,9},{2,10},{3,11},{4,12},{5,13},{6,14},{7,15},{8,0},{9,1},... | collective-permute-start | bytes 49160 | tf_op jit(solution)/shard_map/ppermute | solution.py:335
  97.3 5.8 %collective-permute-start.2 = (bf16[2,2,8,512]{3,2,0,1:T(8,128)(2,1)S(1)}, bf16[2,2,8,512]{3,2,0,1:T(8,128)(2,1)S(1)}, u32[]{:S(2)}, u32[]{:S(2)}) collective-permute-start(bf16[2,2,8,512]{3,2,0,1:T(8,128)(2,1)S(1)} %pad_maximum_fusion.7), channel_id=1, source_target_pairs={{0,4},{1,5},{2,6},{3,7},{4,0},{5,1},{6,2},{7,3},{8,12},{9,13},{10,... | collective-permute-start | bytes 98312 | tf_op jit(solution)/shard_map/ppermute | solution.py:335
  104.1 10.2 %collective-permute-start.5 = (bf16[32,384]{1,0:T(8,128)(2,1)S(1)}, bf16[32,384]{1,0:T(8,128)(2,1)S(1)}, u32[]{:S(2)}, u32[]{:S(2)}) collective-permute-start(bf16[32,384]{1,0:T(8,128)(2,1)S(1)} %bitcast.120), channel_id=1, source_target_pairs={{0,256},{32,288},{64,320},{96,352},{128,384},{160,416},{192,448},{... | collective-permute-start | bytes 73736 | tf_op jit(solution)/shard_map/ppermute | solution.py:335
  111.8 7.7 %collective-permute-start.3 = (bf16[2,2,2,8,512]{4,3,0,1,2:T(8,128)(2,1)S(1)}, bf16[2,2,2,8,512]{4,3,0,1,2:T(8,128)(2,1)S(1)}, u32[]{:S(2)}, u32[]{:S(2)}) collective-permute-start(bf16[2,2,2,8,512]{4,3,0,1,2:T(8,128)(2,1)S(1)} %pad_maximum_fusion.5), channel_id=1, source_target_pairs={{0,2},{1,3},{2,0},{3,1},{4,6},{5,7},{6,4},{7,5},{8,10},{9,11},{10,... | collective-permute-start | bytes 196616 | tf_op jit(solution)/shard_map/ppermute | solution.py:335
  114.4 7.0 %collective-permute-start.6 = (bf16[2,32,384]{2,1,0:T(8,128)(2,1)S(1)}, bf16[2,32,384]{2,1,0:T(8,128)(2,1)S(1)}, u32[]{:S(2)}, u32[]{:S(2)}) collective-permute-start(bf16[2,32,384]{2,1,0:T(8,128)(2,1)S(1)} %pad_maximum_fusion.6), channel_id=1, source_target_pairs={{0,128},{32,160},{64,192},{96,224},{128,0},{160,32},{192,64},{224,... | collective-permute-start | bytes 147464 | tf_op jit(solution)/shard_map/ppermute | solution.py:335
  121.4 6.5 %collective-permute-start.7 = (bf16[2,2,32,384]{3,2,0,1:T(8,128)(2,1)S(1)}, bf16[2,2,32,384]{3,2,0,1:T(8,128)(2,1)S(1)}, u32[]{:S(2)}, u32[]{:S(2)}) collective-permute-start(bf16[2,2,32,384]{3,2,0,1:T(8,128)(2,1)S(1)} %pad_maximum_fusion.4), channel_id=1, source_target_pairs={{0,64},{32,96},{64,0},{96,32},{128,192},{160,224},{192,128},{224,1... | collective-permute-start | bytes 294920 | tf_op jit(solution)/shard_map/ppermute | solution.py:335
  124.9 6.9 %collective-permute-start.4 = (bf16[2,2,2,2,8,512]{5,4,0,1,2,3:T(8,128)(2,1)S(1)}, bf16[2,2,2,2,8,512]{5,4,0,1,2,3:T(8,128)(2,1)S(1)}, u32[]{:S(2)}, u32[]{:S(2)}) collective-permute-start(bf16[2,2,2,2,8,512]{5,4,0,1,2,3:T(8,128)(2,1)S(1)} %pad_maximum_fusion.3), channel_id=1, source_target_pairs={{0,1},{1,0},{2,3},{3,2},{4,5},{5,4},{6,7},{7,6},{8,9},{9,8},{10,11... | collective-permute-start | bytes 393224 | tf_op jit(solution)/shard_map/ppermute | solution.py:335
  128.0 4.6 %collective-permute-start.8 = (bf16[2,2,2,32,384]{4,3,0,1,2:T(8,128)(2,1)S(1)}, bf16[2,2,2,32,384]{4,3,0,1,2:T(8,128)(2,1)S(1)}, u32[]{:S(2)}, u32[]{:S(2)}) collective-permute-start(bf16[2,2,2,32,384]{4,3,0,1,2:T(8,128)(2,1)S(1)} %pad_maximum_fusion.2), channel_id=1, source_target_pairs={{0,32},{32,0},{64,96},{96,64},{128,160},{160,128},{192,224},{224,1... | collective-permute-start | bytes 589832 | tf_op jit(solution)/shard_map/ppermute | solution.py:335
  133.5 1.5 copy-start.1
  147.4 6.0 %copy-start.2 = (f32[512,384]{1,0:T(8,128)S(1)}, f32[512,384]{1,0:T(8,128)}, u32[]{:S(2)}) copy-start(f32[512,384]{1,0:T(8,128)} %get-tuple-element.23) | copy-start | bytes 2359300
  147.4 94.1 %all-to-all-start.2 = ((bf16[32,320,128]{2,1,0:T(8,128)(2,1)}), bf16[32,320,128]{2,1,0:T(8,128)(2,1)S(1)}, u32[]{:S(2)}, u32[]{:S(2)}) async-start(bf16[32,320,128]{2,1,0:T(8,128)(2,1)} %get-tuple-element.17), calls=%async_computation.2 | async-start | bytes 5242880 | tf_op jit(solution)/shard_map/all_to_all | solution.py:330
  153.6 3.6 %collective-permute-start.9 = (f32[2,2,2,32,384]{4,3,0,1,2:T(8,128)S(1)}, f32[2,2,2,32,384]{4,3,0,1,2:T(8,128)S(1)}, u32[]{:S(2)}, u32[]{:S(2)}) collective-permute-start(f32[2,2,2,32,384]{4,3,0,1,2:T(8,128)S(1)} %select_bitcast_fusion), channel_id=1, source_target_pairs={{0,32},{32,0},{64,96},{96,64},{128,160},{160,128},{192,224},{224,1... | collective-permute-start | bytes 1179656 | tf_op jit(solution)/shard_map/ppermute | solution.py:335
  157.3 8.8 %collective-permute-start.10 = (f32[2,2,32,384]{3,2,0,1:T(8,128)S(1)}, f32[2,2,32,384]{3,2,0,1:T(8,128)S(1)}, u32[]{:S(2)}, u32[]{:S(2)}) collective-permute-start(f32[2,2,32,384]{3,2,0,1:T(8,128)S(1)} %select_bitcast_fusion.1), channel_id=1, source_target_pairs={{0,64},{32,96},{64,0},{96,32},{128,192},{160,224},{192,128},{224,1... | collective-permute-start | bytes 589832 | tf_op jit(solution)/shard_map/ppermute | solution.py:335
  166.2 9.0 %collective-permute-start.11 = (f32[2,32,384]{2,1,0:T(8,128)S(1)}, f32[2,32,384]{2,1,0:T(8,128)S(1)}, u32[]{:S(2)}, u32[]{:S(2)}) collective-permute-start(f32[2,32,384]{2,1,0:T(8,128)S(1)} %select_bitcast_fusion.6), channel_id=1, source_target_pairs={{0,128},{32,160},{64,192},{96,224},{128,0},{160,32},{192,64},{224,... | collective-permute-start | bytes 294920 | tf_op jit(solution)/shard_map/ppermute | solution.py:335
  175.2 9.9 %collective-permute-start.12 = (f32[32,384]{1,0:T(8,128)S(1)}, f32[32,384]{1,0:T(8,128)S(1)}, u32[]{:S(2)}, u32[]{:S(2)}) collective-permute-start(f32[32,384]{1,0:T(8,128)S(1)} %select_bitcast_fusion.11), channel_id=1, source_target_pairs={{0,256},{32,288},{64,320},{96,352},{128,384},{160,416},{192,448},{... | collective-permute-start | bytes 147464 | tf_op jit(solution)/shard_map/ppermute | solution.py:335
  185.1 27.3 %collective-permute-start.13 = (f32[2,2,4,384]{3,2,1,0:T(4,128)S(1)}, f32[2,2,4,384]{3,2,1,0:T(4,128)S(1)}, u32[]{:S(2)}, u32[]{:S(2)}) collective-permute-start(f32[2,2,4,384]{3,2,1,0:T(4,128)S(1)} %select_bitcast_fusion.16), channel_id=1, source_target_pairs={{0,4},{1,5},{2,6},{3,7},{4,0},{5,1},{6,2},{7,3},{8,12},{9,13},{10,... | collective-permute-start | bytes 73736 | tf_op jit(solution)/shard_map/ppermute | solution.py:335
  212.5 6.5 %collective-permute-start.14 = (f32[2,4,384]{2,1,0:T(4,128)S(1)}, f32[2,4,384]{2,1,0:T(4,128)S(1)}, u32[]{:S(2)}, u32[]{:S(2)}) collective-permute-start(f32[2,4,384]{2,1,0:T(4,128)S(1)} %select_bitcast_fusion.21), channel_id=1, source_target_pairs={{0,8},{1,9},{2,10},{3,11},{4,12},{5,13},{6,14},{7,15},{8,0},{9,1},... | collective-permute-start | bytes 36872 | tf_op jit(solution)/shard_map/ppermute | solution.py:335
  219.0 9.4 %collective-permute-start.15 = (f32[4,384]{1,0:T(4,128)S(1)}, f32[4,384]{1,0:T(4,128)S(1)}, u32[]{:S(2)}, u32[]{:S(2)}) collective-permute-start(f32[4,384]{1,0:T(4,128)S(1)} %select_bitcast_fusion.24), channel_id=1, source_target_pairs={{0,16},{1,17},{2,18},{3,19},{4,20},{5,21},{6,22},{7,23},{8,24},{9,... | collective-permute-start | bytes 18440 | tf_op jit(solution)/shard_map/ppermute | solution.py:335
  228.4 9.9 %collective-permute-start.16 = (f32[1,384]{1,0:T(1,128)S(1)}, f32[1,384]{1,0:T(1,128)S(1)}, u32[]{:S(2)}, u32[]{:S(2)}) collective-permute-start(f32[1,384]{1,0:T(1,128)S(1)} %get-tuple-element.50), channel_id=1, source_target_pairs={{0,3},{1,2},{2,1},{3,0},{4,7},{5,6},{6,5},{7,4},{8,11},{9,10},{10,... | collective-permute-start | bytes 4616 | tf_op jit(solution)/shard_map/ppermute | solution.py:335
  230.9 7.4 %collective-permute-start.17 = (f32[1,384]{1,0:T(1,128)S(1)}, f32[1,384]{1,0:T(1,128)S(1)}, u32[]{:S(2)}, u32[]{:S(2)}) collective-permute-start(f32[1,384]{1,0:T(1,128)S(1)} %get-tuple-element.49), channel_id=1, source_target_pairs={{0,2},{1,3},{2,0},{3,1},{4,6},{5,7},{6,4},{7,5},{8,10},{9,11},{10,... | collective-permute-start | bytes 4616 | tf_op jit(solution)/shard_map/ppermute | solution.py:335
  235.5 5.5 %collective-permute-start.18 = (f32[1,384]{1,0:T(1,128)S(1)}, f32[1,384]{1,0:T(1,128)S(1)}, u32[]{:S(2)}, u32[]{:S(2)}) collective-permute-start(f32[1,384]{1,0:T(1,128)S(1)} %get-tuple-element.48), channel_id=1, source_target_pairs={{0,1},{1,0},{2,3},{3,2},{4,5},{5,4},{6,7},{7,6},{8,9},{9,8},{10,11... | collective-permute-start | bytes 4616 | tf_op jit(solution)/shard_map/ppermute | solution.py:335
  241.6 1.5 copy-start

commit v2 on v1

--- a/solution.py
+++ b/solution.py
@@ -1,5 +1,3 @@
-import functools
-
 import jax
 import jax.numpy as jnp
 from jax import lax
@@ -23,8 +21,8 @@
 TEXT = 512
 GTEXT = 256
 BLOCK = 2 * HPD * 2 * BUCKET
-TG_ROWS = 32
-OUT_ROWS = OWN * BLOCK + TG_ROWS
+TEXT_ROWS = 32
+MSG_ROWS = OWN * BLOCK + TEXT_ROWS
 
 
 def iota(shape, dim):
@@ -108,7 +106,7 @@
     return owners, jnp.where(mine == owners, 1.0, 0.0)
 
 
-def pack_kernel(msg_ref, dest_ref, q_ref, k_ref, v_ref, g_ref, out_ref, own_ref, sel_ref):
+def pack_kernel(msg_ref, dest_ref, text_ref, q_ref, k_ref, v_ref, g_ref, out_ref, own_ref, sel_ref):
     @pl.when(pl.program_id(0) == 0)
     def _():
         owners, match = owner_match(msg_ref, dest_ref)
@@ -124,29 +122,37 @@
             for h in range(HPD):
                 off = i * BLOCK + (pair * HPD + h) * 2 * BUCKET
                 out_ref[:, 0, off : off + 2 * BUCKET, :] = both[:, i, :, h * LANES : (h + 1) * LANES]
-
-
-def pack(msg, dest, q, k, v, g):
+    text = text_ref[...].astype(F32)
+    for c in range(2):
+        tile = jnp.concatenate(
+            [text[:, 2 * c * LANES : (2 * c + 1) * LANES], text[:, (2 * c + 1) * LANES : (2 * c + 2) * LANES]], axis=0
+        ).astype(BF16)
+        off = OWN * BLOCK + c * 2 * BUCKET
+        for z in range(NZ):
+            out_ref[z, 0, off : off + 2 * BUCKET, :] = tile
+
+
+def pack(msg, dest, text, q, k, v, g):
     full = lambda shape: pl.BlockSpec(shape, lambda x: (0,) * len(shape))
     cols = pl.BlockSpec((ROWS, COLS), lambda x: (0, x))
     return pl.pallas_call(
         pack_kernel,
         grid=(NX,),
-        in_specs=[full((PEERS * 8, LANES)), full((1, LANES)), cols, cols, cols, cols],
+        in_specs=[full((PEERS * 8, LANES)), full((1, LANES)), full((BUCKET, TEXT)), cols, cols, cols, cols],
         out_specs=[
-            pl.BlockSpec((NZ, 1, OWN * BLOCK, LANES), lambda x: (0, x, 0, 0)),
+            pl.BlockSpec((NZ, 1, MSG_ROWS, LANES), lambda x: (0, x, 0, 0)),
             full((COMPACT, LANES)),
         ],
         out_shape=[
-            jax.ShapeDtypeStruct((NZ, NX, OWN * BLOCK, LANES), BF16),
+            jax.ShapeDtypeStruct((NZ, NX, MSG_ROWS, LANES), BF16),
             jax.ShapeDtypeStruct((COMPACT, LANES), F32),
         ],
         scratch_shapes=[pltpu.VMEM((COMPACT * BUCKET, LANES), BF16)],
         name="pack",
-    )(msg, dest, q, k, v, g)
-
-
-def attend_kernel(z_ref, msg_ref, own_ref, in_ref, text_ref, w_ref, out_ref, wg_ref, acc_ref):
+    )(msg, dest, text, q, k, v, g)
+
+
+def attend_kernel(z_ref, msg_ref, own_ref, in_ref, tail_ref, w_ref, out_ref, wg_ref, acc_ref, text_ref):
     i = pl.program_id(0)
     n = SLOTS
 
@@ -173,6 +179,15 @@
     label_row = jnp.sum(jnp.where(diag, label_b, 0.0), axis=0, keepdims=True)
     allowed = ((label_b == jnp.broadcast_to(label_row, (n, n))) & (label_b >= 0.0)) | diag
     bias = jnp.where(allowed, 0.0, -1e30)
+
+    @pl.when(i == 0)
+    def _():
+        for c in range(2):
+            tiles = tail_ref[:, c * 2 * BUCKET : (c + 1) * 2 * BUCKET, :].astype(F32)
+            tiles = tiles.reshape(PEERS, 2, BUCKET, LANES)
+            for half in range(2):
+                span = slice((2 * c + half) * LANES, (2 * c + half + 1) * LANES)
+                text_ref[:, span] = tiles[:, half].reshape(GTEXT, LANES).astype(BF16)
 
     pick = jnp.where(lanef == align, 1.0, 0.0).astype(BF16)
     cond = dot(pick, text_ref[...]).astype(BF16)
@@ -242,7 +257,7 @@
         wg_ref[...] = dot_tn(text, high) + dot_tn(text, low)
 
 
-def attend(zi, msg, own, got, text, w):
+def attend(zi, msg, own, got, w):
     full = lambda shape: pl.BlockSpec(shape, lambda i, z: (0,) * len(shape))
     return pl.pallas_call(
         attend_kernel,
@@ -253,18 +268,19 @@
                 full((PEERS * 8, LANES)),
                 full((COMPACT, LANES)),
                 pl.BlockSpec((PEERS, BLOCK, LANES), lambda i, z: (0, i, 0)),
-                full((GTEXT, TEXT)),
+                pl.BlockSpec((PEERS, TEXT_ROWS, LANES), lambda i, z: (0, OWN * BLOCK // TEXT_ROWS, 0)),
                 full((TEXT, COLS)),
             ],
-            out_specs=[full((PEERS, OUT_ROWS, LANES)), full((TEXT, COLS))],
-            scratch_shapes=[pltpu.VMEM((GTEXT, COLS), F32)],
+            out_specs=[full((PEERS, MSG_ROWS, LANES)), full((TEXT, COLS))],
+            scratch_shapes=[pltpu.VMEM((GTEXT, COLS), F32), pltpu.VMEM((GTEXT, TEXT), BF16)],
         ),
         out_shape=[
-            jax.ShapeDtypeStruct((PEERS, OUT_ROWS, LANES), BF16),
+            jax.ShapeDtypeStruct((PEERS, MSG_ROWS, LANES), BF16),
             jax.ShapeDtypeStruct((TEXT, COLS), F32),
         ],
+        compiler_params=pltpu.CompilerParams(vmem_limit_bytes=24 << 20),
         name="attend",
-    )(zi, msg, own, got, text, w)
+    )(zi, msg, own, got, got, w)
 
 
 def unpack_kernel(msg_ref, dest_ref, in_ref, o_ref, q_ref, k_ref, v_ref, tg_ref, sel_ref):
@@ -317,11 +333,12 @@
         in_specs=[
             full((PEERS * 8, LANES)),
             full((1, LANES)),
-            pl.BlockSpec((NZ, 1, OUT_ROWS, LANES), lambda x: (0, x, 0, 0)),
+            pl.BlockSpec((NZ, 1, MSG_ROWS, LANES), lambda x: (0, x, 0, 0)),
         ],
         out_specs=[cols, cols, cols, cols, full((BUCKET, TEXT))],
         out_shape=[rows, rows, rows, rows, jax.ShapeDtypeStruct((BUCKET, TEXT), F32)],
         scratch_shapes=[pltpu.VMEM((ROWS, COMPACT * BUCKET), BF16)],
+        compiler_params=pltpu.CompilerParams(vmem_limit_bytes=24 << 20),
         name="unpack",
     )(msg, dest, got)
 
@@ -352,41 +369,68 @@
     return jnp.where(up, one, zero) + swap(jnp.where(up, zero, one), axis, bit)
 
 
+def x_split_kernel(x_ref, in_ref, *out_refs):
+    for f, out_ref in enumerate(out_refs):
+        for j in range(NZ):
+            out_ref[pl.ds(j, 1), :] = in_ref[pl.ds(j * NX + (x_ref[0] ^ f), 1), :]
+
+
+def z_split_kernel(z_ref, *refs):
+    for f, out_ref in enumerate(refs[NX:]):
+        for j in range(NX):
+            out_ref[pl.ds(j, 1), :] = refs[j][pl.ds(z_ref[0] ^ f, 1), :]
+
+
+def row_sum_kernel(x_ref, *refs):
+    out_ref, total_ref = refs[NZ:]
+    total = refs[0][...]
+    for f in range(1, NZ):
+        total = total + refs[f][...]
+    total_ref[...] = total
+    for c in range(NX):
+        out_ref[:, c * COLS : (c + 1) * COLS] = total_ref[pl.ds(x_ref[0] ^ c, 1), :]
+
+
+def small_call(kernel, outs, scratch, index, *args):
+    return pl.pallas_call(
+        kernel,
+        out_shape=[jax.ShapeDtypeStruct(shape, F32) for shape in outs],
+        in_specs=[pl.BlockSpec(memory_space=pltpu.SMEM)]
+        + [pl.BlockSpec(memory_space=pltpu.VMEM)] * len(args),
+        scratch_shapes=scratch,
+        compiler_params=pltpu.CompilerParams(vmem_limit_bytes=4 << 20),
+    )(index, *args)
+
+
+def reduce_weight(wg, zi, xi):
+    wg = wg.reshape(2, 2, 2, 2, PEERS, COLS)
+    wg = halve(wg, "dp", 1, 3)
+    for bit, dim in ((2, 2), (4, 1), (8, 0)):
+        wg = halve(wg, "dp", bit, dim)
+    parts = small_call(x_split_kernel, [(NZ, COLS)] * NX, [], xi, wg)
+    parts = [parts[0]] + [swap(parts[f], "seq", f) for f in range(1, NX)]
+    parts = small_call(z_split_kernel, [(NX, COLS)] * NZ, [], zi, *parts)
+    parts = [parts[0]] + [swap(parts[f], "seq", f * NX) for f in range(1, NZ)]
+    return small_call(row_sum_kernel, [(1, NX * COLS)], [pltpu.VMEM((NX, COLS), F32)], xi, *parts)[0]
+
+
 def local(query, key, value, text, cond_weight, cotangent, dest, segment, align):
-    seq = lax.axis_index("seq")
-    zi = (seq // NX).astype(jnp.int32).reshape(1)
-    xi = seq % NX
+    seq = lax.axis_index("seq").astype(jnp.int32)
+    zi = (seq >> 2).reshape(1)
+    xi = (seq & 3).reshape(1)
     dest_row = dest.reshape(1, ROWS)
     first = prep(dest_row, align.reshape(1, ROWS), segment.reshape(1, SLOTS), cond_weight)
     msg3 = exchange(first.reshape(PEERS, 8, LANES))
     msg = msg3.reshape(PEERS * 8, LANES)
-    packed, own = pack(msg, dest_row, query, key, value, cotangent)
-    got = exchange(packed.reshape(PEERS, OWN * BLOCK, LANES))
+    packed, own = pack(msg, dest_row, text, query, key, value, cotangent)
+    got = exchange(packed.reshape(PEERS, MSG_ROWS, LANES))
     my_w = msg3[:, 4 : 4 + HPD, :].astype(BF16).reshape(PEERS, COLS)
     full_w = gather_bits(my_w, "dp", (8, 4, 2, 1)).reshape(TEXT, COLS)
-    full_text = gather_bits(text, "seq", (16, 8, 4, 2, 1)).reshape(GTEXT, TEXT)
-    back, wg = attend(zi, msg, own, got, full_text, full_w)
+    back, wg = attend(zi, msg, own, got, full_w)
     returned = exchange(back)
-    wg = wg.reshape(2, 2, 2, 2, PEERS, COLS)
-    for bit, dim in ((1, 3), (2, 2), (4, 1), (8, 0)):
-        wg = halve(wg, "dp", bit, dim)
-    wg = wg.reshape(2, 2, 2, NX, COLS)
-    for bit, dim in ((4, 2), (8, 1), (16, 0)):
-        wg = halve(wg, "seq", bit, dim)
-    pieces = [lax.dynamic_index_in_dim(wg, xi, 0, True)]
-    for flip in (1, 2, 3):
-        row = lax.dynamic_index_in_dim(wg, xi ^ flip, 0, True)
-        pieces.append(swap(row, "seq", flip))
-    out_cols = []
-    for c in range(NX):
-        flip = xi ^ c
-        col = pieces[0]
-        for m in (1, 2, 3):
-            col = jnp.where(flip == m, pieces[m], col)
-        out_cols.append(col)
-    weight_grad = jnp.concatenate(out_cols, axis=1)
+    weight_grad = reduce_weight(wg, zi, xi)
     attended, query_grad, key_grad, value_grad, text_grad = unpack(
-        msg, dest_row, returned.reshape(NZ, NX, OUT_ROWS, LANES)
+        msg, dest_row, returned.reshape(NZ, NX, MSG_ROWS, LANES)
     )
     return attended, query_grad, key_grad, value_grad, text_grad, weight_grad
 

time: 249 us -> 198 us (0.80)
  the two profiles are of different devices: /device:TPU:4 before, /device:TPU:1 now
where the time goes in v2:
time: 198 us; the launch traced here: 194 us
  starting transfers between devices  90.9 us (46%)
  waiting for transfers between devices  55.1 us (28%)
  blocking collectives  23.2 us (12%)
  Pallas kernels  21.1 us (11%)
  local copies, waits for them, and re-layouts  2.5 us (1%)
    ppermute x18, starting transfers between devices, swap(): return lax.ppermute(x, axis, [(j, j ^ bit) for j in range(size)])  79.5 us
    all_to_all x2, waiting for transfers between devices, exchange(): return lax.all_to_all(x, 'seq', split_axis=0, concat_axis=0, tiled=True)  30.1 us
    ppermute x18, waiting for transfers between devices, swap(): return lax.ppermute(x, axis, [(j, j ^ bit) for j in range(size)])  25 us
    all_to_all x1, blocking collectives, exchange(): return lax.all_to_all(x, 'seq', split_axis=0, concat_axis=0, tiled=True)  23.2 us
    all_to_all x2, starting transfers between devices, exchange(): return lax.all_to_all(x, 'seq', split_axis=0, concat_axis=0, tiled=True)  11.4 us
    pallas_call x1, Pallas kernels, attend(): pl.pallas_call(attend_kernel, grid_spec=pltpu.PrefetchScalarGridSpec(num_...  10.6 us
    pallas_call x1, Pallas kernels, pack(): pl.pallas_call(pack_kernel, grid=(NX,), in_specs=[full((PEERS * 8, LANES)...  5.01 us
  transfers between devices with their start and end apart: 20, of which 12 were waited for; matrix products, arithmetic and copies ran while one was open for 0% of the time, Pallas kernels for 0%

profile of v2, /device:TPU:1, one launch (start us, length us, event | category | flops | bytes accessed | tf_op | source)
XLA Modules:
  0.0 194.2 jit_solution(5279791881073323874)
XLA Ops:
  2.0 23.2 %all_to_all.15 = f32[32,8,128]{2,1,0:T(8,128)} all-to-all(f32[32,8,128]{2,1,0:T(8,128)} %bitcast.59), channel_id=1, replica_groups=mesh['dp'=16,'seq'=32] {'seq'}, dimensions={0} | all-to-all | bytes 262144 | tf_op jit(solution)/shard_map/all_to_all | solution.py:347
  25.2 5.0 %pack.1 = (bf16[8,4,320,128]{3,2,1,0:T(8,128)(2,1)}, f32[24,128]{1,0:T(8,128)}) custom-call(f32[256,128]{1,0:T(8,128)} %bitcast.50, s32[1,128]{1,0:T(1,128)} %bitcast.56, bf16[8,512]{1,0:T(8,128)(2,1)} %text_ref.1, bf16[128,1536]{1,0:T(8,128)(2,1)} %q_ref.1, bf16[128,1536]{1,0:T(8,128)(2,1)} %k_ref.1, bf16[128,1536]{1,0:T(8,128)(2,1)} %v_ref.1, ...), custom_call_target="tpu_custom_call" | custom-call | tf_op jit(solution)/shard_map/pack/pallas_call | solution.py:138
  30.2 4.2 %all-to-all-start.1 = ((bf16[32,320,128]{2,1,0:T(8,128)(2,1)}), bf16[32,320,128]{2,1,0:T(8,128)(2,1)S(1)}, u32[]{:S(2)}, u32[]{:S(2)}) async-start(bf16[32,320,128]{2,1,0:T(8,128)(2,1)} %bitcast.58), calls=%async_computation.1 | async-start | bytes 5242880 | tf_op jit(solution)/shard_map/all_to_all | solution.py:347
  34.5 7.5 %collective-permute-start = (bf16[32,384]{1,0:T(8,128)(2,1)S(1)}, bf16[32,384]{1,0:T(8,128)(2,1)S(1)}, u32[]{:S(2)}, u32[]{:S(2)}) collective-permute-start(bf16[32,384]{1,0:T(8,128)(2,1)S(1)} %bitcast.62), channel_id=1, source_target_pairs={{0,256},{32,288},{64,320},{96,352},{128,384},{160,416},{192,448},{... | collective-permute-start | bytes 73736 | tf_op jit(solution)/shard_map/ppermute | solution.py:352
  43.2 4.3 %collective-permute-start.1 = (bf16[2,32,384]{2,1,0:T(8,128)(2,1)S(1)}, bf16[2,32,384]{2,1,0:T(8,128)(2,1)S(1)}, u32[]{:S(2)}, u32[]{:S(2)}) collective-permute-start(bf16[2,32,384]{2,1,0:T(8,128)(2,1)S(1)} %pad_maximum_fusion.3), channel_id=1, source_target_pairs={{0,128},{32,160},{64,192},{96,224},{128,0},{160,32},{192,64},{224,... | collective-permute-start | bytes 147464 | tf_op jit(solution)/shard_map/ppermute | solution.py:352
  47.5 1.8 collective-permute-done.1
  49.3 3.0 %collective-permute-start.2 = (bf16[2,2,32,384]{3,2,0,1:T(8,128)(2,1)S(1)}, bf16[2,2,32,384]{3,2,0,1:T(8,128)(2,1)S(1)}, u32[]{:S(2)}, u32[]{:S(2)}) collective-permute-start(bf16[2,2,32,384]{3,2,0,1:T(8,128)(2,1)S(1)} %pad_maximum_fusion.2), channel_id=1, source_target_pairs={{0,64},{32,96},{64,0},{96,32},{128,192},{160,224},{192,128},{224,1... | collective-permute-start | bytes 294920 | tf_op jit(solution)/shard_map/ppermute | solution.py:352
  52.3 2.7 %collective-permute-done.2 = bf16[2,2,32,384]{3,2,0,1:T(8,128)(2,1)S(1)} collective-permute-done((bf16[2,2,32,384]{3,2,0,1:T(8,128)(2,1)S(1)}, bf16[2,2,32,384]{3,2,0,1:T(8,128)(2,1)S(1)}, u32[]{:S(2)}, u32[]{:S(2)}) %collective-permute-start.2) | collective-permute-done | bytes 98336 | tf_op jit(solution)/shard_map/ppermute | solution.py:352
  55.0 6.6 %collective-permute-start.3 = (bf16[2,2,2,32,384]{4,3,0,1,2:T(8,128)(2,1)S(1)}, bf16[2,2,2,32,384]{4,3,0,1,2:T(8,128)(2,1)S(1)}, u32[]{:S(2)}, u32[]{:S(2)}) collective-permute-start(bf16[2,2,2,32,384]{4,3,0,1,2:T(8,128)(2,1)S(1)} %pad_maximum_fusion.1), channel_id=1, source_target_pairs={{0,32},{32,0},{64,96},{96,64},{128,160},{160,128},{192,224},{224,1... | collective-permute-start | bytes 589832 | tf_op jit(solution)/shard_map/ppermute | solution.py:352
  62.8 30.1 %all-to-all-done.1.in_ref.tail_ref = bf16[32,320,128]{2,1,0:T(8,128)(2,1)S(1)} async-done(((bf16[32,320,128]{2,1,0:T(8,128)(2,1)}), bf16[32,320,128]{2,1,0:T(8,128)(2,1)S(1)}, u32[]{:S(2)}, u32[]{:S(2)}) %all-to-all-start.1) | async-done | bytes 2621472 | tf_op jit(solution)/shard_map/all_to_all | solution.py:347
  92.9 10.6 %attend.1 = (bf16[32,320,128]{2,1,0:T(8,128)(2,1)S(1)}, f32[512,384]{1,0:T(8,128)S(1)}) custom-call(s32[1]{0:T(128)} %bitcast.5.z_ref, f32[256,128]{1,0:T(8,128)S(1)} %bitcast.51, f32[24,128]{1,0:T(8,128)S(1)} %copy-done.4, bf16[32,320,128]{2,1,0:T(8,128)(2,1)S(1)} %all-to-all-done.1.in_ref.tail_ref, ...), custom_call_target="tpu_custom_call" | custom-call | tf_op jit(solution)/shard_map/attend/pallas_call | solution.py:262
  105.9 7.2 %all-to-all-start.2 = ((bf16[32,320,128]{2,1,0:T(8,128)(2,1)}), bf16[32,320,128]{2,1,0:T(8,128)(2,1)S(1)}, u32[]{:S(2)}, u32[]{:S(2)}) async-start(bf16[32,320,128]{2,1,0:T(8,128)(2,1)} %copy-done), calls=%async_computation.2 | async-start | bytes 5242880 | tf_op jit(solution)/shard_map/all_to_all | solution.py:347
  113.3 4.6 %collective-permute-start.4 = (f32[2,2,2,32,384]{4,3,0,1,2:T(8,128)S(1)}, f32[2,2,2,32,384]{4,3,0,1,2:T(8,128)S(1)}, u32[]{:S(2)}, u32[]{:S(2)}) collective-permute-start(f32[2,2,2,32,384]{4,3,0,1,2:T(8,128)S(1)} %select_bitcast_fusion), channel_id=1, source_target_pairs={{0,32},{32,0},{64,96},{96,64},{128,160},{160,128},{192,224},{224,1... | collective-permute-start | bytes 1179656 | tf_op jit(solution)/shard_map/ppermute | solution.py:352
  119.3 3.2 %collective-permute-start.5 = (f32[2,2,32,384]{3,2,0,1:T(8,128)S(1)}, f32[2,2,32,384]{3,2,0,1:T(8,128)S(1)}, u32[]{:S(2)}, u32[]{:S(2)}) collective-permute-start(f32[2,2,32,384]{3,2,0,1:T(8,128)S(1)} %select_bitcast_fusion.1), channel_id=1, source_target_pairs={{0,64},{32,96},{64,0},{96,32},{128,192},{160,224},{192,128},{224,1... | collective-permute-start | bytes 589832 | tf_op jit(solution)/shard_map/ppermute | solution.py:352
  122.5 4.8 %collective-permute-done.5 = f32[2,2,32,384]{3,2,0,1:T(8,128)S(1)} collective-permute-done((f32[2,2,32,384]{3,2,0,1:T(8,128)S(1)}, f32[2,2,32,384]{3,2,0,1:T(8,128)S(1)}, u32[]{:S(2)}, u32[]{:S(2)}) %collective-permute-start.5) | collective-permute-done | bytes 196640 | tf_op jit(solution)/shard_map/ppermute | solution.py:352
  127.3 4.2 %collective-permute-start.6 = (f32[2,32,384]{2,1,0:T(8,128)S(1)}, f32[2,32,384]{2,1,0:T(8,128)S(1)}, u32[]{:S(2)}, u32[]{:S(2)}) collective-permute-start(f32[2,32,384]{2,1,0:T(8,128)S(1)} %select_bitcast_fusion.4), channel_id=1, source_target_pairs={{0,128},{32,160},{64,192},{96,224},{128,0},{160,32},{192,64},{224,... | collective-permute-start | bytes 294920 | tf_op jit(solution)/shard_map/ppermute | solution.py:352
  131.5 2.3 %collective-permute-done.6 = f32[2,32,384]{2,1,0:T(8,128)S(1)} collective-permute-done((f32[2,32,384]{2,1,0:T(8,128)S(1)}, f32[2,32,384]{2,1,0:T(8,128)S(1)}, u32[]{:S(2)}, u32[]{:S(2)}) %collective-permute-start.6) | collective-permute-done | bytes 98336 | tf_op jit(solution)/shard_map/ppermute | solution.py:352
  133.9 10.0 %collective-permute-start.7 = (f32[32,384]{1,0:T(8,128)S(1)}, f32[32,384]{1,0:T(8,128)S(1)}, u32[]{:S(2)}, u32[]{:S(2)}) collective-permute-start(f32[32,384]{1,0:T(8,128)S(1)} %select_bitcast_fusion.7), channel_id=1, source_target_pairs={{0,256},{32,288},{64,320},{96,352},{128,384},{160,416},{192,448},{... | collective-permute-start | bytes 147464 | tf_op jit(solution)/shard_map/ppermute | solution.py:352
  143.9 1.8 collective-permute-done.7
  145.7 3.4 %collective-permute-start.8 = (f32[8,384]{1,0:T(8,128)S(1)}, f32[8,384]{1,0:T(8,128)S(1)}, u32[]{:S(2)}, u32[]{:S(2)}) collective-permute-start(f32[8,384]{1,0:T(8,128)S(1)} %get-tuple-element.37), channel_id=1, source_target_pairs={{0,1},{1,0},{2,3},{3,2},{4,5},{5,4},{6,7},{7,6},{8,9},{9,8},{10,11... | collective-permute-start | bytes 36872 | tf_op jit(solution)/shard_map/ppermute | solution.py:352
  149.1 4.0 %collective-permute-start.9 = (f32[8,384]{1,0:T(8,128)S(1)}, f32[8,384]{1,0:T(8,128)S(1)}, u32[]{:S(2)}, u32[]{:S(2)}) collective-permute-start(f32[8,384]{1,0:T(8,128)S(1)} %get-tuple-element.38), channel_id=1, source_target_pairs={{0,2},{1,3},{2,0},{3,1},{4,6},{5,7},{6,4},{7,5},{8,10},{9,11},{10,... | collective-permute-start | bytes 36872 | tf_op jit(solution)/shard_map/ppermute | solution.py:352
  153.2 2.2 %collective-permute-start.10 = (f32[8,384]{1,0:T(8,128)S(1)}, f32[8,384]{1,0:T(8,128)S(1)}, u32[]{:S(2)}, u32[]{:S(2)}) collective-permute-start(f32[8,384]{1,0:T(8,128)S(1)} %get-tuple-element.39), channel_id=1, source_target_pairs={{0,3},{1,2},{2,1},{3,0},{4,7},{5,6},{6,5},{7,4},{8,11},{9,10},{10,... | collective-permute-start | bytes 36872 | tf_op jit(solution)/shard_map/ppermute | solution.py:352
  155.5 4.4 %collective-permute-done.10.refs_3_ = f32[8,384]{1,0:T(8,128)S(1)} collective-permute-done((f32[8,384]{1,0:T(8,128)S(1)}, f32[8,384]{1,0:T(8,128)S(1)}, u32[]{:S(2)}, u32[]{:S(2)}) %collective-permute-start.10) | collective-permute-done | bytes 12320 | tf_op jit(solution)/shard_map/ppermute | solution.py:352
  159.9 2.9 %collective-permute-start.11 = (f32[4,384]{1,0:T(4,128)S(1)}, f32[4,384]{1,0:T(4,128)S(1)}, u32[]{:S(2)}, u32[]{:S(2)}) collective-permute-start(f32[4,384]{1,0:T(4,128)S(1)} %get-tuple-element.41), channel_id=1, source_target_pairs={{0,4},{1,5},{2,6},{3,7},{4,0},{5,1},{6,2},{7,3},{8,12},{9,13},{10,... | collective-permute-start | bytes 18440 | tf_op jit(solution)/shard_map/ppermute | solution.py:352
  162.8 3.5 %collective-permute-start.12 = (f32[4,384]{1,0:T(4,128)S(1)}, f32[4,384]{1,0:T(4,128)S(1)}, u32[]{:S(2)}, u32[]{:S(2)}) collective-permute-start(f32[4,384]{1,0:T(4,128)S(1)} %get-tuple-element.42), channel_id=1, source_target_pairs={{0,8},{1,9},{2,10},{3,11},{4,12},{5,13},{6,14},{7,15},{8,0},{9,1},... | collective-permute-start | bytes 18440 | tf_op jit(solution)/shard_map/ppermute | solution.py:352
  166.3 2.9 %collective-permute-start.13 = (f32[4,384]{1,0:T(4,128)S(1)}, f32[4,384]{1,0:T(4,128)S(1)}, u32[]{:S(2)}, u32[]{:S(2)}) collective-permute-start(f32[4,384]{1,0:T(4,128)S(1)} %get-tuple-element.43), channel_id=1, source_target_pairs={{0,12},{1,13},{2,14},{3,15},{4,8},{5,9},{6,10},{7,11},{8,4},{9,5},... | collective-permute-start | bytes 18440 | tf_op jit(solution)/shard_map/ppermute | solution.py:352
  169.2 8.0 %collective-permute-start.14 = (f32[4,384]{1,0:T(4,128)S(1)}, f32[4,384]{1,0:T(4,128)S(1)}, u32[]{:S(2)}, u32[]{:S(2)}) collective-permute-start(f32[4,384]{1,0:T(4,128)S(1)} %get-tuple-element.44), channel_id=1, source_target_pairs={{0,16},{1,17},{2,18},{3,19},{4,20},{5,21},{6,22},{7,23},{8,24},{9,... | collective-permute-start | bytes 18440 | tf_op jit(solution)/shard_map/ppermute | solution.py:352
  177.2 1.9 collective-permute-start.15
  179.1 5.5 %collective-permute-start.16 = (f32[4,384]{1,0:T(4,128)S(1)}, f32[4,384]{1,0:T(4,128)S(1)}, u32[]{:S(2)}, u32[]{:S(2)}) collective-permute-start(f32[4,384]{1,0:T(4,128)S(1)} %get-tuple-element.46), channel_id=1, source_target_pairs={{0,24},{1,25},{2,26},{3,27},{4,28},{5,29},{6,30},{7,31},{8,16},{9,... | collective-permute-start | bytes 18440 | tf_op jit(solution)/shard_map/ppermute | solution.py:352
  184.6 1.9 collective-permute-start.17
  186.6 3.6 %collective-permute-done.17.refs_7_ = f32[4,384]{1,0:T(4,128)S(1)} collective-permute-done((f32[4,384]{1,0:T(4,128)S(1)}, f32[4,384]{1,0:T(4,128)S(1)}, u32[]{:S(2)}, u32[]{:S(2)}) %collective-permute-start.17) | collective-permute-done | bytes 6176 | tf_op jit(solution)/shard_map/ppermute | solution.py:352
  190.8 3.4 %unpack.1 = (bf16[128,1536]{1,0:T(8,128)(2,1)}, bf16[128,1536]{1,0:T(8,128)(2,1)}, bf16[128,1536]{1,0:T(8,128)(2,1)}, bf16[128,1536]{1,0:T(8,128)(2,1)}, f32[8,512]{1,0:T(8,128)}) custom-call(f32[256,128]{1,0:T(8,128)S(1)} %bitcast.52, s32[1,128]{1,0:T(1,128)S(1)} %bitcast.57, bf16[8,4,320,128]{3,2,1,0:T(8,128)(2,1)S(1)} %bitcast.49), custom_call_target="tpu_custom_call" | custom-call | tf_op jit(solution)/shard_map/unpack/pallas_call | solution.py:330
  (48 shorter events, 8.7 us)
Async XLA Ops:
  30.2 4.2 %copy-start.1 = (f32[32,8,128]{2,1,0:T(8,128)S(1)}, f32[32,8,128]{2,1,0:T(8,128)}, u32[]{:S(2)}) copy-start(f32[32,8,128]{2,1,0:T(8,128)} %all_to_all.15) | copy-start | bytes 393220
  30.2 62.7 %all-to-all-start.1 = ((bf16[32,320,128]{2,1,0:T(8,128)(2,1)}), bf16[32,320,128]{2,1,0:T(8,128)(2,1)S(1)}, u32[]{:S(2)}, u32[]{:S(2)}) async-start(bf16[32,320,128]{2,1,0:T(8,128)(2,1)} %bitcast.58), calls=%async_computation.1 | async-start | bytes 5242880 | tf_op jit(solution)/shard_map/all_to_all | solution.py:347
  34.4 58.5 %copy-start.4 = (f32[24,128]{1,0:T(8,128)S(1)}, f32[24,128]{1,0:T(8,128)}, u32[]{:S(2)}) copy-start(f32[24,128]{1,0:T(8,128)} %get-tuple-element.27.own_ref) | copy-start | bytes 36868
  34.5 8.7 %collective-permute-start = (bf16[32,384]{1,0:T(8,128)(2,1)S(1)}, bf16[32,384]{1,0:T(8,128)(2,1)S(1)}, u32[]{:S(2)}, u32[]{:S(2)}) collective-permute-start(bf16[32,384]{1,0:T(8,128)(2,1)S(1)} %bitcast.62), channel_id=1, source_target_pairs={{0,256},{32,288},{64,320},{96,352},{128,384},{160,416},{192,448},{... | collective-permute-start | bytes 73736 | tf_op jit(solution)/shard_map/ppermute | solution.py:352
  43.2 6.1 %collective-permute-start.1 = (bf16[2,32,384]{2,1,0:T(8,128)(2,1)S(1)}, bf16[2,32,384]{2,1,0:T(8,128)(2,1)S(1)}, u32[]{:S(2)}, u32[]{:S(2)}) collective-permute-start(bf16[2,32,384]{2,1,0:T(8,128)(2,1)S(1)} %pad_maximum_fusion.3), channel_id=1, source_target_pairs={{0,128},{32,160},{64,192},{96,224},{128,0},{160,32},{192,64},{224,... | collective-permute-start | bytes 147464 | tf_op jit(solution)/shard_map/ppermute | solution.py:352
  49.3 5.7 %collective-permute-start.2 = (bf16[2,2,32,384]{3,2,0,1:T(8,128)(2,1)S(1)}, bf16[2,2,32,384]{3,2,0,1:T(8,128)(2,1)S(1)}, u32[]{:S(2)}, u32[]{:S(2)}) collective-permute-start(bf16[2,2,32,384]{3,2,0,1:T(8,128)(2,1)S(1)} %pad_maximum_fusion.2), channel_id=1, source_target_pairs={{0,64},{32,96},{64,0},{96,32},{128,192},{160,224},{192,128},{224,1... | collective-permute-start | bytes 294920 | tf_op jit(solution)/shard_map/ppermute | solution.py:352
  55.0 7.6 %collective-permute-start.3 = (bf16[2,2,2,32,384]{4,3,0,1,2:T(8,128)(2,1)S(1)}, bf16[2,2,2,32,384]{4,3,0,1,2:T(8,128)(2,1)S(1)}, u32[]{:S(2)}, u32[]{:S(2)}) collective-permute-start(bf16[2,2,2,32,384]{4,3,0,1,2:T(8,128)(2,1)S(1)} %pad_maximum_fusion.1), channel_id=1, source_target_pairs={{0,32},{32,0},{64,96},{96,64},{128,160},{160,128},{192,224},{224,1... | collective-permute-start | bytes 589832 | tf_op jit(solution)/shard_map/ppermute | solution.py:352
  103.5 1.5 copy-start
  105.0 0.9 copy-start.2
  105.9 7.3 %copy-start.3 = (f32[512,384]{1,0:T(8,128)S(1)}, f32[512,384]{1,0:T(8,128)}, u32[]{:S(2)}) copy-start(f32[512,384]{1,0:T(8,128)} %copy-done.2) | copy-start | bytes 2359300
  105.9 85.0 %all-to-all-start.2 = ((bf16[32,320,128]{2,1,0:T(8,128)(2,1)}), bf16[32,320,128]{2,1,0:T(8,128)(2,1)S(1)}, u32[]{:S(2)}, u32[]{:S(2)}) async-start(bf16[32,320,128]{2,1,0:T(8,128)(2,1)} %copy-done), calls=%async_computation.2 | async-start | bytes 5242880 | tf_op jit(solution)/shard_map/all_to_all | solution.py:347
  113.2 77.6 %copy-start.5 = (s32[128]{0:T(128)S(1)}, s32[128]{0:T(128)}, u32[]{:S(2)}) copy-start(s32[128]{0:T(128)} %param.15) | copy-start | bytes 1540
  113.3 5.9 %collective-permute-start.4 = (f32[2,2,2,32,384]{4,3,0,1,2:T(8,128)S(1)}, f32[2,2,2,32,384]{4,3,0,1,2:T(8,128)S(1)}, u32[]{:S(2)}, u32[]{:S(2)}) collective-permute-start(f32[2,2,2,32,384]{4,3,0,1,2:T(8,128)S(1)} %select_bitcast_fusion), channel_id=1, source_target_pairs={{0,32},{32,0},{64,96},{96,64},{128,160},{160,128},{192,224},{224,1... | collective-permute-start | bytes 1179656 | tf_op jit(solution)/shard_map/ppermute | solution.py:352
  119.3 8.0 %collective-permute-start.5 = (f32[2,2,32,384]{3,2,0,1:T(8,128)S(1)}, f32[2,2,32,384]{3,2,0,1:T(8,128)S(1)}, u32[]{:S(2)}, u32[]{:S(2)}) collective-permute-start(f32[2,2,32,384]{3,2,0,1:T(8,128)S(1)} %select_bitcast_fusion.1), channel_id=1, source_target_pairs={{0,64},{32,96},{64,0},{96,32},{128,192},{160,224},{192,128},{224,1... | collective-permute-start | bytes 589832 | tf_op jit(solution)/shard_map/ppermute | solution.py:352
  127.3 6.6 %collective-permute-start.6 = (f32[2,32,384]{2,1,0:T(8,128)S(1)}, f32[2,32,384]{2,1,0:T(8,128)S(1)}, u32[]{:S(2)}, u32[]{:S(2)}) collective-permute-start(f32[2,32,384]{2,1,0:T(8,128)S(1)} %select_bitcast_fusion.4), channel_id=1, source_target_pairs={{0,128},{32,160},{64,192},{96,224},{128,0},{160,32},{192,64},{224,... | collective-permute-start | bytes 294920 | tf_op jit(solution)/shard_map/ppermute | solution.py:352
  133.9 11.7 %collective-permute-start.7 = (f32[32,384]{1,0:T(8,128)S(1)}, f32[32,384]{1,0:T(8,128)S(1)}, u32[]{:S(2)}, u32[]{:S(2)}) collective-permute-start(f32[32,384]{1,0:T(8,128)S(1)} %select_bitcast_fusion.7), channel_id=1, source_target_pairs={{0,256},{32,288},{64,320},{96,352},{128,384},{160,416},{192,448},{... | collective-permute-start | bytes 147464 | tf_op jit(solution)/shard_map/ppermute | solution.py:352
  145.7 9.7 %collective-permute-start.8 = (f32[8,384]{1,0:T(8,128)S(1)}, f32[8,384]{1,0:T(8,128)S(1)}, u32[]{:S(2)}, u32[]{:S(2)}) collective-permute-start(f32[8,384]{1,0:T(8,128)S(1)} %get-tuple-element.37), channel_id=1, source_target_pairs={{0,1},{1,0},{2,3},{3,2},{4,5},{5,4},{6,7},{7,6},{8,9},{9,8},{10,11... | collective-permute-start | bytes 36872 | tf_op jit(solution)/shard_map/ppermute | solution.py:352
  149.1 6.3 %collective-permute-start.9 = (f32[8,384]{1,0:T(8,128)S(1)}, f32[8,384]{1,0:T(8,128)S(1)}, u32[]{:S(2)}, u32[]{:S(2)}) collective-permute-start(f32[8,384]{1,0:T(8,128)S(1)} %get-tuple-element.38), channel_id=1, source_target_pairs={{0,2},{1,3},{2,0},{3,1},{4,6},{5,7},{6,4},{7,5},{8,10},{9,11},{10,... | collective-permute-start | bytes 36872 | tf_op jit(solution)/shard_map/ppermute | solution.py:352
  153.2 6.7 %collective-permute-start.10 = (f32[8,384]{1,0:T(8,128)S(1)}, f32[8,384]{1,0:T(8,128)S(1)}, u32[]{:S(2)}, u32[]{:S(2)}) collective-permute-start(f32[8,384]{1,0:T(8,128)S(1)} %get-tuple-element.39), channel_id=1, source_target_pairs={{0,3},{1,2},{2,1},{3,0},{4,7},{5,6},{6,5},{7,4},{8,11},{9,10},{10,... | collective-permute-start | bytes 36872 | tf_op jit(solution)/shard_map/ppermute | solution.py:352
  159.9 19.2 %collective-permute-start.11 = (f32[4,384]{1,0:T(4,128)S(1)}, f32[4,384]{1,0:T(4,128)S(1)}, u32[]{:S(2)}, u32[]{:S(2)}) collective-permute-start(f32[4,384]{1,0:T(4,128)S(1)} %get-tuple-element.41), channel_id=1, source_target_pairs={{0,4},{1,5},{2,6},{3,7},{4,0},{5,1},{6,2},{7,3},{8,12},{9,13},{10,... | collective-permute-start | bytes 18440 | tf_op jit(solution)/shard_map/ppermute | solution.py:352
  162.8 21.9 %collective-permute-start.12 = (f32[4,384]{1,0:T(4,128)S(1)}, f32[4,384]{1,0:T(4,128)S(1)}, u32[]{:S(2)}, u32[]{:S(2)}) collective-permute-start(f32[4,384]{1,0:T(4,128)S(1)} %get-tuple-element.42), channel_id=1, source_target_pairs={{0,8},{1,9},{2,10},{3,11},{4,12},{5,13},{6,14},{7,15},{8,0},{9,1},... | collective-permute-start | bytes 18440 | tf_op jit(solution)/shard_map/ppermute | solution.py:352
  166.3 20.3 %collective-permute-start.13 = (f32[4,384]{1,0:T(4,128)S(1)}, f32[4,384]{1,0:T(4,128)S(1)}, u32[]{:S(2)}, u32[]{:S(2)}) collective-permute-start(f32[4,384]{1,0:T(4,128)S(1)} %get-tuple-element.43), channel_id=1, source_target_pairs={{0,12},{1,13},{2,14},{3,15},{4,8},{5,9},{6,10},{7,11},{8,4},{9,5},... | collective-permute-start | bytes 18440 | tf_op jit(solution)/shard_map/ppermute | solution.py:352
  169.2 17.4 %collective-permute-start.14 = (f32[4,384]{1,0:T(4,128)S(1)}, f32[4,384]{1,0:T(4,128)S(1)}, u32[]{:S(2)}, u32[]{:S(2)}) collective-permute-start(f32[4,384]{1,0:T(4,128)S(1)} %get-tuple-element.44), channel_id=1, source_target_pairs={{0,16},{1,17},{2,18},{3,19},{4,20},{5,21},{6,22},{7,23},{8,24},{9,... | collective-permute-start | bytes 18440 | tf_op jit(solution)/shard_map/ppermute | solution.py:352
  177.2 9.4 %collective-permute-start.15 = (f32[4,384]{1,0:T(4,128)S(1)}, f32[4,384]{1,0:T(4,128)S(1)}, u32[]{:S(2)}, u32[]{:S(2)}) collective-permute-start(f32[4,384]{1,0:T(4,128)S(1)} %get-tuple-element.45), channel_id=1, source_target_pairs={{0,20},{1,21},{2,22},{3,23},{4,16},{5,17},{6,18},{7,19},{8,28},{9,... | collective-permute-start | bytes 18440 | tf_op jit(solution)/shard_map/ppermute | solution.py:352
  179.1 7.5 %collective-permute-start.16 = (f32[4,384]{1,0:T(4,128)S(1)}, f32[4,384]{1,0:T(4,128)S(1)}, u32[]{:S(2)}, u32[]{:S(2)}) collective-permute-start(f32[4,384]{1,0:T(4,128)S(1)} %get-tuple-element.46), channel_id=1, source_target_pairs={{0,24},{1,25},{2,26},{3,27},{4,28},{5,29},{6,30},{7,31},{8,16},{9,... | collective-permute-start | bytes 18440 | tf_op jit(solution)/shard_map/ppermute | solution.py:352
  184.6 5.6 %collective-permute-start.17 = (f32[4,384]{1,0:T(4,128)S(1)}, f32[4,384]{1,0:T(4,128)S(1)}, u32[]{:S(2)}, u32[]{:S(2)}) collective-permute-start(f32[4,384]{1,0:T(4,128)S(1)} %get-tuple-element.47), channel_id=1, source_target_pairs={{0,28},{1,29},{2,30},{3,31},{4,24},{5,25},{6,26},{7,27},{8,20},{9,... | collective-permute-start | bytes 18440 | tf_op jit(solution)/shard_map/ppermute | solution.py:352

commit v3 on v2

--- a/solution.py
+++ b/solution.py
@@ -156,89 +156,92 @@
     i = pl.program_id(0)
     n = SLOTS
 
-    owner = jnp.broadcast_to(own_ref[pl.ds(z_ref[0] * OWN + i, 1), :], (PEERS, LANES))
-    dest = msg_ref[pl.ds(0, PEERS, stride=8), :].astype(jnp.int32)
-    match = jnp.where((dest >> 8).astype(F32) == owner, 1.0, 0.0)
-    sel = bucket_select(match)
-    valid = jnp.sum(sel, axis=1, keepdims=True)
-    slot = jnp.sum(sel * spread8((dest & (SLOTS - 1)).astype(F32)), axis=1, keepdims=True)
-    slot = jnp.where(valid > 0.5, slot, -1.0)
-    align = jnp.sum(sel * spread8(msg_ref[pl.ds(1, PEERS, stride=8), :]), axis=1, keepdims=True)
-    align = jnp.where(valid > 0.5, align, -1.0)
-
-    mine = iota((PEERS, LANES), 0).astype(F32) == owner
-    seg_lo = jnp.sum(jnp.where(mine, msg_ref[pl.ds(2, PEERS, stride=8), :], 0.0), axis=0, keepdims=True)
-    seg_hi = jnp.sum(jnp.where(mine, msg_ref[pl.ds(3, PEERS, stride=8), :], 0.0), axis=0, keepdims=True)
-    seg = jnp.concatenate([seg_lo, seg_hi], axis=1)
-    lane = iota((n, n), 1)
-    lanef = lane.astype(F32)
-    diag = iota((n, n), 0) == lane
-    label = jnp.sum(jnp.where(lanef == slot, jnp.broadcast_to(seg, (n, n)), 0.0), axis=1, keepdims=True)
-    label = jnp.where(valid > 0.5, label, -1.0)
-    label_b = jnp.broadcast_to(label, (n, n))
-    label_row = jnp.sum(jnp.where(diag, label_b, 0.0), axis=0, keepdims=True)
-    allowed = ((label_b == jnp.broadcast_to(label_row, (n, n))) & (label_b >= 0.0)) | diag
-    bias = jnp.where(allowed, 0.0, -1e30)
-
-    @pl.when(i == 0)
+    @pl.when(i < OWN)
     def _():
-        for c in range(2):
-            tiles = tail_ref[:, c * 2 * BUCKET : (c + 1) * 2 * BUCKET, :].astype(F32)
-            tiles = tiles.reshape(PEERS, 2, BUCKET, LANES)
-            for half in range(2):
-                span = slice((2 * c + half) * LANES, (2 * c + half + 1) * LANES)
-                text_ref[:, span] = tiles[:, half].reshape(GTEXT, LANES).astype(BF16)
-
-    pick = jnp.where(lanef == align, 1.0, 0.0).astype(BF16)
-    cond = dot(pick, text_ref[...]).astype(BF16)
-    extra = dot(cond, w_ref[...])
-
-    scale = LANES ** (-0.5)
-
-    def pair_of(pair, h):
-        off = (pair * HPD + h) * 2 * BUCKET
-        both = in_ref[:, off : off + 2 * BUCKET, :].astype(F32).reshape(PEERS, 2, BUCKET, LANES)
-        return both[:, 0].reshape(n, LANES), both[:, 1].reshape(n, LANES)
-
-    def put(pair, h, a, b):
-        off = (pair * HPD + h) * 2 * BUCKET
-        both = jnp.concatenate(
-            [a.reshape(PEERS, BUCKET, LANES), b.reshape(PEERS, BUCKET, LANES)], axis=1
-        ).astype(BF16)
-        out_ref[:, pl.ds(pl.multiple_of(i * BLOCK + off, 16), 2 * BUCKET), :] = both
-
-    value_grads = []
-    for h in range(HPD):
-        q, k = pair_of(0, h)
-        v, g = pair_of(1, h)
-        q, k, g = q.astype(BF16), k.astype(BF16), g.astype(BF16)
-        v = (v + extra[:, h * LANES : (h + 1) * LANES]).astype(BF16)
-        s = dot_nt(q, k) * scale + bias
-        e = jnp.exp(s - jnp.max(s, axis=1, keepdims=True))
-        p = e * (1.0 / jnp.sum(e, axis=1, keepdims=True))
-        w = p.astype(BF16)
-        out = dot(w, v)
-        value_grad = dot_tn(w, g)
-        pg = dot_nt(g, v)
-        centre = jnp.sum(p * pg, axis=1, keepdims=True)
-        sg = (p * (pg - centre)).astype(BF16)
-        query_grad = dot(sg, k) * scale
-        key_grad = dot_tn(sg, q) * scale
-        put(0, h, out, query_grad)
-        put(1, h, key_grad, value_grad)
-        value_grads.append(value_grad.astype(BF16))
-
-    part = dot_tn(pick, jnp.concatenate(value_grads, axis=1))
-
-    @pl.when(i == 0)
-    def _():
-        acc_ref[...] = part
-
-    @pl.when(i > 0)
-    def _():
-        acc_ref[...] += part
-
-    @pl.when(i == OWN - 1)
+
+        owner = jnp.broadcast_to(own_ref[pl.ds(z_ref[0] * OWN + i, 1), :], (PEERS, LANES))
+        dest = msg_ref[pl.ds(0, PEERS, stride=8), :].astype(jnp.int32)
+        match = jnp.where((dest >> 8).astype(F32) == owner, 1.0, 0.0)
+        sel = bucket_select(match)
+        valid = jnp.sum(sel, axis=1, keepdims=True)
+        slot = jnp.sum(sel * spread8((dest & (SLOTS - 1)).astype(F32)), axis=1, keepdims=True)
+        slot = jnp.where(valid > 0.5, slot, -1.0)
+        align = jnp.sum(sel * spread8(msg_ref[pl.ds(1, PEERS, stride=8), :]), axis=1, keepdims=True)
+        align = jnp.where(valid > 0.5, align, -1.0)
+
+        mine = iota((PEERS, LANES), 0).astype(F32) == owner
+        seg_lo = jnp.sum(jnp.where(mine, msg_ref[pl.ds(2, PEERS, stride=8), :], 0.0), axis=0, keepdims=True)
+        seg_hi = jnp.sum(jnp.where(mine, msg_ref[pl.ds(3, PEERS, stride=8), :], 0.0), axis=0, keepdims=True)
+        seg = jnp.concatenate([seg_lo, seg_hi], axis=1)
+        lane = iota((n, n), 1)
+        lanef = lane.astype(F32)
+        diag = iota((n, n), 0) == lane
+        label = jnp.sum(jnp.where(lanef == slot, jnp.broadcast_to(seg, (n, n)), 0.0), axis=1, keepdims=True)
+        label = jnp.where(valid > 0.5, label, -1.0)
+        label_b = jnp.broadcast_to(label, (n, n))
+        label_row = jnp.sum(jnp.where(diag, label_b, 0.0), axis=0, keepdims=True)
+        allowed = ((label_b == jnp.broadcast_to(label_row, (n, n))) & (label_b >= 0.0)) | diag
+        bias = jnp.where(allowed, 0.0, -1e30)
+
+        @pl.when(i == 0)
+        def _():
+            for c in range(2):
+                tiles = tail_ref[:, c * 2 * BUCKET : (c + 1) * 2 * BUCKET, :].astype(F32)
+                tiles = tiles.reshape(PEERS, 2, BUCKET, LANES)
+                for half in range(2):
+                    span = slice((2 * c + half) * LANES, (2 * c + half + 1) * LANES)
+                    text_ref[:, span] = tiles[:, half].reshape(GTEXT, LANES).astype(BF16)
+
+        pick = jnp.where(lanef == align, 1.0, 0.0).astype(BF16)
+        cond = dot(pick, text_ref[...]).astype(BF16)
+        extra = dot(cond, w_ref[...])
+
+        scale = LANES ** (-0.5)
+
+        def pair_of(pair, h):
+            off = (pair * HPD + h) * 2 * BUCKET
+            both = in_ref[:, off : off + 2 * BUCKET, :].astype(F32).reshape(PEERS, 2, BUCKET, LANES)
+            return both[:, 0].reshape(n, LANES), both[:, 1].reshape(n, LANES)
+
+        def put(pair, h, a, b):
+            off = (pair * HPD + h) * 2 * BUCKET
+            both = jnp.concatenate(
+                [a.reshape(PEERS, BUCKET, LANES), b.reshape(PEERS, BUCKET, LANES)], axis=1
+            ).astype(BF16)
+            out_ref[:, off : off + 2 * BUCKET, :] = both
+
+        value_grads = []
+        for h in range(HPD):
+            q, k = pair_of(0, h)
+            v, g = pair_of(1, h)
+            q, k, g = q.astype(BF16), k.astype(BF16), g.astype(BF16)
+            v = (v + extra[:, h * LANES : (h + 1) * LANES]).astype(BF16)
+            s = dot_nt(q, k) * scale + bias
+            e = jnp.exp(s - jnp.max(s, axis=1, keepdims=True))
+            p = e * (1.0 / jnp.sum(e, axis=1, keepdims=True))
+            w = p.astype(BF16)
+            out = dot(w, v)
+            value_grad = dot_tn(w, g)
+            pg = dot_nt(g, v)
+            centre = jnp.sum(p * pg, axis=1, keepdims=True)
+            sg = (p * (pg - centre)).astype(BF16)
+            query_grad = dot(sg, k) * scale
+            key_grad = dot_tn(sg, q) * scale
+            put(0, h, out, query_grad)
+            put(1, h, key_grad, value_grad)
+            value_grads.append(value_grad.astype(BF16))
+
+        part = dot_tn(pick, jnp.concatenate(value_grads, axis=1))
+
+        @pl.when(i == 0)
+        def _():
+            acc_ref[...] = part
+
+        @pl.when(i > 0)
+        def _():
+            acc_ref[...] += part
+
+    @pl.when(i == OWN)
     def _():
         acc = acc_ref[...]
         high = acc.astype(BF16)
@@ -251,7 +254,7 @@
                 [tg[:, :, 2 * c * LANES : (2 * c + 1) * LANES], tg[:, :, (2 * c + 1) * LANES : (2 * c + 2) * LANES]],
                 axis=1,
             ).astype(BF16)
-            off = OWN * BLOCK + c * 2 * BUCKET
+            off = c * 2 * BUCKET
             out_ref[:, off : off + 2 * BUCKET, :] = both
         text = text_ref[...]
         wg_ref[...] = dot_tn(text, high) + dot_tn(text, low)
@@ -263,19 +266,19 @@
         attend_kernel,
         grid_spec=pltpu.PrefetchScalarGridSpec(
             num_scalar_prefetch=1,
-            grid=(OWN,),
+            grid=(OWN + 1,),
             in_specs=[
                 full((PEERS * 8, LANES)),
                 full((COMPACT, LANES)),
-                pl.BlockSpec((PEERS, BLOCK, LANES), lambda i, z: (0, i, 0)),
+                pl.BlockSpec((PEERS, BLOCK, LANES), lambda i, z: (0, jnp.minimum(i, OWN - 1), 0)),
                 pl.BlockSpec((PEERS, TEXT_ROWS, LANES), lambda i, z: (0, OWN * BLOCK // TEXT_ROWS, 0)),
                 full((TEXT, COLS)),
             ],
-            out_specs=[full((PEERS, MSG_ROWS, LANES)), full((TEXT, COLS))],
+            out_specs=[pl.BlockSpec((PEERS, BLOCK, LANES), lambda i, z: (0, i, 0)), full((TEXT, COLS))],
             scratch_shapes=[pltpu.VMEM((GTEXT, COLS), F32), pltpu.VMEM((GTEXT, TEXT), BF16)],
         ),
         out_shape=[
-            jax.ShapeDtypeStruct((PEERS, MSG_ROWS, LANES), BF16),
+            pltpu.HBM((PEERS, MSG_ROWS, LANES), BF16),
             jax.ShapeDtypeStruct((TEXT, COLS), F32),
         ],
         compiler_params=pltpu.CompilerParams(vmem_limit_bytes=24 << 20),
@@ -363,30 +366,37 @@
     return x
 
 
-def halve(x, axis, bit, dim):
+def halve(x, axis, bit, dim, kind):
     up = (lax.axis_index(axis) & bit) != 0
     zero, one = lax.index_in_dim(x, 0, dim, False), lax.index_in_dim(x, 1, dim, False)
-    return jnp.where(up, one, zero) + swap(jnp.where(up, zero, one), axis, bit)
-
-
-def x_split_kernel(x_ref, in_ref, *out_refs):
-    for f, out_ref in enumerate(out_refs):
+    return jnp.where(up, one, zero), swap(jnp.where(up, zero, one).astype(kind), axis, bit)
+
+
+def y_split_kernel(y_ref, keep_ref, got_ref, own_ref, *send_refs):
+    for h in range(2):
+        for f, out_ref in enumerate((own_ref,) + send_refs):
+            j = h * 4 + (y_ref[0] ^ f)
+            out_ref[h] = (keep_ref[j] + got_ref[j].astype(F32)).astype(out_ref.dtype)
+
+
+def x_split_kernel(x_ref, keep_ref, got_ref, *refs):
+    total_ref = refs[NX]
+    total_ref[...] = keep_ref[...] + got_ref[...].astype(F32)
+    for f, out_ref in enumerate(refs[:NX]):
         for j in range(NZ):
-            out_ref[pl.ds(j, 1), :] = in_ref[pl.ds(j * NX + (x_ref[0] ^ f), 1), :]
+            out_ref[pl.ds(j, 1), :] = total_ref[pl.ds(j * NX + (x_ref[0] ^ f), 1), :]
 
 
 def z_split_kernel(z_ref, *refs):
+    low = z_ref[0] & 3
     for f, out_ref in enumerate(refs[NX:]):
-        for j in range(NX):
-            out_ref[pl.ds(j, 1), :] = refs[j][pl.ds(z_ref[0] ^ f, 1), :]
-
-
-def row_sum_kernel(x_ref, *refs):
-    out_ref, total_ref = refs[NZ:]
-    total = refs[0][...]
-    for f in range(1, NZ):
-        total = total + refs[f][...]
-    total_ref[...] = total
+        for h in range(2):
+            for j in range(NX):
+                out_ref[pl.ds(h * NX + j, 1), :] = refs[j][pl.ds(h * 4 + (low ^ f), 1), :]
+
+
+def row_sum_kernel(x_ref, keep_ref, got_ref, out_ref, total_ref):
+    total_ref[...] = keep_ref[...] + got_ref[...]
     for c in range(NX):
         out_ref[:, c * COLS : (c + 1) * COLS] = total_ref[pl.ds(x_ref[0] ^ c, 1), :]
 
@@ -394,24 +404,34 @@
 def small_call(kernel, outs, scratch, index, *args):
     return pl.pallas_call(
         kernel,
-        out_shape=[jax.ShapeDtypeStruct(shape, F32) for shape in outs],
+        out_shape=[jax.ShapeDtypeStruct(shape, kind) for shape, kind in outs],
         in_specs=[pl.BlockSpec(memory_space=pltpu.SMEM)]
         + [pl.BlockSpec(memory_space=pltpu.VMEM)] * len(args),
         scratch_shapes=scratch,
-        compiler_params=pltpu.CompilerParams(vmem_limit_bytes=4 << 20),
+        compiler_params=pltpu.CompilerParams(vmem_limit_bytes=8 << 20),
     )(index, *args)
 
 
 def reduce_weight(wg, zi, xi):
-    wg = wg.reshape(2, 2, 2, 2, PEERS, COLS)
-    wg = halve(wg, "dp", 1, 3)
-    for bit, dim in ((2, 2), (4, 1), (8, 0)):
-        wg = halve(wg, "dp", bit, dim)
-    parts = small_call(x_split_kernel, [(NZ, COLS)] * NX, [], xi, wg)
+    wg = wg.reshape(8, 2, PEERS, COLS)
+    keep, got = halve(wg, "dp", 1, 1, BF16)
+    yi = ((lax.axis_index("dp").astype(jnp.int32) >> 1) & 3).reshape(1)
+    half = (2, PEERS, COLS)
+    parts = small_call(y_split_kernel, [(half, F32)] + [(half, BF16)] * 3, [], yi, keep, got)
+    total = parts[0]
+    for f in range(1, 4):
+        total = total + swap(parts[f], "dp", 2 * f).astype(F32)
+    keep, got = halve(total, "dp", 8, 0, BF16)
+    piece = ((NZ, COLS), F32)
+    parts = small_call(x_split_kernel, [piece] * NX, [pltpu.VMEM((PEERS, COLS), F32)], xi, keep, got)
     parts = [parts[0]] + [swap(parts[f], "seq", f) for f in range(1, NX)]
-    parts = small_call(z_split_kernel, [(NX, COLS)] * NZ, [], zi, *parts)
-    parts = [parts[0]] + [swap(parts[f], "seq", f * NX) for f in range(1, NZ)]
-    return small_call(row_sum_kernel, [(1, NX * COLS)], [pltpu.VMEM((NX, COLS), F32)], xi, *parts)[0]
+    parts = small_call(z_split_kernel, [piece] * 4, [], zi, *parts)
+    total = parts[0]
+    for f in range(1, 4):
+        total = total + swap(parts[f], "seq", f * NX)
+    keep, got = halve(total.reshape(2, NX, COLS), "seq", 16, 0, F32)
+    row = [((1, NX * COLS), F32)]
+    return small_call(row_sum_kernel, row, [pltpu.VMEM((NX, COLS), F32)], xi, keep, got)[0]
 
 
 def local(query, key, value, text, cond_weight, cotangent, dest, segment, align):

time: 198 us -> 187 us (0.944)
  the two profiles are of different devices: /device:TPU:1 before, /device:TPU:4 now
where the time goes in v3:
time: 187 us; the launch traced here: 186 us
  starting transfers between devices  72.5 us (39%)
  waiting for transfers between devices  66.4 us (36%)
  blocking collectives  22 us (12%)
  Pallas kernels  21.9 us (12%)
    ppermute x16, starting transfers between devices, swap(): return lax.ppermute(x, axis, [(j, j ^ bit) for j in range(size)])  60.8 us
    all_to_all x2, waiting for transfers between devices, exchange(): return lax.all_to_all(x, 'seq', split_axis=0, concat_axis=0, tiled=True)  33.3 us
    ppermute x16, waiting for transfers between devices, swap(): return lax.ppermute(x, axis, [(j, j ^ bit) for j in range(size)])  33.1 us
    all_to_all x1, blocking collectives, exchange(): return lax.all_to_all(x, 'seq', split_axis=0, concat_axis=0, tiled=True)  22 us
    all_to_all x2, starting transfers between devices, exchange(): return lax.all_to_all(x, 'seq', split_axis=0, concat_axis=0, tiled=True)  11.7 us
    pallas_call x1, Pallas kernels, attend(): pl.pallas_call(attend_kernel, grid_spec=pltpu.PrefetchScalarGridSpec(num_...  11.4 us
    pallas_call x1, Pallas kernels, pack(): pl.pallas_call(pack_kernel, grid=(NX,), in_specs=[full((PEERS * 8, LANES)...  5.01 us
  transfers between devices with their start and end apart: 18, of which 13 were waited for; matrix products, arithmetic and copies ran while one was open for 1% of the time, Pallas kernels for 0%

profile of v3, /device:TPU:4, one launch (start us, length us, event | category | flops | bytes accessed | tf_op | source)
XLA Modules:
  0.0 185.8 jit_solution(1359463627700548303)
XLA Ops:
  2.0 22.0 %all_to_all.15 = f32[32,8,128]{2,1,0:T(8,128)} all-to-all(f32[32,8,128]{2,1,0:T(8,128)} %bitcast.69), channel_id=1, replica_groups=mesh['dp'=16,'seq'=32] {'seq'}, dimensions={0} | all-to-all | bytes 262144 | tf_op jit(solution)/shard_map/all_to_all | solution.py:350
  24.0 5.0 %pack.1 = (bf16[8,4,320,128]{3,2,1,0:T(8,128)(2,1)}, f32[24,128]{1,0:T(8,128)}) custom-call(f32[256,128]{1,0:T(8,128)} %bitcast.59, s32[1,128]{1,0:T(1,128)} %bitcast.66, bf16[8,512]{1,0:T(8,128)(2,1)} %text_ref.1, bf16[128,1536]{1,0:T(8,128)(2,1)} %q_ref.1, bf16[128,1536]{1,0:T(8,128)(2,1)} %k_ref.1, bf16[128,1536]{1,0:T(8,128)(2,1)} %v_ref.1, ...), custom_call_target="tpu_custom_call" | custom-call | tf_op jit(solution)/shard_map/pack/pallas_call | solution.py:138
  29.0 6.1 %all-to-all-start.1 = ((bf16[32,320,128]{2,1,0:T(8,128)(2,1)}), bf16[32,320,128]{2,1,0:T(8,128)(2,1)S(1)}, u32[]{:S(2)}, u32[]{:S(2)}) async-start(bf16[32,320,128]{2,1,0:T(8,128)(2,1)} %bitcast.68), calls=%async_computation.1 | async-start | bytes 5242880 | tf_op jit(solution)/shard_map/all_to_all | solution.py:350
  35.2 7.7 %collective-permute-start = (bf16[32,384]{1,0:T(8,128)(2,1)S(1)}, bf16[32,384]{1,0:T(8,128)(2,1)S(1)}, u32[]{:S(2)}, u32[]{:S(2)}) collective-permute-start(bf16[32,384]{1,0:T(8,128)(2,1)S(1)} %bitcast.72), channel_id=1, source_target_pairs={{0,256},{32,288},{64,320},{96,352},{128,384},{160,416},{192,448},{... | collective-permute-start | bytes 73736 | tf_op jit(solution)/shard_map/ppermute | solution.py:355
  42.9 1.9 %collective-permute-done = bf16[32,384]{1,0:T(8,128)(2,1)S(1)} collective-permute-done((bf16[32,384]{1,0:T(8,128)(2,1)S(1)}, bf16[32,384]{1,0:T(8,128)(2,1)S(1)}, u32[]{:S(2)}, u32[]{:S(2)}) %collective-permute-start) | collective-permute-done | bytes 24608 | tf_op jit(solution)/shard_map/ppermute | solution.py:355
  44.9 4.5 %collective-permute-start.1 = (bf16[2,32,384]{2,1,0:T(8,128)(2,1)S(1)}, bf16[2,32,384]{2,1,0:T(8,128)(2,1)S(1)}, u32[]{:S(2)}, u32[]{:S(2)}) collective-permute-start(bf16[2,32,384]{2,1,0:T(8,128)(2,1)S(1)} %pad_maximum_fusion.3), channel_id=1, source_target_pairs={{0,128},{32,160},{64,192},{96,224},{128,0},{160,32},{192,64},{224,... | collective-permute-start | bytes 147464 | tf_op jit(solution)/shard_map/ppermute | solution.py:355
  49.4 2.3 %collective-permute-done.1 = bf16[2,32,384]{2,1,0:T(8,128)(2,1)S(1)} collective-permute-done((bf16[2,32,384]{2,1,0:T(8,128)(2,1)S(1)}, bf16[2,32,384]{2,1,0:T(8,128)(2,1)S(1)}, u32[]{:S(2)}, u32[]{:S(2)}) %collective-permute-start.1) | collective-permute-done | bytes 49184 | tf_op jit(solution)/shard_map/ppermute | solution.py:355
  51.8 3.5 %collective-permute-start.2 = (bf16[2,2,32,384]{3,2,0,1:T(8,128)(2,1)S(1)}, bf16[2,2,32,384]{3,2,0,1:T(8,128)(2,1)S(1)}, u32[]{:S(2)}, u32[]{:S(2)}) collective-permute-start(bf16[2,2,32,384]{3,2,0,1:T(8,128)(2,1)S(1)} %pad_maximum_fusion.2), channel_id=1, source_target_pairs={{0,64},{32,96},{64,0},{96,32},{128,192},{160,224},{192,128},{224,1... | collective-permute-start | bytes 294920 | tf_op jit(solution)/shard_map/ppermute | solution.py:355
  55.3 3.0 %collective-permute-done.2 = bf16[2,2,32,384]{3,2,0,1:T(8,128)(2,1)S(1)} collective-permute-done((bf16[2,2,32,384]{3,2,0,1:T(8,128)(2,1)S(1)}, bf16[2,2,32,384]{3,2,0,1:T(8,128)(2,1)S(1)}, u32[]{:S(2)}, u32[]{:S(2)}) %collective-permute-start.2) | collective-permute-done | bytes 98336 | tf_op jit(solution)/shard_map/ppermute | solution.py:355
  58.4 1.9 %collective-permute-start.3 = (bf16[2,2,2,32,384]{4,3,0,1,2:T(8,128)(2,1)S(1)}, bf16[2,2,2,32,384]{4,3,0,1,2:T(8,128)(2,1)S(1)}, u32[]{:S(2)}, u32[]{:S(2)}) collective-permute-start(bf16[2,2,2,32,384]{4,3,0,1,2:T(8,128)(2,1)S(1)} %pad_maximum_fusion.1), channel_id=1, source_target_pairs={{0,32},{32,0},{64,96},{96,64},{128,160},{160,128},{192,224},{224,1... | collective-permute-start | bytes 589832 | tf_op jit(solution)/shard_map/ppermute | solution.py:355
  62.6 33.3 %all-to-all-done.1.in_ref.tail_ref = bf16[32,320,128]{2,1,0:T(8,128)(2,1)S(1)} async-done(((bf16[32,320,128]{2,1,0:T(8,128)(2,1)}), bf16[32,320,128]{2,1,0:T(8,128)(2,1)S(1)}, u32[]{:S(2)}, u32[]{:S(2)}) %all-to-all-start.1) | async-done | bytes 2621472 | tf_op jit(solution)/shard_map/all_to_all | solution.py:350
  96.9 11.4 %attend.1 = (bf16[32,320,128]{2,1,0:T(8,128)(2,1)}, f32[512,384]{1,0:T(8,128)S(1)}) custom-call(s32[1]{0:T(128)} %bitcast.5.z_ref, f32[256,128]{1,0:T(8,128)S(1)} %bitcast.60, f32[24,128]{1,0:T(8,128)S(1)} %copy-done.2, bf16[32,320,128]{2,1,0:T(8,128)(2,1)S(1)} %all-to-all-done.1.in_ref.tail_ref, bf16[32,320,128]{2,1,0:T(8,128)(2,1)S(1)} %all-to-all-done.1.in_ref.tail_ref, ...), custom_call_target="tpu_custom_call" | custom-call | tf_op jit(solution)/shard_map/attend/pallas_call | solution.py:265
  108.3 5.6 %all-to-all-start.2 = ((bf16[32,320,128]{2,1,0:T(8,128)(2,1)}), bf16[32,320,128]{2,1,0:T(8,128)(2,1)S(1)}, u32[]{:S(2)}, u32[]{:S(2)}) async-start(bf16[32,320,128]{2,1,0:T(8,128)(2,1)} %get-tuple-element.29), calls=%async_computation.2 | async-start | bytes 5242880 | tf_op jit(solution)/shard_map/all_to_all | solution.py:350
  113.9 1.9 %collective-permute-start.4 = (bf16[8,32,384]{2,1,0:T(8,128)(2,1)S(1)}, bf16[8,32,384]{2,1,0:T(8,128)(2,1)S(1)}, u32[]{:S(2)}, u32[]{:S(2)}) collective-permute-start(bf16[8,32,384]{2,1,0:T(8,128)(2,1)S(1)} %fusion), channel_id=1, source_target_pairs={{0,32},{32,0},{64,96},{96,64},{128,160},{160,128},{192,224},{224,1... | collective-permute-start | bytes 589832 | tf_op jit(solution)/shard_map/ppermute | solution.py:355
  117.3 3.5 %collective-permute-start.5 = (bf16[2,32,384]{2,1,0:T(8,128)(2,1)S(1)}, bf16[2,32,384]{2,1,0:T(8,128)(2,1)S(1)}, u32[]{:S(2)}, u32[]{:S(2)}) collective-permute-start(bf16[2,32,384]{2,1,0:T(8,128)(2,1)S(1)} %get-tuple-element.37), channel_id=1, source_target_pairs={{0,64},{32,96},{64,0},{96,32},{128,192},{160,224},{192,128},{224,1... | collective-permute-start | bytes 147464 | tf_op jit(solution)/shard_map/ppermute | solution.py:355
  120.8 4.5 %collective-permute-start.6 = (bf16[2,32,384]{2,1,0:T(8,128)(2,1)S(1)}, bf16[2,32,384]{2,1,0:T(8,128)(2,1)S(1)}, u32[]{:S(2)}, u32[]{:S(2)}) collective-permute-start(bf16[2,32,384]{2,1,0:T(8,128)(2,1)S(1)} %get-tuple-element.38), channel_id=1, source_target_pairs={{0,128},{32,160},{64,192},{96,224},{128,0},{160,32},{192,64},{224,... | collective-permute-start | bytes 147464 | tf_op jit(solution)/shard_map/ppermute | solution.py:355
  125.3 2.1 %collective-permute-start.7 = (bf16[2,32,384]{2,1,0:T(8,128)(2,1)S(1)}, bf16[2,32,384]{2,1,0:T(8,128)(2,1)S(1)}, u32[]{:S(2)}, u32[]{:S(2)}) collective-permute-start(bf16[2,32,384]{2,1,0:T(8,128)(2,1)S(1)} %get-tuple-element.39), channel_id=1, source_target_pairs={{0,192},{32,224},{64,128},{96,160},{128,64},{160,96},{192,0},{224,... | collective-permute-start | bytes 147464 | tf_op jit(solution)/shard_map/ppermute | solution.py:355
  128.1 5.0 %collective-permute-done.7 = bf16[2,32,384]{2,1,0:T(8,128)(2,1)S(1)} collective-permute-done((bf16[2,32,384]{2,1,0:T(8,128)(2,1)S(1)}, bf16[2,32,384]{2,1,0:T(8,128)(2,1)S(1)}, u32[]{:S(2)}, u32[]{:S(2)}) %collective-permute-start.7) | collective-permute-done | bytes 49184 | tf_op jit(solution)/shard_map/ppermute | solution.py:355
  133.1 5.0 %collective-permute-start.8 = (bf16[32,384]{1,0:T(8,128)(2,1)S(1)}, bf16[32,384]{1,0:T(8,128)(2,1)S(1)}, u32[]{:S(2)}, u32[]{:S(2)}) collective-permute-start(bf16[32,384]{1,0:T(8,128)(2,1)S(1)} %fusion.1), channel_id=1, source_target_pairs={{0,256},{32,288},{64,320},{96,352},{128,384},{160,416},{192,448},{... | collective-permute-start | bytes 73736 | tf_op jit(solution)/shard_map/ppermute | solution.py:355
  138.2 4.6 %collective-permute-done.8.got_ref = bf16[32,384]{1,0:T(8,128)(2,1)S(1)} collective-permute-done((bf16[32,384]{1,0:T(8,128)(2,1)S(1)}, bf16[32,384]{1,0:T(8,128)(2,1)S(1)}, u32[]{:S(2)}, u32[]{:S(2)}) %collective-permute-start.8) | collective-permute-done | bytes 24608 | tf_op jit(solution)/shard_map/ppermute | solution.py:355
  142.8 2.1 %collective-permute-start.10 = (f32[8,384]{1,0:T(8,128)S(1)}, f32[8,384]{1,0:T(8,128)S(1)}, u32[]{:S(2)}, u32[]{:S(2)}) collective-permute-start(f32[8,384]{1,0:T(8,128)S(1)} %get-tuple-element.42), channel_id=1, source_target_pairs={{0,2},{1,3},{2,0},{3,1},{4,6},{5,7},{6,4},{7,5},{8,10},{9,11},{10,... | collective-permute-start | bytes 36872 | tf_op jit(solution)/shard_map/ppermute | solution.py:355
  145.0 4.3 %collective-permute-start.11 = (f32[8,384]{1,0:T(8,128)S(1)}, f32[8,384]{1,0:T(8,128)S(1)}, u32[]{:S(2)}, u32[]{:S(2)}) collective-permute-start(f32[8,384]{1,0:T(8,128)S(1)} %get-tuple-element.43), channel_id=1, source_target_pairs={{0,3},{1,2},{2,1},{3,0},{4,7},{5,6},{6,5},{7,4},{8,11},{9,10},{10,... | collective-permute-start | bytes 36872 | tf_op jit(solution)/shard_map/ppermute | solution.py:355
  149.3 4.0 %collective-permute-start.9 = (f32[8,384]{1,0:T(8,128)S(1)}, f32[8,384]{1,0:T(8,128)S(1)}, u32[]{:S(2)}, u32[]{:S(2)}) collective-permute-start(f32[8,384]{1,0:T(8,128)S(1)} %get-tuple-element.41), channel_id=1, source_target_pairs={{0,1},{1,0},{2,3},{3,2},{4,5},{5,4},{6,7},{7,6},{8,9},{9,8},{10,11... | collective-permute-start | bytes 36872 | tf_op jit(solution)/shard_map/ppermute | solution.py:355
  153.3 2.0 %collective-permute-done.9.refs_1_ = f32[8,384]{1,0:T(8,128)S(1)} collective-permute-done((f32[8,384]{1,0:T(8,128)S(1)}, f32[8,384]{1,0:T(8,128)S(1)}, u32[]{:S(2)}, u32[]{:S(2)}) %collective-permute-start.9) | collective-permute-done | bytes 12320 | tf_op jit(solution)/shard_map/ppermute | solution.py:355
  155.3 3.1 %collective-permute-start.12 = (f32[8,384]{1,0:T(8,128)S(1)}, f32[8,384]{1,0:T(8,128)S(1)}, u32[]{:S(2)}, u32[]{:S(2)}) collective-permute-start(f32[8,384]{1,0:T(8,128)S(1)} %get-tuple-element.45), channel_id=1, source_target_pairs={{0,4},{1,5},{2,6},{3,7},{4,0},{5,1},{6,2},{7,3},{8,12},{9,13},{10,... | collective-permute-start | bytes 36872 | tf_op jit(solution)/shard_map/ppermute | solution.py:355
  158.4 4.4 %collective-permute-start.13 = (f32[8,384]{1,0:T(8,128)S(1)}, f32[8,384]{1,0:T(8,128)S(1)}, u32[]{:S(2)}, u32[]{:S(2)}) collective-permute-start(f32[8,384]{1,0:T(8,128)S(1)} %get-tuple-element.46), channel_id=1, source_target_pairs={{0,8},{1,9},{2,10},{3,11},{4,12},{5,13},{6,14},{7,15},{8,0},{9,1},... | collective-permute-start | bytes 36872 | tf_op jit(solution)/shard_map/ppermute | solution.py:355
  162.8 2.6 %collective-permute-start.14 = (f32[8,384]{1,0:T(8,128)S(1)}, f32[8,384]{1,0:T(8,128)S(1)}, u32[]{:S(2)}, u32[]{:S(2)}) collective-permute-start(f32[8,384]{1,0:T(8,128)S(1)} %get-tuple-element.47), channel_id=1, source_target_pairs={{0,12},{1,13},{2,14},{3,15},{4,8},{5,9},{6,10},{7,11},{8,4},{9,5},... | collective-permute-start | bytes 36872 | tf_op jit(solution)/shard_map/ppermute | solution.py:355
  165.5 5.2 %collective-permute-done.12 = f32[8,384]{1,0:T(8,128)S(1)} collective-permute-done((f32[8,384]{1,0:T(8,128)S(1)}, f32[8,384]{1,0:T(8,128)S(1)}, u32[]{:S(2)}, u32[]{:S(2)}) %collective-permute-start.12) | collective-permute-done | bytes 12320 | tf_op jit(solution)/shard_map/ppermute | solution.py:355
  170.7 1.8 collective-permute-done.14
  172.4 5.5 %collective-permute-start.15 = (f32[4,384]{1,0:T(4,128)S(1)}, f32[4,384]{1,0:T(4,128)S(1)}, u32[]{:S(2)}, u32[]{:S(2)}) collective-permute-start(f32[4,384]{1,0:T(4,128)S(1)} %get-tuple-element.56), channel_id=1, source_target_pairs={{0,16},{1,17},{2,18},{3,19},{4,20},{5,21},{6,22},{7,23},{8,24},{9,... | collective-permute-start | bytes 18440 | tf_op jit(solution)/shard_map/ppermute | solution.py:355
  177.9 4.0 %collective-permute-done.15.got_ref = f32[4,384]{1,0:T(4,128)S(1)} collective-permute-done((f32[4,384]{1,0:T(4,128)S(1)}, f32[4,384]{1,0:T(4,128)S(1)}, u32[]{:S(2)}, u32[]{:S(2)}) %collective-permute-start.15) | collective-permute-done | bytes 6176 | tf_op jit(solution)/shard_map/ppermute | solution.py:355
  182.5 3.4 %unpack.1 = (bf16[128,1536]{1,0:T(8,128)(2,1)}, bf16[128,1536]{1,0:T(8,128)(2,1)}, bf16[128,1536]{1,0:T(8,128)(2,1)}, bf16[128,1536]{1,0:T(8,128)(2,1)}, f32[8,512]{1,0:T(8,128)}) custom-call(f32[256,128]{1,0:T(8,128)S(1)} %bitcast.61, s32[1,128]{1,0:T(1,128)S(1)} %bitcast.67, bf16[8,4,320,128]{3,2,1,0:T(8,128)(2,1)S(1)} %bitcast.58), custom_call_target="tpu_custom_call" | custom-call | tf_op jit(solution)/shard_map/unpack/pallas_call | solution.py:333
  (39 shorter events, 7.7 us)
Async XLA Ops:
  29.0 6.1 %copy-start = (f32[32,8,128]{2,1,0:T(8,128)S(1)}, f32[32,8,128]{2,1,0:T(8,128)}, u32[]{:S(2)}) copy-start(f32[32,8,128]{2,1,0:T(8,128)} %all_to_all.15) | copy-start | bytes 393220
  29.0 66.9 %all-to-all-start.1 = ((bf16[32,320,128]{2,1,0:T(8,128)(2,1)}), bf16[32,320,128]{2,1,0:T(8,128)(2,1)S(1)}, u32[]{:S(2)}, u32[]{:S(2)}) async-start(bf16[32,320,128]{2,1,0:T(8,128)(2,1)} %bitcast.68), calls=%async_computation.1 | async-start | bytes 5242880 | tf_op jit(solution)/shard_map/all_to_all | solution.py:350
  35.1 60.7 %copy-start.2 = (f32[24,128]{1,0:T(8,128)S(1)}, f32[24,128]{1,0:T(8,128)}, u32[]{:S(2)}) copy-start(f32[24,128]{1,0:T(8,128)} %get-tuple-element.27.own_ref) | copy-start | bytes 36868
  35.2 9.6 %collective-permute-start = (bf16[32,384]{1,0:T(8,128)(2,1)S(1)}, bf16[32,384]{1,0:T(8,128)(2,1)S(1)}, u32[]{:S(2)}, u32[]{:S(2)}) collective-permute-start(bf16[32,384]{1,0:T(8,128)(2,1)S(1)} %bitcast.72), channel_id=1, source_target_pairs={{0,256},{32,288},{64,320},{96,352},{128,384},{160,416},{192,448},{... | collective-permute-start | bytes 73736 | tf_op jit(solution)/shard_map/ppermute | solution.py:355
  44.9 6.9 %collective-permute-start.1 = (bf16[2,32,384]{2,1,0:T(8,128)(2,1)S(1)}, bf16[2,32,384]{2,1,0:T(8,128)(2,1)S(1)}, u32[]{:S(2)}, u32[]{:S(2)}) collective-permute-start(bf16[2,32,384]{2,1,0:T(8,128)(2,1)S(1)} %pad_maximum_fusion.3), channel_id=1, source_target_pairs={{0,128},{32,160},{64,192},{96,224},{128,0},{160,32},{192,64},{224,... | collective-permute-start | bytes 147464 | tf_op jit(solution)/shard_map/ppermute | solution.py:355
  51.8 6.5 %collective-permute-start.2 = (bf16[2,2,32,384]{3,2,0,1:T(8,128)(2,1)S(1)}, bf16[2,2,32,384]{3,2,0,1:T(8,128)(2,1)S(1)}, u32[]{:S(2)}, u32[]{:S(2)}) collective-permute-start(bf16[2,2,32,384]{3,2,0,1:T(8,128)(2,1)S(1)} %pad_maximum_fusion.2), channel_id=1, source_target_pairs={{0,64},{32,96},{64,0},{96,32},{128,192},{160,224},{192,128},{224,1... | collective-permute-start | bytes 294920 | tf_op jit(solution)/shard_map/ppermute | solution.py:355
  58.4 3.3 %collective-permute-start.3 = (bf16[2,2,2,32,384]{4,3,0,1,2:T(8,128)(2,1)S(1)}, bf16[2,2,2,32,384]{4,3,0,1,2:T(8,128)(2,1)S(1)}, u32[]{:S(2)}, u32[]{:S(2)}) collective-permute-start(bf16[2,2,2,32,384]{4,3,0,1,2:T(8,128)(2,1)S(1)} %pad_maximum_fusion.1), channel_id=1, source_target_pairs={{0,32},{32,0},{64,96},{96,64},{128,160},{160,128},{192,224},{224,1... | collective-permute-start | bytes 589832 | tf_op jit(solution)/shard_map/ppermute | solution.py:355
  95.9 1.0 copy-start.1
  108.3 74.2 %all-to-all-start.2 = ((bf16[32,320,128]{2,1,0:T(8,128)(2,1)}), bf16[32,320,128]{2,1,0:T(8,128)(2,1)S(1)}, u32[]{:S(2)}, u32[]{:S(2)}) async-start(bf16[32,320,128]{2,1,0:T(8,128)(2,1)} %get-tuple-element.29), calls=%async_computation.2 | async-start | bytes 5242880 | tf_op jit(solution)/shard_map/all_to_all | solution.py:350
  113.9 68.6 %copy-start.3 = (s32[128]{0:T(128)S(1)}, s32[128]{0:T(128)}, u32[]{:S(2)}) copy-start(s32[128]{0:T(128)} %param.15) | copy-start | bytes 1540
  113.9 3.3 %collective-permute-start.4 = (bf16[8,32,384]{2,1,0:T(8,128)(2,1)S(1)}, bf16[8,32,384]{2,1,0:T(8,128)(2,1)S(1)}, u32[]{:S(2)}, u32[]{:S(2)}) collective-permute-start(bf16[8,32,384]{2,1,0:T(8,128)(2,1)S(1)} %fusion), channel_id=1, source_target_pairs={{0,32},{32,0},{64,96},{96,64},{128,160},{160,128},{192,224},{224,1... | collective-permute-start | bytes 589832 | tf_op jit(solution)/shard_map/ppermute | solution.py:355
  117.3 10.1 %collective-permute-start.5 = (bf16[2,32,384]{2,1,0:T(8,128)(2,1)S(1)}, bf16[2,32,384]{2,1,0:T(8,128)(2,1)S(1)}, u32[]{:S(2)}, u32[]{:S(2)}) collective-permute-start(bf16[2,32,384]{2,1,0:T(8,128)(2,1)S(1)} %get-tuple-element.37), channel_id=1, source_target_pairs={{0,64},{32,96},{64,0},{96,32},{128,192},{160,224},{192,128},{224,1... | collective-permute-start | bytes 147464 | tf_op jit(solution)/shard_map/ppermute | solution.py:355
  120.8 7.3 %collective-permute-start.6 = (bf16[2,32,384]{2,1,0:T(8,128)(2,1)S(1)}, bf16[2,32,384]{2,1,0:T(8,128)(2,1)S(1)}, u32[]{:S(2)}, u32[]{:S(2)}) collective-permute-start(bf16[2,32,384]{2,1,0:T(8,128)(2,1)S(1)} %get-tuple-element.38), channel_id=1, source_target_pairs={{0,128},{32,160},{64,192},{96,224},{128,0},{160,32},{192,64},{224,... | collective-permute-start | bytes 147464 | tf_op jit(solution)/shard_map/ppermute | solution.py:355
  125.3 7.8 %collective-permute-start.7 = (bf16[2,32,384]{2,1,0:T(8,128)(2,1)S(1)}, bf16[2,32,384]{2,1,0:T(8,128)(2,1)S(1)}, u32[]{:S(2)}, u32[]{:S(2)}) collective-permute-start(bf16[2,32,384]{2,1,0:T(8,128)(2,1)S(1)} %get-tuple-element.39), channel_id=1, source_target_pairs={{0,192},{32,224},{64,128},{96,160},{128,64},{160,96},{192,0},{224,... | collective-permute-start | bytes 147464 | tf_op jit(solution)/shard_map/ppermute | solution.py:355
  133.1 9.6 %collective-permute-start.8 = (bf16[32,384]{1,0:T(8,128)(2,1)S(1)}, bf16[32,384]{1,0:T(8,128)(2,1)S(1)}, u32[]{:S(2)}, u32[]{:S(2)}) collective-permute-start(bf16[32,384]{1,0:T(8,128)(2,1)S(1)} %fusion.1), channel_id=1, source_target_pairs={{0,256},{32,288},{64,320},{96,352},{128,384},{160,416},{192,448},{... | collective-permute-start | bytes 73736 | tf_op jit(solution)/shard_map/ppermute | solution.py:355
  142.8 10.5 %collective-permute-start.10 = (f32[8,384]{1,0:T(8,128)S(1)}, f32[8,384]{1,0:T(8,128)S(1)}, u32[]{:S(2)}, u32[]{:S(2)}) collective-permute-start(f32[8,384]{1,0:T(8,128)S(1)} %get-tuple-element.42), channel_id=1, source_target_pairs={{0,2},{1,3},{2,0},{3,1},{4,6},{5,7},{6,4},{7,5},{8,10},{9,11},{10,... | collective-permute-start | bytes 36872 | tf_op jit(solution)/shard_map/ppermute | solution.py:355
  145.0 8.3 %collective-permute-start.11 = (f32[8,384]{1,0:T(8,128)S(1)}, f32[8,384]{1,0:T(8,128)S(1)}, u32[]{:S(2)}, u32[]{:S(2)}) collective-permute-start(f32[8,384]{1,0:T(8,128)S(1)} %get-tuple-element.43), channel_id=1, source_target_pairs={{0,3},{1,2},{2,1},{3,0},{4,7},{5,6},{6,5},{7,4},{8,11},{9,10},{10,... | collective-permute-start | bytes 36872 | tf_op jit(solution)/shard_map/ppermute | solution.py:355
  149.3 6.0 %collective-permute-start.9 = (f32[8,384]{1,0:T(8,128)S(1)}, f32[8,384]{1,0:T(8,128)S(1)}, u32[]{:S(2)}, u32[]{:S(2)}) collective-permute-start(f32[8,384]{1,0:T(8,128)S(1)} %get-tuple-element.41), channel_id=1, source_target_pairs={{0,1},{1,0},{2,3},{3,2},{4,5},{5,4},{6,7},{7,6},{8,9},{9,8},{10,11... | collective-permute-start | bytes 36872 | tf_op jit(solution)/shard_map/ppermute | solution.py:355
  155.3 15.4 %collective-permute-start.12 = (f32[8,384]{1,0:T(8,128)S(1)}, f32[8,384]{1,0:T(8,128)S(1)}, u32[]{:S(2)}, u32[]{:S(2)}) collective-permute-start(f32[8,384]{1,0:T(8,128)S(1)} %get-tuple-element.45), channel_id=1, source_target_pairs={{0,4},{1,5},{2,6},{3,7},{4,0},{5,1},{6,2},{7,3},{8,12},{9,13},{10,... | collective-permute-start | bytes 36872 | tf_op jit(solution)/shard_map/ppermute | solution.py:355
  158.4 12.3 %collective-permute-start.13 = (f32[8,384]{1,0:T(8,128)S(1)}, f32[8,384]{1,0:T(8,128)S(1)}, u32[]{:S(2)}, u32[]{:S(2)}) collective-permute-start(f32[8,384]{1,0:T(8,128)S(1)} %get-tuple-element.46), channel_id=1, source_target_pairs={{0,8},{1,9},{2,10},{3,11},{4,12},{5,13},{6,14},{7,15},{8,0},{9,1},... | collective-permute-start | bytes 36872 | tf_op jit(solution)/shard_map/ppermute | solution.py:355
  162.8 9.6 %collective-permute-start.14 = (f32[8,384]{1,0:T(8,128)S(1)}, f32[8,384]{1,0:T(8,128)S(1)}, u32[]{:S(2)}, u32[]{:S(2)}) collective-permute-start(f32[8,384]{1,0:T(8,128)S(1)} %get-tuple-element.47), channel_id=1, source_target_pairs={{0,12},{1,13},{2,14},{3,15},{4,8},{5,9},{6,10},{7,11},{8,4},{9,5},... | collective-permute-start | bytes 36872 | tf_op jit(solution)/shard_map/ppermute | solution.py:355
  172.4 9.4 %collective-permute-start.15 = (f32[4,384]{1,0:T(4,128)S(1)}, f32[4,384]{1,0:T(4,128)S(1)}, u32[]{:S(2)}, u32[]{:S(2)}) collective-permute-start(f32[4,384]{1,0:T(4,128)S(1)} %get-tuple-element.56), channel_id=1, source_target_pairs={{0,16},{1,17},{2,18},{3,19},{4,20},{5,21},{6,22},{7,23},{8,24},{9,... | collective-permute-start | bytes 18440 | tf_op jit(solution)/shard_map/ppermute | solution.py:355

commit v4 on v2

--- a/solution.py
+++ b/solution.py
@@ -13,16 +13,20 @@
 ROWS = 128
 SLOTS = 256
 BUCKET = 8
-OWN = 3
+OWNERS = 21
 HPD = 3
-COMPACT = NZ * OWN
+UNITS = 8
+COMPACT = 24
+NEAR = 4
 LANES = 128
 COLS = HPD * LANES
 TEXT = 512
 GTEXT = 256
-BLOCK = 2 * HPD * 2 * BUCKET
+BLOCK = 2 * 2 * BUCKET
 TEXT_ROWS = 32
-MSG_ROWS = OWN * BLOCK + TEXT_ROWS
+BODY_ROWS = UNITS * BLOCK
+MSG_ROWS = BODY_ROWS + TEXT_ROWS
+STEP = 2
 
 
 def iota(shape, dim):
@@ -117,17 +121,17 @@
     for pair, (a_ref, b_ref) in enumerate(((q_ref, k_ref), (v_ref, g_ref))):
         a = dot(sel, a_ref[...]).reshape(COMPACT, BUCKET, COLS)
         b = dot(sel, b_ref[...]).reshape(COMPACT, BUCKET, COLS)
-        both = jnp.concatenate([a, b], axis=1).astype(BF16).reshape(NZ, OWN, 2 * BUCKET, COLS)
-        for i in range(OWN):
-            for h in range(HPD):
-                off = i * BLOCK + (pair * HPD + h) * 2 * BUCKET
-                out_ref[:, 0, off : off + 2 * BUCKET, :] = both[:, i, :, h * LANES : (h + 1) * LANES]
+        both = jnp.concatenate([a, b], axis=1).astype(BF16)
+        for unit in range(NZ * UNITS):
+            owner, h = divmod(unit, HPD)
+            off = unit % UNITS * BLOCK + pair * 2 * BUCKET
+            out_ref[unit // UNITS, 0, off : off + 2 * BUCKET, :] = both[owner, :, h * LANES : (h + 1) * LANES]
     text = text_ref[...].astype(F32)
     for c in range(2):
         tile = jnp.concatenate(
             [text[:, 2 * c * LANES : (2 * c + 1) * LANES], text[:, (2 * c + 1) * LANES : (2 * c + 2) * LANES]], axis=0
         ).astype(BF16)
-        off = OWN * BLOCK + c * 2 * BUCKET
+        off = BODY_ROWS + c * 2 * BUCKET
         for z in range(NZ):
             out_ref[z, 0, off : off + 2 * BUCKET, :] = tile
 
@@ -152,11 +156,8 @@
     )(msg, dest, text, q, k, v, g)
 
 
-def attend_kernel(z_ref, msg_ref, own_ref, in_ref, tail_ref, w_ref, out_ref, wg_ref, acc_ref, text_ref):
-    i = pl.program_id(0)
+def owner_setup(owner, msg_ref, text):
     n = SLOTS
-
-    owner = jnp.broadcast_to(own_ref[pl.ds(z_ref[0] * OWN + i, 1), :], (PEERS, LANES))
     dest = msg_ref[pl.ds(0, PEERS, stride=8), :].astype(jnp.int32)
     match = jnp.where((dest >> 8).astype(F32) == owner, 1.0, 0.0)
     sel = bucket_select(match)
@@ -178,7 +179,18 @@
     label_b = jnp.broadcast_to(label, (n, n))
     label_row = jnp.sum(jnp.where(diag, label_b, 0.0), axis=0, keepdims=True)
     allowed = ((label_b == jnp.broadcast_to(label_row, (n, n))) & (label_b >= 0.0)) | diag
-    bias = jnp.where(allowed, 0.0, -1e30)
+    pick = jnp.where(lanef == align, 1.0, 0.0).astype(BF16)
+    return jnp.where(allowed, 0.0, -1e30), pick, dot(pick, text).astype(BF16)
+
+
+def attend_kernel(
+    z_ref, msg_ref, own_ref, in_ref, tail_ref, w_ref, out_ref, wg_ref,
+    acc_ref, text_ref, w3_ref, bias_ref, pick_ref, cond_ref,
+):
+    i = pl.program_id(0)
+    n = SLOTS
+    unit0 = z_ref[0] * UNITS
+    owner0 = unit0 // HPD
 
     @pl.when(i == 0)
     def _():
@@ -188,97 +200,107 @@
             for half in range(2):
                 span = slice((2 * c + half) * LANES, (2 * c + half + 1) * LANES)
                 text_ref[:, span] = tiles[:, half].reshape(GTEXT, LANES).astype(BF16)
-
-    pick = jnp.where(lanef == align, 1.0, 0.0).astype(BF16)
-    cond = dot(pick, text_ref[...]).astype(BF16)
-    extra = dot(cond, w_ref[...])
+        text = text_ref[...]
+        for t in range(NEAR):
+            owner = jnp.broadcast_to(own_ref[pl.ds(owner0 + t, 1), :], (PEERS, LANES))
+            bias, pick, cond = owner_setup(owner, msg_ref, text)
+            bias_ref[t] = bias
+            pick_ref[t] = pick
+            cond_ref[t] = cond
+        for h in range(HPD):
+            w3_ref[h] = w_ref[:, h * LANES : (h + 1) * LANES]
+        acc_ref[...] = jnp.zeros_like(acc_ref)
 
     scale = LANES ** (-0.5)
 
-    def pair_of(pair, h):
-        off = (pair * HPD + h) * 2 * BUCKET
-        both = in_ref[:, off : off + 2 * BUCKET, :].astype(F32).reshape(PEERS, 2, BUCKET, LANES)
-        return both[:, 0].reshape(n, LANES), both[:, 1].reshape(n, LANES)
-
-    def put(pair, h, a, b):
-        off = (pair * HPD + h) * 2 * BUCKET
-        both = jnp.concatenate(
-            [a.reshape(PEERS, BUCKET, LANES), b.reshape(PEERS, BUCKET, LANES)], axis=1
-        ).astype(BF16)
-        out_ref[:, pl.ds(pl.multiple_of(i * BLOCK + off, 16), 2 * BUCKET), :] = both
-
-    value_grads = []
-    for h in range(HPD):
-        q, k = pair_of(0, h)
-        v, g = pair_of(1, h)
-        q, k, g = q.astype(BF16), k.astype(BF16), g.astype(BF16)
-        v = (v + extra[:, h * LANES : (h + 1) * LANES]).astype(BF16)
-        s = dot_nt(q, k) * scale + bias
-        e = jnp.exp(s - jnp.max(s, axis=1, keepdims=True))
-        p = e * (1.0 / jnp.sum(e, axis=1, keepdims=True))
-        w = p.astype(BF16)
-        out = dot(w, v)
-        value_grad = dot_tn(w, g)
-        pg = dot_nt(g, v)
-        centre = jnp.sum(p * pg, axis=1, keepdims=True)
-        sg = (p * (pg - centre)).astype(BF16)
-        query_grad = dot(sg, k) * scale
-        key_grad = dot_tn(sg, q) * scale
-        put(0, h, out, query_grad)
-        put(1, h, key_grad, value_grad)
-        value_grads.append(value_grad.astype(BF16))
-
-    part = dot_tn(pick, jnp.concatenate(value_grads, axis=1))
-
-    @pl.when(i == 0)
+    @pl.when(i < UNITS // STEP)
     def _():
-        acc_ref[...] = part
-
-    @pl.when(i > 0)
+        for u in range(STEP):
+            unit = unit0 + i * STEP + u
+            owner = unit // HPD
+            h = unit - owner * HPD
+            t = owner - owner0
+
+            def pair_of(pair):
+                off = u * BLOCK + pair * 2 * BUCKET
+                both = in_ref[:, off : off + 2 * BUCKET, :].astype(F32).reshape(PEERS, 2, BUCKET, LANES)
+                return both[:, 0].reshape(n, LANES), both[:, 1].reshape(n, LANES)
+
+            def put(pair, a, b):
+                off = u * BLOCK + pair * 2 * BUCKET
+                out_ref[:, off : off + 2 * BUCKET, :] = jnp.concatenate(
+                    [a.reshape(PEERS, BUCKET, LANES), b.reshape(PEERS, BUCKET, LANES)], axis=1
+                ).astype(BF16)
+
+            q, k = pair_of(0)
+            v, g = pair_of(1)
+            q, k, g = q.astype(BF16), k.astype(BF16), g.astype(BF16)
+            v = (v + dot(cond_ref[t], w3_ref[h])).astype(BF16)
+            s = dot_nt(q, k) * scale + bias_ref[t]
+            e = jnp.exp(s - jnp.max(s, axis=1, keepdims=True))
+            p = e * (1.0 / jnp.sum(e, axis=1, keepdims=True))
+            w = p.astype(BF16)
+            out = dot(w, v)
+            value_grad = dot_tn(w, g)
+            pg = dot_nt(g, v)
+            centre = jnp.sum(p * pg, axis=1, keepdims=True)
+            sg = (p * (pg - centre)).astype(BF16)
+            query_grad = dot(sg, k) * scale
+            key_grad = dot_tn(sg, q) * scale
+            put(0, out, query_grad)
+            put(1, key_grad, value_grad)
+            acc_ref[h] += dot_tn(pick_ref[t], value_grad.astype(BF16))
+
+    @pl.when(i == UNITS // STEP)
     def _():
-        acc_ref[...] += part
-
-    @pl.when(i == OWN - 1)
-    def _():
-        acc = acc_ref[...]
-        high = acc.astype(BF16)
-        low = (acc - high.astype(F32)).astype(BF16)
-        weight = w_ref[...]
-        tg = dot_nt(high, weight) + dot_nt(low, weight)
+        text = text_ref[...]
+        tg = jnp.zeros((GTEXT, TEXT), F32)
+        for h in range(HPD):
+            acc = acc_ref[h]
+            high = acc.astype(BF16)
+            low = (acc - high.astype(F32)).astype(BF16)
+            tg = tg + dot_nt(high, w3_ref[h]) + dot_nt(low, w3_ref[h])
+            wg_ref[:, h * LANES : (h + 1) * LANES] = dot_tn(text, high) + dot_tn(text, low)
         tg = tg.reshape(PEERS, BUCKET, TEXT)
         for c in range(2):
             both = jnp.concatenate(
                 [tg[:, :, 2 * c * LANES : (2 * c + 1) * LANES], tg[:, :, (2 * c + 1) * LANES : (2 * c + 2) * LANES]],
                 axis=1,
             ).astype(BF16)
-            off = OWN * BLOCK + c * 2 * BUCKET
+            off = c * 2 * BUCKET
             out_ref[:, off : off + 2 * BUCKET, :] = both
-        text = text_ref[...]
-        wg_ref[...] = dot_tn(text, high) + dot_tn(text, low)
 
 
 def attend(zi, msg, own, got, w):
     full = lambda shape: pl.BlockSpec(shape, lambda i, z: (0,) * len(shape))
+    last = UNITS // STEP - 1
     return pl.pallas_call(
         attend_kernel,
         grid_spec=pltpu.PrefetchScalarGridSpec(
             num_scalar_prefetch=1,
-            grid=(OWN,),
+            grid=(UNITS // STEP + 1,),
             in_specs=[
                 full((PEERS * 8, LANES)),
                 full((COMPACT, LANES)),
-                pl.BlockSpec((PEERS, BLOCK, LANES), lambda i, z: (0, i, 0)),
-                pl.BlockSpec((PEERS, TEXT_ROWS, LANES), lambda i, z: (0, OWN * BLOCK // TEXT_ROWS, 0)),
+                pl.BlockSpec((PEERS, STEP * BLOCK, LANES), lambda i, z: (0, jnp.minimum(i, last), 0)),
+                pl.BlockSpec((PEERS, TEXT_ROWS, LANES), lambda i, z: (0, BODY_ROWS // TEXT_ROWS, 0)),
                 full((TEXT, COLS)),
             ],
-            out_specs=[full((PEERS, MSG_ROWS, LANES)), full((TEXT, COLS))],
-            scratch_shapes=[pltpu.VMEM((GTEXT, COLS), F32), pltpu.VMEM((GTEXT, TEXT), BF16)],
+            out_specs=[pl.BlockSpec((PEERS, STEP * BLOCK, LANES), lambda i, z: (0, i, 0)), full((TEXT, COLS))],
+            scratch_shapes=[
+                pltpu.VMEM((HPD, GTEXT, LANES), F32),
+                pltpu.VMEM((GTEXT, TEXT), BF16),
+                pltpu.VMEM((HPD, TEXT, LANES), BF16),
+                pltpu.VMEM((NEAR, SLOTS, SLOTS), F32),
+                pltpu.VMEM((NEAR, SLOTS, GTEXT), BF16),
+                pltpu.VMEM((NEAR, SLOTS, TEXT), BF16),
+            ],
         ),
         out_shape=[
-            jax.ShapeDtypeStruct((PEERS, MSG_ROWS, LANES), BF16),
-            jax.ShapeDtypeStruct((TEXT, COLS), F32),
+            pltpu.HBM((PEERS, MSG_ROWS, LANES), BF16),
+            pltpu.HBM((TEXT, COLS), F32),
         ],
-        compiler_params=pltpu.CompilerParams(vmem_limit_bytes=24 << 20),
+        compiler_params=pltpu.CompilerParams(vmem_limit_bytes=28 << 20),
         name="attend",
     )(zi, msg, own, got, got, w)
 
@@ -294,21 +316,20 @@
     sel = sel_ref[...]
     for pair, (a_ref, b_ref) in enumerate(((o_ref, q_ref), (k_ref, v_ref))):
         for h in range(HPD):
-            parts = []
-            for i in range(OWN):
-                off = i * BLOCK + (pair * HPD + h) * 2 * BUCKET
-                parts.append(
-                    in_ref[:, 0, off : off + 2 * BUCKET, :].astype(F32).reshape(NZ, 1, 2, BUCKET, LANES)
-                )
-            both = jnp.concatenate(parts, axis=1)
-            a = both[:, :, 0].reshape(COMPACT * BUCKET, LANES).astype(BF16)
-            b = both[:, :, 1].reshape(COMPACT * BUCKET, LANES).astype(BF16)
+            tiles = []
+            for owner in range(OWNERS):
+                unit = owner * HPD + h
+                off = unit % UNITS * BLOCK + pair * 2 * BUCKET
+                tiles.append(in_ref[unit // UNITS, 0, off : off + 2 * BUCKET, :].astype(F32))
+            blank = [jnp.zeros((BUCKET, LANES), F32)] * (COMPACT - OWNERS)
+            a = jnp.concatenate([t[:BUCKET] for t in tiles] + blank, axis=0).astype(BF16)
+            b = jnp.concatenate([t[BUCKET:] for t in tiles] + blank, axis=0).astype(BF16)
             span = slice(h * LANES, (h + 1) * LANES)
             a_ref[:, span] = dot(sel, a).astype(BF16)
             b_ref[:, span] = dot(sel, b).astype(BF16)
 
     for c in range(2):
-        off = OWN * BLOCK + c * 2 * BUCKET
+        off = BODY_ROWS + c * 2 * BUCKET
         total = jnp.sum(in_ref[:, 0, off : off + 2 * BUCKET, :].astype(F32), axis=0)
         for half in range(2):
             span = slice((2 * c + half) * LANES, (2 * c + half + 1) * LANES)
@@ -363,30 +384,30 @@
     return x
 
 
-def halve(x, axis, bit, dim):
+def halve(x, axis, bit, dim, kind):
     up = (lax.axis_index(axis) & bit) != 0
     zero, one = lax.index_in_dim(x, 0, dim, False), lax.index_in_dim(x, 1, dim, False)
-    return jnp.where(up, one, zero) + swap(jnp.where(up, zero, one), axis, bit)
-
-
-def x_split_kernel(x_ref, in_ref, *out_refs):
-    for f, out_ref in enumerate(out_refs):
+    return jnp.where(up, one, zero), swap(jnp.where(up, zero, one).astype(kind), axis, bit)
+
+
+def x_split_kernel(x_ref, keep_ref, got_ref, *refs):
+    total_ref = refs[NX]
+    total_ref[...] = keep_ref[...] + got_ref[...].astype(F32)
+    for f, out_ref in enumerate(refs[:NX]):
         for j in range(NZ):
-            out_ref[pl.ds(j, 1), :] = in_ref[pl.ds(j * NX + (x_ref[0] ^ f), 1), :]
+            out_ref[pl.ds(j, 1), :] = total_ref[pl.ds(j * NX + (x_ref[0] ^ f), 1), :]
 
 
 def z_split_kernel(z_ref, *refs):
+    low = z_ref[0] & 3
     for f, out_ref in enumerate(refs[NX:]):
-        for j in range(NX):
-            out_ref[pl.ds(j, 1), :] = refs[j][pl.ds(z_ref[0] ^ f, 1), :]
-
-
-def row_sum_kernel(x_ref, *refs):
-    out_ref, total_ref = refs[NZ:]
-    total = refs[0][...]
-    for f in range(1, NZ):
-        total = total + refs[f][...]
-    total_ref[...] = total
+        for h in range(2):
+            for j in range(NX):
+                out_ref[pl.ds(h * NX + j, 1), :] = refs[j][pl.ds(h * 4 + (low ^ f), 1), :]
+
+
+def row_sum_kernel(x_ref, keep_ref, got_ref, out_ref, total_ref):
+    total_ref[...] = keep_ref[...] + got_ref[...]
     for c in range(NX):
         out_ref[:, c * COLS : (c + 1) * COLS] = total_ref[pl.ds(x_ref[0] ^ c, 1), :]
 
@@ -394,24 +415,29 @@
 def small_call(kernel, outs, scratch, index, *args):
     return pl.pallas_call(
         kernel,
-        out_shape=[jax.ShapeDtypeStruct(shape, F32) for shape in outs],
+        out_shape=[jax.ShapeDtypeStruct(shape, kind) for shape, kind in outs],
         in_specs=[pl.BlockSpec(memory_space=pltpu.SMEM)]
         + [pl.BlockSpec(memory_space=pltpu.VMEM)] * len(args),
         scratch_shapes=scratch,
-        compiler_params=pltpu.CompilerParams(vmem_limit_bytes=4 << 20),
+        compiler_params=pltpu.CompilerParams(vmem_limit_bytes=8 << 20),
     )(index, *args)
 
 
 def reduce_weight(wg, zi, xi):
     wg = wg.reshape(2, 2, 2, 2, PEERS, COLS)
-    wg = halve(wg, "dp", 1, 3)
+    keep, got = halve(wg, "dp", 1, 3, BF16)
     for bit, dim in ((2, 2), (4, 1), (8, 0)):
-        wg = halve(wg, "dp", bit, dim)
-    parts = small_call(x_split_kernel, [(NZ, COLS)] * NX, [], xi, wg)
+        keep, got = halve(keep + got.astype(F32), "dp", bit, dim, BF16)
+    piece = ((NZ, COLS), F32)
+    parts = small_call(x_split_kernel, [piece] * NX, [pltpu.VMEM((PEERS, COLS), F32)], xi, keep, got)
     parts = [parts[0]] + [swap(parts[f], "seq", f) for f in range(1, NX)]
-    parts = small_call(z_split_kernel, [(NX, COLS)] * NZ, [], zi, *parts)
-    parts = [parts[0]] + [swap(parts[f], "seq", f * NX) for f in range(1, NZ)]
-    return small_call(row_sum_kernel, [(1, NX * COLS)], [pltpu.VMEM((NX, COLS), F32)], xi, *parts)[0]
+    parts = small_call(z_split_kernel, [piece] * 4, [], zi, *parts)
+    total = parts[0]
+    for f in range(1, 4):
+        total = total + swap(parts[f], "seq", f * NX)
+    keep, got = halve(total.reshape(2, NX, COLS), "seq", 16, 0, F32)
+    row = [((1, NX * COLS), F32)]
+    return small_call(row_sum_kernel, row, [pltpu.VMEM((NX, COLS), F32)], xi, keep, got)[0]
 
 
 def local(query, key, value, text, cond_weight, cotangent, dest, segment, align):

time: 198 us -> 179 us (0.904)
  the two profiles are of different devices: /device:TPU:1 before, /device:TPU:40 now
where the time goes in v4:
time: 179 us; the launch traced here: 178 us
  waiting for transfers between devices  71.6 us (40%)
  starting transfers between devices  59.1 us (33%)
  blocking collectives  23.7 us (13%)
  Pallas kernels  22.3 us (12%)
    ppermute x15, starting transfers between devices, swap(): return lax.ppermute(x, axis, [(j, j ^ bit) for j in range(size)])  49.5 us
    ppermute x15, waiting for transfers between devices, swap(): return lax.ppermute(x, axis, [(j, j ^ bit) for j in range(size)])  43.1 us
    all_to_all x2, waiting for transfers between devices, exchange(): return lax.all_to_all(x, 'seq', split_axis=0, concat_axis=0, tiled=True)  28.5 us
    all_to_all x1, blocking collectives, exchange(): return lax.all_to_all(x, 'seq', split_axis=0, concat_axis=0, tiled=True)  23.7 us
    pallas_call x1, Pallas kernels, attend(): pl.pallas_call(attend_kernel, grid_spec=pltpu.PrefetchScalarGridSpec(num_...  11.9 us
    all_to_all x2, starting transfers between devices, exchange(): return lax.all_to_all(x, 'seq', split_axis=0, concat_axis=0, tiled=True)  9.57 us
    pallas_call x1, Pallas kernels, pack(): pl.pallas_call(pack_kernel, grid=(NX,), in_specs=[full((PEERS * 8, LANES)...  4.98 us
  transfers between devices with their start and end apart: 17, of which 14 were waited for; matrix products, arithmetic and copies ran while one was open for 0% of the time, Pallas kernels for 0%

profile of v4, /device:TPU:40, one launch (start us, length us, event | category | flops | bytes accessed | tf_op | source)
XLA Modules:
  0.0 178.3 jit_solution(17089966329065834308)
XLA Ops:
  0.6 1.4 prep.1
  2.0 23.7 %all_to_all.15 = f32[32,8,128]{2,1,0:T(8,128)} all-to-all(f32[32,8,128]{2,1,0:T(8,128)} %bitcast.59), channel_id=1, replica_groups=mesh['dp'=16,'seq'=32] {'seq'}, dimensions={0} | all-to-all | bytes 262144 | tf_op jit(solution)/shard_map/all_to_all | solution.py:368
  25.8 5.0 %pack.1 = (bf16[8,4,288,128]{3,2,1,0:T(8,128)(2,1)}, f32[24,128]{1,0:T(8,128)}) custom-call(f32[256,128]{1,0:T(8,128)} %bitcast.50, s32[1,128]{1,0:T(1,128)} %bitcast.55, bf16[8,512]{1,0:T(8,128)(2,1)} %text_ref.1, bf16[128,1536]{1,0:T(8,128)(2,1)} %q_ref.1, bf16[128,1536]{1,0:T(8,128)(2,1)} %k_ref.1, bf16[128,1536]{1,0:T(8,128)(2,1)} %v_ref.1, ...), custom_call_target="tpu_custom_call" | custom-call | tf_op jit(solution)/shard_map/pack/pallas_call | solution.py:142
  30.8 4.2 %all-to-all-start.1 = ((bf16[32,288,128]{2,1,0:T(8,128)(2,1)}), bf16[32,288,128]{2,1,0:T(8,128)(2,1)S(1)}, u32[]{:S(2)}, u32[]{:S(2)}) async-start(bf16[32,288,128]{2,1,0:T(8,128)(2,1)} %bitcast.57), calls=%async_computation.1 | async-start | bytes 4718592 | tf_op jit(solution)/shard_map/all_to_all | solution.py:368
  35.0 2.9 %collective-permute-start = (bf16[32,384]{1,0:T(8,128)(2,1)S(1)}, bf16[32,384]{1,0:T(8,128)(2,1)S(1)}, u32[]{:S(2)}, u32[]{:S(2)}) collective-permute-start(bf16[32,384]{1,0:T(8,128)(2,1)S(1)} %bitcast.62), channel_id=1, source_target_pairs={{0,256},{32,288},{64,320},{96,352},{128,384},{160,416},{192,448},{... | collective-permute-start | bytes 73736 | tf_op jit(solution)/shard_map/ppermute | solution.py:373
  37.9 6.7 %collective-permute-done = bf16[32,384]{1,0:T(8,128)(2,1)S(1)} collective-permute-done((bf16[32,384]{1,0:T(8,128)(2,1)S(1)}, bf16[32,384]{1,0:T(8,128)(2,1)S(1)}, u32[]{:S(2)}, u32[]{:S(2)}) %collective-permute-start) | collective-permute-done | bytes 24608 | tf_op jit(solution)/shard_map/ppermute | solution.py:373
  44.7 2.7 %collective-permute-start.1 = (bf16[2,32,384]{2,1,0:T(8,128)(2,1)S(1)}, bf16[2,32,384]{2,1,0:T(8,128)(2,1)S(1)}, u32[]{:S(2)}, u32[]{:S(2)}) collective-permute-start(bf16[2,32,384]{2,1,0:T(8,128)(2,1)S(1)} %pad_maximum_fusion.3), channel_id=1, source_target_pairs={{0,128},{32,160},{64,192},{96,224},{128,0},{160,32},{192,64},{224,... | collective-permute-start | bytes 147464 | tf_op jit(solution)/shard_map/ppermute | solution.py:373
  47.4 4.2 %collective-permute-done.1 = bf16[2,32,384]{2,1,0:T(8,128)(2,1)S(1)} collective-permute-done((bf16[2,32,384]{2,1,0:T(8,128)(2,1)S(1)}, bf16[2,32,384]{2,1,0:T(8,128)(2,1)S(1)}, u32[]{:S(2)}, u32[]{:S(2)}) %collective-permute-start.1) | collective-permute-done | bytes 49184 | tf_op jit(solution)/shard_map/ppermute | solution.py:373
  51.7 3.7 %collective-permute-start.2 = (bf16[2,2,32,384]{3,2,0,1:T(8,128)(2,1)S(1)}, bf16[2,2,32,384]{3,2,0,1:T(8,128)(2,1)S(1)}, u32[]{:S(2)}, u32[]{:S(2)}) collective-permute-start(bf16[2,2,32,384]{3,2,0,1:T(8,128)(2,1)S(1)} %pad_maximum_fusion.2), channel_id=1, source_target_pairs={{0,64},{32,96},{64,0},{96,32},{128,192},{160,224},{192,128},{224,1... | collective-permute-start | bytes 294920 | tf_op jit(solution)/shard_map/ppermute | solution.py:373
  55.5 2.8 %collective-permute-done.2 = bf16[2,2,32,384]{3,2,0,1:T(8,128)(2,1)S(1)} collective-permute-done((bf16[2,2,32,384]{3,2,0,1:T(8,128)(2,1)S(1)}, bf16[2,2,32,384]{3,2,0,1:T(8,128)(2,1)S(1)}, u32[]{:S(2)}, u32[]{:S(2)}) %collective-permute-start.2) | collective-permute-done | bytes 98336 | tf_op jit(solution)/shard_map/ppermute | solution.py:373
  58.3 1.9 %collective-permute-start.3 = (bf16[2,2,2,32,384]{4,3,0,1,2:T(8,128)(2,1)S(1)}, bf16[2,2,2,32,384]{4,3,0,1,2:T(8,128)(2,1)S(1)}, u32[]{:S(2)}, u32[]{:S(2)}) collective-permute-start(bf16[2,2,2,32,384]{4,3,0,1,2:T(8,128)(2,1)S(1)} %pad_maximum_fusion.1), channel_id=1, source_target_pairs={{0,32},{32,0},{64,96},{96,64},{128,160},{160,128},{192,224},{224,1... | collective-permute-start | bytes 589832 | tf_op jit(solution)/shard_map/ppermute | solution.py:373
  61.8 28.5 %all-to-all-done.1.in_ref.tail_ref = bf16[32,288,128]{2,1,0:T(8,128)(2,1)S(1)} async-done(((bf16[32,288,128]{2,1,0:T(8,128)(2,1)}), bf16[32,288,128]{2,1,0:T(8,128)(2,1)S(1)}, u32[]{:S(2)}, u32[]{:S(2)}) %all-to-all-start.1) | async-done | bytes 2359328 | tf_op jit(solution)/shard_map/all_to_all | solution.py:368
  90.3 11.9 %attend.1 = (bf16[32,288,128]{2,1,0:T(8,128)(2,1)}, f32[512,384]{1,0:T(8,128)}) custom-call(s32[1]{0:T(128)} %bitcast.5.z_ref, f32[256,128]{1,0:T(8,128)S(1)} %bitcast.51, f32[24,128]{1,0:T(8,128)S(1)} %copy-done.1, bf16[32,288,128]{2,1,0:T(8,128)(2,1)S(1)} %all-to-all-done.1.in_ref.tail_ref, bf16[32,288,128]{2,1,0:T(8,128)(2,1)S(1)} %all-to-all-done.1.in_ref.tail_ref, ...), custom_call_target="tpu_custom_call" | custom-call | tf_op jit(solution)/shard_map/attend/pallas_call | solution.py:277
  102.2 5.4 %all-to-all-start.2 = ((bf16[32,288,128]{2,1,0:T(8,128)(2,1)}), bf16[32,288,128]{2,1,0:T(8,128)(2,1)S(1)}, u32[]{:S(2)}, u32[]{:S(2)}) async-start(bf16[32,288,128]{2,1,0:T(8,128)(2,1)} %get-tuple-element.25), calls=%async_computation.2 | async-start | bytes 4718592 | tf_op jit(solution)/shard_map/all_to_all | solution.py:368
  107.7 1.9 %collective-permute-start.4 = (bf16[2,2,2,32,384]{4,3,0,1,2:T(8,128)(2,1)S(1)}, bf16[2,2,2,32,384]{4,3,0,1,2:T(8,128)(2,1)S(1)}, u32[]{:S(2)}, u32[]{:S(2)}) collective-permute-start(bf16[2,2,2,32,384]{4,3,0,1,2:T(8,128)(2,1)S(1)} %fusion), channel_id=1, source_target_pairs={{0,32},{32,0},{64,96},{96,64},{128,160},{160,128},{192,224},{224,1... | collective-permute-start | bytes 589832 | tf_op jit(solution)/shard_map/ppermute | solution.py:373
  111.2 3.2 %collective-permute-start.5 = (bf16[2,2,32,384]{3,2,0,1:T(8,128)(2,1)S(1)}, bf16[2,2,32,384]{3,2,0,1:T(8,128)(2,1)S(1)}, u32[]{:S(2)}, u32[]{:S(2)}) collective-permute-start(bf16[2,2,32,384]{3,2,0,1:T(8,128)(2,1)S(1)} %fusion.1), channel_id=1, source_target_pairs={{0,64},{32,96},{64,0},{96,32},{128,192},{160,224},{192,128},{224,1... | collective-permute-start | bytes 294920 | tf_op jit(solution)/shard_map/ppermute | solution.py:373
  114.4 3.5 %collective-permute-done.5 = bf16[2,2,32,384]{3,2,0,1:T(8,128)(2,1)S(1)} collective-permute-done((bf16[2,2,32,384]{3,2,0,1:T(8,128)(2,1)S(1)}, bf16[2,2,32,384]{3,2,0,1:T(8,128)(2,1)S(1)}, u32[]{:S(2)}, u32[]{:S(2)}) %collective-permute-start.5) | collective-permute-done | bytes 98336 | tf_op jit(solution)/shard_map/ppermute | solution.py:373
  117.9 2.7 %collective-permute-start.6 = (bf16[2,32,384]{2,1,0:T(8,128)(2,1)S(1)}, bf16[2,32,384]{2,1,0:T(8,128)(2,1)S(1)}, u32[]{:S(2)}, u32[]{:S(2)}) collective-permute-start(bf16[2,32,384]{2,1,0:T(8,128)(2,1)S(1)} %fusion.2), channel_id=1, source_target_pairs={{0,128},{32,160},{64,192},{96,224},{128,0},{160,32},{192,64},{224,... | collective-permute-start | bytes 147464 | tf_op jit(solution)/shard_map/ppermute | solution.py:373
  120.6 4.3 %collective-permute-done.6 = bf16[2,32,384]{2,1,0:T(8,128)(2,1)S(1)} collective-permute-done((bf16[2,32,384]{2,1,0:T(8,128)(2,1)S(1)}, bf16[2,32,384]{2,1,0:T(8,128)(2,1)S(1)}, u32[]{:S(2)}, u32[]{:S(2)}) %collective-permute-start.6) | collective-permute-done | bytes 49184 | tf_op jit(solution)/shard_map/ppermute | solution.py:373
  125.0 2.8 %collective-permute-start.7 = (bf16[32,384]{1,0:T(8,128)(2,1)S(1)}, bf16[32,384]{1,0:T(8,128)(2,1)S(1)}, u32[]{:S(2)}, u32[]{:S(2)}) collective-permute-start(bf16[32,384]{1,0:T(8,128)(2,1)S(1)} %fusion.3), channel_id=1, source_target_pairs={{0,256},{32,288},{64,320},{96,352},{128,384},{160,416},{192,448},{... | collective-permute-start | bytes 73736 | tf_op jit(solution)/shard_map/ppermute | solution.py:373
  127.8 7.1 %collective-permute-done.7.got_ref = bf16[32,384]{1,0:T(8,128)(2,1)S(1)} collective-permute-done((bf16[32,384]{1,0:T(8,128)(2,1)S(1)}, bf16[32,384]{1,0:T(8,128)(2,1)S(1)}, u32[]{:S(2)}, u32[]{:S(2)}) %collective-permute-start.7) | collective-permute-done | bytes 24608 | tf_op jit(solution)/shard_map/ppermute | solution.py:373
  134.9 4.9 %collective-permute-start.10 = (f32[8,384]{1,0:T(8,128)S(1)}, f32[8,384]{1,0:T(8,128)S(1)}, u32[]{:S(2)}, u32[]{:S(2)}) collective-permute-start(f32[8,384]{1,0:T(8,128)S(1)} %get-tuple-element.35), channel_id=1, source_target_pairs={{0,3},{1,2},{2,1},{3,0},{4,7},{5,6},{6,5},{7,4},{8,11},{9,10},{10,... | collective-permute-start | bytes 36872 | tf_op jit(solution)/shard_map/ppermute | solution.py:373
  139.8 2.2 %collective-permute-start.8 = (f32[8,384]{1,0:T(8,128)S(1)}, f32[8,384]{1,0:T(8,128)S(1)}, u32[]{:S(2)}, u32[]{:S(2)}) collective-permute-start(f32[8,384]{1,0:T(8,128)S(1)} %get-tuple-element.33), channel_id=1, source_target_pairs={{0,1},{1,0},{2,3},{3,2},{4,5},{5,4},{6,7},{7,6},{8,9},{9,8},{10,11... | collective-permute-start | bytes 36872 | tf_op jit(solution)/shard_map/ppermute | solution.py:373
  142.0 3.4 %collective-permute-start.9 = (f32[8,384]{1,0:T(8,128)S(1)}, f32[8,384]{1,0:T(8,128)S(1)}, u32[]{:S(2)}, u32[]{:S(2)}) collective-permute-start(f32[8,384]{1,0:T(8,128)S(1)} %get-tuple-element.34), channel_id=1, source_target_pairs={{0,2},{1,3},{2,0},{3,1},{4,6},{5,7},{6,4},{7,5},{8,10},{9,11},{10,... | collective-permute-start | bytes 36872 | tf_op jit(solution)/shard_map/ppermute | solution.py:373
  145.6 3.9 %collective-permute-done.9.refs_2_ = f32[8,384]{1,0:T(8,128)S(1)} collective-permute-done((f32[8,384]{1,0:T(8,128)S(1)}, f32[8,384]{1,0:T(8,128)S(1)}, u32[]{:S(2)}, u32[]{:S(2)}) %collective-permute-start.9) | collective-permute-done | bytes 12320 | tf_op jit(solution)/shard_map/ppermute | solution.py:373
  149.5 5.1 %collective-permute-start.11 = (f32[8,384]{1,0:T(8,128)S(1)}, f32[8,384]{1,0:T(8,128)S(1)}, u32[]{:S(2)}, u32[]{:S(2)}) collective-permute-start(f32[8,384]{1,0:T(8,128)S(1)} %get-tuple-element.37), channel_id=1, source_target_pairs={{0,4},{1,5},{2,6},{3,7},{4,0},{5,1},{6,2},{7,3},{8,12},{9,13},{10,... | collective-permute-start | bytes 36872 | tf_op jit(solution)/shard_map/ppermute | solution.py:373
  154.6 2.9 %collective-permute-start.12 = (f32[8,384]{1,0:T(8,128)S(1)}, f32[8,384]{1,0:T(8,128)S(1)}, u32[]{:S(2)}, u32[]{:S(2)}) collective-permute-start(f32[8,384]{1,0:T(8,128)S(1)} %get-tuple-element.38), channel_id=1, source_target_pairs={{0,8},{1,9},{2,10},{3,11},{4,12},{5,13},{6,14},{7,15},{8,0},{9,1},... | collective-permute-start | bytes 36872 | tf_op jit(solution)/shard_map/ppermute | solution.py:373
  157.6 3.3 %collective-permute-start.13 = (f32[8,384]{1,0:T(8,128)S(1)}, f32[8,384]{1,0:T(8,128)S(1)}, u32[]{:S(2)}, u32[]{:S(2)}) collective-permute-start(f32[8,384]{1,0:T(8,128)S(1)} %get-tuple-element.39), channel_id=1, source_target_pairs={{0,12},{1,13},{2,14},{3,15},{4,8},{5,9},{6,10},{7,11},{8,4},{9,5},... | collective-permute-start | bytes 36872 | tf_op jit(solution)/shard_map/ppermute | solution.py:373
  161.1 3.8 %collective-permute-done.13 = f32[8,384]{1,0:T(8,128)S(1)} collective-permute-done((f32[8,384]{1,0:T(8,128)S(1)}, f32[8,384]{1,0:T(8,128)S(1)}, u32[]{:S(2)}, u32[]{:S(2)}) %collective-permute-start.13) | collective-permute-done | bytes 12320 | tf_op jit(solution)/shard_map/ppermute | solution.py:373
  165.0 5.9 %collective-permute-start.14 = (f32[4,384]{1,0:T(4,128)S(1)}, f32[4,384]{1,0:T(4,128)S(1)}, u32[]{:S(2)}, u32[]{:S(2)}) collective-permute-start(f32[4,384]{1,0:T(4,128)S(1)} %get-tuple-element.50), channel_id=1, source_target_pairs={{0,16},{1,17},{2,18},{3,19},{4,20},{5,21},{6,22},{7,23},{8,24},{9,... | collective-permute-start | bytes 18440 | tf_op jit(solution)/shard_map/ppermute | solution.py:373
  170.8 3.5 %collective-permute-done.14.got_ref = f32[4,384]{1,0:T(4,128)S(1)} collective-permute-done((f32[4,384]{1,0:T(4,128)S(1)}, f32[4,384]{1,0:T(4,128)S(1)}, u32[]{:S(2)}, u32[]{:S(2)}) %collective-permute-start.14) | collective-permute-done | bytes 6176 | tf_op jit(solution)/shard_map/ppermute | solution.py:373
  175.0 3.3 %unpack.1 = (bf16[128,1536]{1,0:T(8,128)(2,1)}, bf16[128,1536]{1,0:T(8,128)(2,1)}, bf16[128,1536]{1,0:T(8,128)(2,1)}, bf16[128,1536]{1,0:T(8,128)(2,1)}, f32[8,512]{1,0:T(8,128)}) custom-call(f32[256,128]{1,0:T(8,128)S(1)} %bitcast.52, s32[1,128]{1,0:T(1,128)S(1)} %bitcast.56, bf16[8,4,288,128]{3,2,1,0:T(8,128)(2,1)S(1)} %bitcast.49), custom_call_target="tpu_custom_call" | custom-call | tf_op jit(solution)/shard_map/unpack/pallas_call | solution.py:351
  (40 shorter events, 4.5 us)
Async XLA Ops:
  30.7 4.2 %copy-start = (f32[32,8,128]{2,1,0:T(8,128)S(1)}, f32[32,8,128]{2,1,0:T(8,128)}, u32[]{:S(2)}) copy-start(f32[32,8,128]{2,1,0:T(8,128)} %all_to_all.15) | copy-start | bytes 393220
  30.8 59.5 %all-to-all-start.1 = ((bf16[32,288,128]{2,1,0:T(8,128)(2,1)}), bf16[32,288,128]{2,1,0:T(8,128)(2,1)S(1)}, u32[]{:S(2)}, u32[]{:S(2)}) async-start(bf16[32,288,128]{2,1,0:T(8,128)(2,1)} %bitcast.57), calls=%async_computation.1 | async-start | bytes 4718592 | tf_op jit(solution)/shard_map/all_to_all | solution.py:368
  35.0 55.3 %copy-start.1 = (f32[24,128]{1,0:T(8,128)S(1)}, f32[24,128]{1,0:T(8,128)}, u32[]{:S(2)}) copy-start(f32[24,128]{1,0:T(8,128)} %get-tuple-element.23.own_ref) | copy-start | bytes 36868
  35.0 9.6 %collective-permute-start = (bf16[32,384]{1,0:T(8,128)(2,1)S(1)}, bf16[32,384]{1,0:T(8,128)(2,1)S(1)}, u32[]{:S(2)}, u32[]{:S(2)}) collective-permute-start(bf16[32,384]{1,0:T(8,128)(2,1)S(1)} %bitcast.62), channel_id=1, source_target_pairs={{0,256},{32,288},{64,320},{96,352},{128,384},{160,416},{192,448},{... | collective-permute-start | bytes 73736 | tf_op jit(solution)/shard_map/ppermute | solution.py:373
  44.7 7.0 %collective-permute-start.1 = (bf16[2,32,384]{2,1,0:T(8,128)(2,1)S(1)}, bf16[2,32,384]{2,1,0:T(8,128)(2,1)S(1)}, u32[]{:S(2)}, u32[]{:S(2)}) collective-permute-start(bf16[2,32,384]{2,1,0:T(8,128)(2,1)S(1)} %pad_maximum_fusion.3), channel_id=1, source_target_pairs={{0,128},{32,160},{64,192},{96,224},{128,0},{160,32},{192,64},{224,... | collective-permute-start | bytes 147464 | tf_op jit(solution)/shard_map/ppermute | solution.py:373
  51.7 6.5 %collective-permute-start.2 = (bf16[2,2,32,384]{3,2,0,1:T(8,128)(2,1)S(1)}, bf16[2,2,32,384]{3,2,0,1:T(8,128)(2,1)S(1)}, u32[]{:S(2)}, u32[]{:S(2)}) collective-permute-start(bf16[2,2,32,384]{3,2,0,1:T(8,128)(2,1)S(1)} %pad_maximum_fusion.2), channel_id=1, source_target_pairs={{0,64},{32,96},{64,0},{96,32},{128,192},{160,224},{192,128},{224,1... | collective-permute-start | bytes 294920 | tf_op jit(solution)/shard_map/ppermute | solution.py:373
  58.3 3.3 %collective-permute-start.3 = (bf16[2,2,2,32,384]{4,3,0,1,2:T(8,128)(2,1)S(1)}, bf16[2,2,2,32,384]{4,3,0,1,2:T(8,128)(2,1)S(1)}, u32[]{:S(2)}, u32[]{:S(2)}) collective-permute-start(bf16[2,2,2,32,384]{4,3,0,1,2:T(8,128)(2,1)S(1)} %pad_maximum_fusion.1), channel_id=1, source_target_pairs={{0,32},{32,0},{64,96},{96,64},{128,160},{160,128},{192,224},{224,1... | collective-permute-start | bytes 589832 | tf_op jit(solution)/shard_map/ppermute | solution.py:373
  102.2 5.4 %copy-start.3 = (f32[512,384]{1,0:T(8,128)S(1)}, f32[512,384]{1,0:T(8,128)}, u32[]{:S(2)}) copy-start(f32[512,384]{1,0:T(8,128)} %get-tuple-element.31) | copy-start | bytes 2359300
  102.2 72.8 %all-to-all-start.2 = ((bf16[32,288,128]{2,1,0:T(8,128)(2,1)}), bf16[32,288,128]{2,1,0:T(8,128)(2,1)S(1)}, u32[]{:S(2)}, u32[]{:S(2)}) async-start(bf16[32,288,128]{2,1,0:T(8,128)(2,1)} %get-tuple-element.25), calls=%async_computation.2 | async-start | bytes 4718592 | tf_op jit(solution)/shard_map/all_to_all | solution.py:368
  107.7 67.3 %copy-start.2 = (s32[128]{0:T(128)S(1)}, s32[128]{0:T(128)}, u32[]{:S(2)}) copy-start(s32[128]{0:T(128)} %param.15) | copy-start | bytes 1540
  107.7 3.3 %collective-permute-start.4 = (bf16[2,2,2,32,384]{4,3,0,1,2:T(8,128)(2,1)S(1)}, bf16[2,2,2,32,384]{4,3,0,1,2:T(8,128)(2,1)S(1)}, u32[]{:S(2)}, u32[]{:S(2)}) collective-permute-start(bf16[2,2,2,32,384]{4,3,0,1,2:T(8,128)(2,1)S(1)} %fusion), channel_id=1, source_target_pairs={{0,32},{32,0},{64,96},{96,64},{128,160},{160,128},{192,224},{224,1... | collective-permute-start | bytes 589832 | tf_op jit(solution)/shard_map/ppermute | solution.py:373
  111.2 6.7 %collective-permute-start.5 = (bf16[2,2,32,384]{3,2,0,1:T(8,128)(2,1)S(1)}, bf16[2,2,32,384]{3,2,0,1:T(8,128)(2,1)S(1)}, u32[]{:S(2)}, u32[]{:S(2)}) collective-permute-start(bf16[2,2,32,384]{3,2,0,1:T(8,128)(2,1)S(1)} %fusion.1), channel_id=1, source_target_pairs={{0,64},{32,96},{64,0},{96,32},{128,192},{160,224},{192,128},{224,1... | collective-permute-start | bytes 294920 | tf_op jit(solution)/shard_map/ppermute | solution.py:373
  117.9 7.0 %collective-permute-start.6 = (bf16[2,32,384]{2,1,0:T(8,128)(2,1)S(1)}, bf16[2,32,384]{2,1,0:T(8,128)(2,1)S(1)}, u32[]{:S(2)}, u32[]{:S(2)}) collective-permute-start(bf16[2,32,384]{2,1,0:T(8,128)(2,1)S(1)} %fusion.2), channel_id=1, source_target_pairs={{0,128},{32,160},{64,192},{96,224},{128,0},{160,32},{192,64},{224,... | collective-permute-start | bytes 147464 | tf_op jit(solution)/shard_map/ppermute | solution.py:373
  125.0 9.9 %collective-permute-start.7 = (bf16[32,384]{1,0:T(8,128)(2,1)S(1)}, bf16[32,384]{1,0:T(8,128)(2,1)S(1)}, u32[]{:S(2)}, u32[]{:S(2)}) collective-permute-start(bf16[32,384]{1,0:T(8,128)(2,1)S(1)} %fusion.3), channel_id=1, source_target_pairs={{0,256},{32,288},{64,320},{96,352},{128,384},{160,416},{192,448},{... | collective-permute-start | bytes 73736 | tf_op jit(solution)/shard_map/ppermute | solution.py:373
  134.9 10.5 %collective-permute-start.10 = (f32[8,384]{1,0:T(8,128)S(1)}, f32[8,384]{1,0:T(8,128)S(1)}, u32[]{:S(2)}, u32[]{:S(2)}) collective-permute-start(f32[8,384]{1,0:T(8,128)S(1)} %get-tuple-element.35), channel_id=1, source_target_pairs={{0,3},{1,2},{2,1},{3,0},{4,7},{5,6},{6,5},{7,4},{8,11},{9,10},{10,... | collective-permute-start | bytes 36872 | tf_op jit(solution)/shard_map/ppermute | solution.py:373
  139.8 5.7 %collective-permute-start.8 = (f32[8,384]{1,0:T(8,128)S(1)}, f32[8,384]{1,0:T(8,128)S(1)}, u32[]{:S(2)}, u32[]{:S(2)}) collective-permute-start(f32[8,384]{1,0:T(8,128)S(1)} %get-tuple-element.33), channel_id=1, source_target_pairs={{0,1},{1,0},{2,3},{3,2},{4,5},{5,4},{6,7},{7,6},{8,9},{9,8},{10,11... | collective-permute-start | bytes 36872 | tf_op jit(solution)/shard_map/ppermute | solution.py:373
  142.0 7.5 %collective-permute-start.9 = (f32[8,384]{1,0:T(8,128)S(1)}, f32[8,384]{1,0:T(8,128)S(1)}, u32[]{:S(2)}, u32[]{:S(2)}) collective-permute-start(f32[8,384]{1,0:T(8,128)S(1)} %get-tuple-element.34), channel_id=1, source_target_pairs={{0,2},{1,3},{2,0},{3,1},{4,6},{5,7},{6,4},{7,5},{8,10},{9,11},{10,... | collective-permute-start | bytes 36872 | tf_op jit(solution)/shard_map/ppermute | solution.py:373
  149.5 11.3 %collective-permute-start.11 = (f32[8,384]{1,0:T(8,128)S(1)}, f32[8,384]{1,0:T(8,128)S(1)}, u32[]{:S(2)}, u32[]{:S(2)}) collective-permute-start(f32[8,384]{1,0:T(8,128)S(1)} %get-tuple-element.37), channel_id=1, source_target_pairs={{0,4},{1,5},{2,6},{3,7},{4,0},{5,1},{6,2},{7,3},{8,12},{9,13},{10,... | collective-permute-start | bytes 36872 | tf_op jit(solution)/shard_map/ppermute | solution.py:373
  154.6 6.5 %collective-permute-start.12 = (f32[8,384]{1,0:T(8,128)S(1)}, f32[8,384]{1,0:T(8,128)S(1)}, u32[]{:S(2)}, u32[]{:S(2)}) collective-permute-start(f32[8,384]{1,0:T(8,128)S(1)} %get-tuple-element.38), channel_id=1, source_target_pairs={{0,8},{1,9},{2,10},{3,11},{4,12},{5,13},{6,14},{7,15},{8,0},{9,1},... | collective-permute-start | bytes 36872 | tf_op jit(solution)/shard_map/ppermute | solution.py:373
  157.6 7.4 %collective-permute-start.13 = (f32[8,384]{1,0:T(8,128)S(1)}, f32[8,384]{1,0:T(8,128)S(1)}, u32[]{:S(2)}, u32[]{:S(2)}) collective-permute-start(f32[8,384]{1,0:T(8,128)S(1)} %get-tuple-element.39), channel_id=1, source_target_pairs={{0,12},{1,13},{2,14},{3,15},{4,8},{5,9},{6,10},{7,11},{8,4},{9,5},... | collective-permute-start | bytes 36872 | tf_op jit(solution)/shard_map/ppermute | solution.py:373
  165.0 9.4 %collective-permute-start.14 = (f32[4,384]{1,0:T(4,128)S(1)}, f32[4,384]{1,0:T(4,128)S(1)}, u32[]{:S(2)}, u32[]{:S(2)}) collective-permute-start(f32[4,384]{1,0:T(4,128)S(1)} %get-tuple-element.50), channel_id=1, source_target_pairs={{0,16},{1,17},{2,18},{3,19},{4,20},{5,21},{6,22},{7,23},{8,24},{9,... | collective-permute-start | bytes 18440 | tf_op jit(solution)/shard_map/ppermute | solution.py:373

commit v5 on v4

--- a/solution.py
+++ b/solution.py
@@ -156,7 +156,7 @@
     )(msg, dest, text, q, k, v, g)
 
 
-def owner_setup(owner, msg_ref, text):
+def owner_setup(owner, msg_ref):
     n = SLOTS
     dest = msg_ref[pl.ds(0, PEERS, stride=8), :].astype(jnp.int32)
     match = jnp.where((dest >> 8).astype(F32) == owner, 1.0, 0.0)
@@ -180,12 +180,31 @@
     label_row = jnp.sum(jnp.where(diag, label_b, 0.0), axis=0, keepdims=True)
     allowed = ((label_b == jnp.broadcast_to(label_row, (n, n))) & (label_b >= 0.0)) | diag
     pick = jnp.where(lanef == align, 1.0, 0.0).astype(BF16)
-    return jnp.where(allowed, 0.0, -1e30), pick, dot(pick, text).astype(BF16)
+    return jnp.where(allowed, 0.0, -1e30), pick
+
+
+def setup_kernel(z_ref, msg_ref, own_ref, bias_ref, pick_ref):
+    owner0 = z_ref[0] * UNITS // HPD
+    for t in range(NEAR):
+        owner = jnp.broadcast_to(own_ref[pl.ds(owner0 + t, 1), :], (PEERS, LANES))
+        bias_ref[t], pick_ref[t] = owner_setup(owner, msg_ref)
+
+
+def setup(zi, msg, own):
+    return pl.pallas_call(
+        setup_kernel,
+        in_specs=[pl.BlockSpec(memory_space=pltpu.SMEM)] + [pl.BlockSpec(memory_space=pltpu.VMEM)] * 2,
+        out_shape=[
+            pltpu.HBM((NEAR, SLOTS, SLOTS), F32),
+            pltpu.HBM((NEAR, SLOTS, GTEXT), BF16),
+        ],
+        compiler_params=pltpu.CompilerParams(vmem_limit_bytes=24 << 20),
+        name="setup",
+    )(zi, msg, own)
 
 
 def attend_kernel(
-    z_ref, msg_ref, own_ref, in_ref, tail_ref, w_ref, out_ref, wg_ref,
-    acc_ref, text_ref, w3_ref, bias_ref, pick_ref, cond_ref,
+    z_ref, bias_ref, pick_ref, in_ref, tail_ref, w_ref, out_ref, wg_ref, acc_ref, text_ref, w3_ref, cond_ref
 ):
     i = pl.program_id(0)
     n = SLOTS
@@ -202,11 +221,7 @@
                 text_ref[:, span] = tiles[:, half].reshape(GTEXT, LANES).astype(BF16)
         text = text_ref[...]
         for t in range(NEAR):
-            owner = jnp.broadcast_to(own_ref[pl.ds(owner0 + t, 1), :], (PEERS, LANES))
-            bias, pick, cond = owner_setup(owner, msg_ref, text)
-            bias_ref[t] = bias
-            pick_ref[t] = pick
-            cond_ref[t] = cond
+            cond_ref[t] = dot(pick_ref[t], text).astype(BF16)
         for h in range(HPD):
             w3_ref[h] = w_ref[:, h * LANES : (h + 1) * LANES]
         acc_ref[...] = jnp.zeros_like(acc_ref)
@@ -271,7 +286,7 @@
             out_ref[:, off : off + 2 * BUCKET, :] = both
 
 
-def attend(zi, msg, own, got, w):
+def attend(zi, bias, pick, got, w):
     full = lambda shape: pl.BlockSpec(shape, lambda i, z: (0,) * len(shape))
     last = UNITS // STEP - 1
     return pl.pallas_call(
@@ -280,8 +295,8 @@
             num_scalar_prefetch=1,
             grid=(UNITS // STEP + 1,),
             in_specs=[
-                full((PEERS * 8, LANES)),
-                full((COMPACT, LANES)),
+                full((NEAR, SLOTS, SLOTS)),
+                full((NEAR, SLOTS, GTEXT)),
                 pl.BlockSpec((PEERS, STEP * BLOCK, LANES), lambda i, z: (0, jnp.minimum(i, last), 0)),
                 pl.BlockSpec((PEERS, TEXT_ROWS, LANES), lambda i, z: (0, BODY_ROWS // TEXT_ROWS, 0)),
                 full((TEXT, COLS)),
@@ -291,8 +306,6 @@
                 pltpu.VMEM((HPD, GTEXT, LANES), F32),
                 pltpu.VMEM((GTEXT, TEXT), BF16),
                 pltpu.VMEM((HPD, TEXT, LANES), BF16),
-                pltpu.VMEM((NEAR, SLOTS, SLOTS), F32),
-                pltpu.VMEM((NEAR, SLOTS, GTEXT), BF16),
                 pltpu.VMEM((NEAR, SLOTS, TEXT), BF16),
             ],
         ),
@@ -302,7 +315,7 @@
         ],
         compiler_params=pltpu.CompilerParams(vmem_limit_bytes=28 << 20),
         name="attend",
-    )(zi, msg, own, got, got, w)
+    )(zi, bias, pick, got, got, w)
 
 
 def unpack_kernel(msg_ref, dest_ref, in_ref, o_ref, q_ref, k_ref, v_ref, tg_ref, sel_ref):
@@ -398,16 +411,18 @@
             out_ref[pl.ds(j, 1), :] = total_ref[pl.ds(j * NX + (x_ref[0] ^ f), 1), :]
 
 
-def z_split_kernel(z_ref, *refs):
-    low = z_ref[0] & 3
-    for f, out_ref in enumerate(refs[NX:]):
-        for h in range(2):
-            for j in range(NX):
-                out_ref[pl.ds(h * NX + j, 1), :] = refs[j][pl.ds(h * 4 + (low ^ f), 1), :]
-
-
-def row_sum_kernel(x_ref, keep_ref, got_ref, out_ref, total_ref):
-    total_ref[...] = keep_ref[...] + got_ref[...]
+def join_kernel(x_ref, *refs):
+    out_ref = refs[NX]
+    for z in range(NZ):
+        for f in range(NX):
+            out_ref[z, pl.ds(f, 1), :] = refs[f][pl.ds(z, 1), :]
+
+
+def row_sum_kernel(x_ref, in_ref, out_ref, total_ref):
+    total = in_ref[0]
+    for z in range(1, NZ):
+        total = total + in_ref[z]
+    total_ref[...] = total
     for c in range(NX):
         out_ref[:, c * COLS : (c + 1) * COLS] = total_ref[pl.ds(x_ref[0] ^ c, 1), :]
 
@@ -423,7 +438,7 @@
     )(index, *args)
 
 
-def reduce_weight(wg, zi, xi):
+def reduce_weight(wg, xi):
     wg = wg.reshape(2, 2, 2, 2, PEERS, COLS)
     keep, got = halve(wg, "dp", 1, 3, BF16)
     for bit, dim in ((2, 2), (4, 1), (8, 0)):
@@ -431,13 +446,11 @@
     piece = ((NZ, COLS), F32)
     parts = small_call(x_split_kernel, [piece] * NX, [pltpu.VMEM((PEERS, COLS), F32)], xi, keep, got)
     parts = [parts[0]] + [swap(parts[f], "seq", f) for f in range(1, NX)]
-    parts = small_call(z_split_kernel, [piece] * 4, [], zi, *parts)
-    total = parts[0]
-    for f in range(1, 4):
-        total = total + swap(parts[f], "seq", f * NX)
-    keep, got = halve(total.reshape(2, NX, COLS), "seq", 16, 0, F32)
+    lines = small_call(join_kernel, [((NZ, NX, COLS), F32)], [], xi, *parts)[0]
+    groups = [[z * NX + x for z in range(NZ)] for x in range(NX)]
+    lines = lax.all_to_all(lines, "seq", 0, 0, axis_index_groups=groups, tiled=True)
     row = [((1, NX * COLS), F32)]
-    return small_call(row_sum_kernel, row, [pltpu.VMEM((NX, COLS), F32)], xi, keep, got)[0]
+    return small_call(row_sum_kernel, row, [pltpu.VMEM((NX, COLS), F32)], xi, lines)[0]
 
 
 def local(query, key, value, text, cond_weight, cotangent, dest, segment, align):
@@ -450,11 +463,12 @@
     msg = msg3.reshape(PEERS * 8, LANES)
     packed, own = pack(msg, dest_row, text, query, key, value, cotangent)
     got = exchange(packed.reshape(PEERS, MSG_ROWS, LANES))
+    bias, pick = setup(zi, msg, own)
     my_w = msg3[:, 4 : 4 + HPD, :].astype(BF16).reshape(PEERS, COLS)
     full_w = gather_bits(my_w, "dp", (8, 4, 2, 1)).reshape(TEXT, COLS)
-    back, wg = attend(zi, msg, own, got, full_w)
+    back, wg = attend(zi, bias, pick, got, full_w)
     returned = exchange(back)
-    weight_grad = reduce_weight(wg, zi, xi)
+    weight_grad = reduce_weight(wg, xi)
     attended, query_grad, key_grad, value_grad, text_grad = unpack(
         msg, dest_row, returned.reshape(NZ, NX, MSG_ROWS, LANES)
     )

time: 179 us -> 216 us (1.21)
  the two profiles are of different devices: /device:TPU:40 before, /device:TPU:2 now
where the time goes in v5:
time: 216 us; the launch traced here: 215 us
  waiting for transfers between devices  95.5 us (44%)
  starting transfers between devices  58.5 us (27%)
  blocking collectives  33 us (15%)
  Pallas kernels  23.2 us (11%)
  local copies, waits for them, and re-layouts  2.48 us (1%)
    all_to_all x2, waiting for transfers between devices, exchange(): return lax.all_to_all(x, 'seq', split_axis=0, concat_axis=0, tiled=True)  75.8 us
    ppermute x11, starting transfers between devices, swap(): return lax.ppermute(x, axis, [(j, j ^ bit) for j in range(size)])  45.9 us
    all_to_all x1, blocking collectives, exchange(): return lax.all_to_all(x, 'seq', split_axis=0, concat_axis=0, tiled=True)  22.4 us
    ppermute x11, waiting for transfers between devices, swap(): return lax.ppermute(x, axis, [(j, j ^ bit) for j in range(size)])  19.7 us
    all_to_all x2, starting transfers between devices, exchange(): return lax.all_to_all(x, 'seq', split_axis=0, concat_axis=0, tiled=True)  12.5 us
    pallas_call x1, Pallas kernels, attend(): pl.pallas_call(attend_kernel, grid_spec=pltpu.PrefetchScalarGridSpec(num_...  10.7 us
    all_to_all x1, blocking collectives, reduce_weight(): lax.all_to_all(lines, 'seq', 0, 0, axis_index_groups=groups, tiled=True)  10.6 us
    pallas_call x1, Pallas kernels, pack(): pl.pallas_call(pack_kernel, grid=(NX,), in_specs=[full((PEERS * 8, LANES)...  4.97 us
  transfers between devices with their start and end apart: 13, of which 11 were waited for; matrix products, arithmetic and copies ran while one was open for 1% of the time, Pallas kernels for 1%

profile of v5, /device:TPU:2, one launch (start us, length us, event | category | flops | bytes accessed | tf_op | source)
XLA Modules:
  0.0 215.0 jit_solution(16382829715194856141)
XLA Ops:
  0.6 1.4 prep.1
  2.0 22.4 %all_to_all.20 = f32[32,8,128]{2,1,0:T(8,128)} all-to-all(f32[32,8,128]{2,1,0:T(8,128)} %bitcast.59), channel_id=1, replica_groups=mesh['dp'=16,'seq'=32] {'seq'}, dimensions={0} | all-to-all | bytes 262144 | tf_op jit(solution)/shard_map/all_to_all | solution.py:381
  24.5 5.0 %pack.1 = (bf16[8,4,288,128]{3,2,1,0:T(8,128)(2,1)}, f32[24,128]{1,0:T(8,128)}) custom-call(f32[256,128]{1,0:T(8,128)} %bitcast.50, s32[1,128]{1,0:T(1,128)} %bitcast.55, bf16[8,512]{1,0:T(8,128)(2,1)} %text_ref.1, bf16[128,1536]{1,0:T(8,128)(2,1)} %q_ref.1, bf16[128,1536]{1,0:T(8,128)(2,1)} %k_ref.1, bf16[128,1536]{1,0:T(8,128)(2,1)} %v_ref.1, ...), custom_call_target="tpu_custom_call" | custom-call | tf_op jit(solution)/shard_map/pack/pallas_call | solution.py:142
  29.4 5.7 %all-to-all-start.1 = ((bf16[32,288,128]{2,1,0:T(8,128)(2,1)}), bf16[32,288,128]{2,1,0:T(8,128)(2,1)S(1)}, u32[]{:S(2)}, u32[]{:S(2)}) async-start(bf16[32,288,128]{2,1,0:T(8,128)(2,1)} %bitcast.57), calls=%async_computation.1 | async-start | bytes 4718592 | tf_op jit(solution)/shard_map/all_to_all | solution.py:381
  35.2 7.7 %collective-permute-start = (bf16[32,384]{1,0:T(8,128)(2,1)S(1)}, bf16[32,384]{1,0:T(8,128)(2,1)S(1)}, u32[]{:S(2)}, u32[]{:S(2)}) collective-permute-start(bf16[32,384]{1,0:T(8,128)(2,1)S(1)} %bitcast.62), channel_id=1, source_target_pairs={{0,256},{32,288},{64,320},{96,352},{128,384},{160,416},{192,448},{... | collective-permute-start | bytes 73736 | tf_op jit(solution)/shard_map/ppermute | solution.py:386
  42.9 1.9 collective-permute-done
  44.9 4.5 %collective-permute-start.1 = (bf16[2,32,384]{2,1,0:T(8,128)(2,1)S(1)}, bf16[2,32,384]{2,1,0:T(8,128)(2,1)S(1)}, u32[]{:S(2)}, u32[]{:S(2)}) collective-permute-start(bf16[2,32,384]{2,1,0:T(8,128)(2,1)S(1)} %pad_maximum_fusion.3), channel_id=1, source_target_pairs={{0,128},{32,160},{64,192},{96,224},{128,0},{160,32},{192,64},{224,... | collective-permute-start | bytes 147464 | tf_op jit(solution)/shard_map/ppermute | solution.py:386
  49.4 2.3 %collective-permute-done.1 = bf16[2,32,384]{2,1,0:T(8,128)(2,1)S(1)} collective-permute-done((bf16[2,32,384]{2,1,0:T(8,128)(2,1)S(1)}, bf16[2,32,384]{2,1,0:T(8,128)(2,1)S(1)}, u32[]{:S(2)}, u32[]{:S(2)}) %collective-permute-start.1) | collective-permute-done | bytes 49184 | tf_op jit(solution)/shard_map/ppermute | solution.py:386
  51.8 3.5 %collective-permute-start.2 = (bf16[2,2,32,384]{3,2,0,1:T(8,128)(2,1)S(1)}, bf16[2,2,32,384]{3,2,0,1:T(8,128)(2,1)S(1)}, u32[]{:S(2)}, u32[]{:S(2)}) collective-permute-start(bf16[2,2,32,384]{3,2,0,1:T(8,128)(2,1)S(1)} %pad_maximum_fusion.2), channel_id=1, source_target_pairs={{0,64},{32,96},{64,0},{96,32},{128,192},{160,224},{192,128},{224,1... | collective-permute-start | bytes 294920 | tf_op jit(solution)/shard_map/ppermute | solution.py:386
  55.3 3.0 %collective-permute-done.2 = bf16[2,2,32,384]{3,2,0,1:T(8,128)(2,1)S(1)} collective-permute-done((bf16[2,2,32,384]{3,2,0,1:T(8,128)(2,1)S(1)}, bf16[2,2,32,384]{3,2,0,1:T(8,128)(2,1)S(1)}, u32[]{:S(2)}, u32[]{:S(2)}) %collective-permute-start.2) | collective-permute-done | bytes 98336 | tf_op jit(solution)/shard_map/ppermute | solution.py:386
  58.4 1.9 collective-permute-start.3
  60.3 2.1 setup.1
  63.5 25.3 %all-to-all-done.1.in_ref.tail_ref = bf16[32,288,128]{2,1,0:T(8,128)(2,1)S(1)} async-done(((bf16[32,288,128]{2,1,0:T(8,128)(2,1)}), bf16[32,288,128]{2,1,0:T(8,128)(2,1)S(1)}, u32[]{:S(2)}, u32[]{:S(2)}) %all-to-all-start.1) | async-done | bytes 2359328 | tf_op jit(solution)/shard_map/all_to_all | solution.py:381
  88.9 1.2 copy-done.1
  90.1 10.7 %attend.1 = (bf16[32,288,128]{2,1,0:T(8,128)(2,1)}, f32[512,384]{1,0:T(8,128)}) custom-call(s32[1]{0:T(128)} %bitcast.5.z_ref, f32[4,256,256]{2,1,0:T(8,128)S(1)} %copy-done.1, bf16[4,256,256]{2,1,0:T(8,128)(2,1)S(1)} %copy-done.2, bf16[32,288,128]{2,1,0:T(8,128)(2,1)S(1)} %all-to-all-done.1.in_ref.tail_ref, ...), custom_call_target="tpu_custom_call" | custom-call | tf_op jit(solution)/shard_map/attend/pallas_call | solution.py:292
  100.8 1.2 fusion.4
  102.1 1.9 collective-permute-start.4
  104.0 1.4 collective-permute-done.4
  105.5 3.5 %collective-permute-start.5 = (bf16[2,2,32,384]{3,2,0,1:T(8,128)(2,1)S(1)}, bf16[2,2,32,384]{3,2,0,1:T(8,128)(2,1)S(1)}, u32[]{:S(2)}, u32[]{:S(2)}) collective-permute-start(bf16[2,2,32,384]{3,2,0,1:T(8,128)(2,1)S(1)} %fusion.1), channel_id=1, source_target_pairs={{0,64},{32,96},{64,0},{96,32},{128,192},{160,224},{192,128},{224,1... | collective-permute-start | bytes 294920 | tf_op jit(solution)/shard_map/ppermute | solution.py:386
  109.0 3.2 %collective-permute-done.5 = bf16[2,2,32,384]{3,2,0,1:T(8,128)(2,1)S(1)} collective-permute-done((bf16[2,2,32,384]{3,2,0,1:T(8,128)(2,1)S(1)}, bf16[2,2,32,384]{3,2,0,1:T(8,128)(2,1)S(1)}, u32[]{:S(2)}, u32[]{:S(2)}) %collective-permute-start.5) | collective-permute-done | bytes 98336 | tf_op jit(solution)/shard_map/ppermute | solution.py:386
  112.3 4.5 %collective-permute-start.6 = (bf16[2,32,384]{2,1,0:T(8,128)(2,1)S(1)}, bf16[2,32,384]{2,1,0:T(8,128)(2,1)S(1)}, u32[]{:S(2)}, u32[]{:S(2)}) collective-permute-start(bf16[2,32,384]{2,1,0:T(8,128)(2,1)S(1)} %fusion.2), channel_id=1, source_target_pairs={{0,128},{32,160},{64,192},{96,224},{128,0},{160,32},{192,64},{224,... | collective-permute-start | bytes 147464 | tf_op jit(solution)/shard_map/ppermute | solution.py:386
  116.8 2.4 %collective-permute-done.6 = bf16[2,32,384]{2,1,0:T(8,128)(2,1)S(1)} collective-permute-done((bf16[2,32,384]{2,1,0:T(8,128)(2,1)S(1)}, bf16[2,32,384]{2,1,0:T(8,128)(2,1)S(1)}, u32[]{:S(2)}, u32[]{:S(2)}) %collective-permute-start.6) | collective-permute-done | bytes 49184 | tf_op jit(solution)/shard_map/ppermute | solution.py:386
  119.2 8.3 %collective-permute-start.7 = (bf16[32,384]{1,0:T(8,128)(2,1)S(1)}, bf16[32,384]{1,0:T(8,128)(2,1)S(1)}, u32[]{:S(2)}, u32[]{:S(2)}) collective-permute-start(bf16[32,384]{1,0:T(8,128)(2,1)S(1)} %fusion.3), channel_id=1, source_target_pairs={{0,256},{32,288},{64,320},{96,352},{128,384},{160,416},{192,448},{... | collective-permute-start | bytes 73736 | tf_op jit(solution)/shard_map/ppermute | solution.py:386
  127.5 1.9 collective-permute-done.7.got_ref
  129.4 3.9 %collective-permute-start.8 = (f32[8,384]{1,0:T(8,128)S(1)}, f32[8,384]{1,0:T(8,128)S(1)}, u32[]{:S(2)}, u32[]{:S(2)}) collective-permute-start(f32[8,384]{1,0:T(8,128)S(1)} %get-tuple-element.33), channel_id=1, source_target_pairs={{0,1},{1,0},{2,3},{3,2},{4,5},{5,4},{6,7},{7,6},{8,9},{9,8},{10,11... | collective-permute-start | bytes 36872 | tf_op jit(solution)/shard_map/ppermute | solution.py:386
  133.3 4.3 %collective-permute-start.9 = (f32[8,384]{1,0:T(8,128)S(1)}, f32[8,384]{1,0:T(8,128)S(1)}, u32[]{:S(2)}, u32[]{:S(2)}) collective-permute-start(f32[8,384]{1,0:T(8,128)S(1)} %get-tuple-element.34), channel_id=1, source_target_pairs={{0,2},{1,3},{2,0},{3,1},{4,6},{5,7},{6,4},{7,5},{8,10},{9,11},{10,... | collective-permute-start | bytes 36872 | tf_op jit(solution)/shard_map/ppermute | solution.py:386
  137.6 1.9 collective-permute-start.10
  140.4 2.8 %collective-permute-done.10.refs_3_ = f32[8,384]{1,0:T(8,128)S(1)} collective-permute-done((f32[8,384]{1,0:T(8,128)S(1)}, f32[8,384]{1,0:T(8,128)S(1)}, u32[]{:S(2)}, u32[]{:S(2)}) %collective-permute-start.10) | collective-permute-done | bytes 12320 | tf_op jit(solution)/shard_map/ppermute | solution.py:386
  143.2 10.6 %all_to_all.21.in_ref = f32[8,4,384]{2,1,0:T(4,128)S(1)} all-to-all(f32[8,4,384]{2,1,0:T(4,128)S(1)} %shard_map.137), channel_id=1, replica_groups={{0,4,8,12,16,20,24,28},{1,5,9,13,17,21,25,29},{2,6,10,14,18,22,26,30},{..., dimensions={0} | all-to-all | bytes 98304 | tf_op jit(solution)/shard_map/all_to_all | solution.py:451
  153.8 6.8 %all-to-all-start.2 = ((bf16[32,288,128]{2,1,0:T(8,128)(2,1)}), bf16[32,288,128]{2,1,0:T(8,128)(2,1)S(1)}, u32[]{:S(2)}, u32[]{:S(2)}) async-start(bf16[32,288,128]{2,1,0:T(8,128)(2,1)} %get-tuple-element.25), calls=%async_computation.2 | async-start | bytes 4718592 | tf_op jit(solution)/shard_map/all_to_all | solution.py:381
  161.2 50.4 %all-to-all-done.2 = bf16[32,288,128]{2,1,0:T(8,128)(2,1)S(1)} async-done(((bf16[32,288,128]{2,1,0:T(8,128)(2,1)}), bf16[32,288,128]{2,1,0:T(8,128)(2,1)S(1)}, u32[]{:S(2)}, u32[]{:S(2)}) %all-to-all-start.2) | async-done | bytes 2359328 | tf_op jit(solution)/shard_map/all_to_all | solution.py:381
  211.6 3.3 %unpack.1 = (bf16[128,1536]{1,0:T(8,128)(2,1)}, bf16[128,1536]{1,0:T(8,128)(2,1)}, bf16[128,1536]{1,0:T(8,128)(2,1)}, bf16[128,1536]{1,0:T(8,128)(2,1)}, f32[8,512]{1,0:T(8,128)}) custom-call(f32[256,128]{1,0:T(8,128)S(1)} %bitcast.52, s32[1,128]{1,0:T(1,128)S(1)} %bitcast.56, bf16[8,4,288,128]{3,2,1,0:T(8,128)(2,1)S(1)} %bitcast.49), custom_call_target="tpu_custom_call" | custom-call | tf_op jit(solution)/shard_map/unpack/pallas_call | solution.py:364
  (34 shorter events, 3.0 us)
Async XLA Ops:
  29.4 5.7 %copy-start = (f32[32,8,128]{2,1,0:T(8,128)S(1)}, f32[32,8,128]{2,1,0:T(8,128)}, u32[]{:S(2)}) copy-start(f32[32,8,128]{2,1,0:T(8,128)} %all_to_all.20) | copy-start | bytes 393220
  29.4 30.9 %copy-start.3 = (f32[24,128]{1,0:T(8,128)S(1)}, f32[24,128]{1,0:T(8,128)}, u32[]{:S(2)}) copy-start(f32[24,128]{1,0:T(8,128)} %get-tuple-element.21.own_ref) | copy-start | bytes 36868
  29.4 59.4 %all-to-all-start.1 = ((bf16[32,288,128]{2,1,0:T(8,128)(2,1)}), bf16[32,288,128]{2,1,0:T(8,128)(2,1)S(1)}, u32[]{:S(2)}, u32[]{:S(2)}) async-start(bf16[32,288,128]{2,1,0:T(8,128)(2,1)} %bitcast.57), calls=%async_computation.1 | async-start | bytes 4718592 | tf_op jit(solution)/shard_map/all_to_all | solution.py:381
  35.2 9.6 %collective-permute-start = (bf16[32,384]{1,0:T(8,128)(2,1)S(1)}, bf16[32,384]{1,0:T(8,128)(2,1)S(1)}, u32[]{:S(2)}, u32[]{:S(2)}) collective-permute-start(bf16[32,384]{1,0:T(8,128)(2,1)S(1)} %bitcast.62), channel_id=1, source_target_pairs={{0,256},{32,288},{64,320},{96,352},{128,384},{160,416},{192,448},{... | collective-permute-start | bytes 73736 | tf_op jit(solution)/shard_map/ppermute | solution.py:386
  44.9 6.9 %collective-permute-start.1 = (bf16[2,32,384]{2,1,0:T(8,128)(2,1)S(1)}, bf16[2,32,384]{2,1,0:T(8,128)(2,1)S(1)}, u32[]{:S(2)}, u32[]{:S(2)}) collective-permute-start(bf16[2,32,384]{2,1,0:T(8,128)(2,1)S(1)} %pad_maximum_fusion.3), channel_id=1, source_target_pairs={{0,128},{32,160},{64,192},{96,224},{128,0},{160,32},{192,64},{224,... | collective-permute-start | bytes 147464 | tf_op jit(solution)/shard_map/ppermute | solution.py:386
  51.8 6.5 %collective-permute-start.2 = (bf16[2,2,32,384]{3,2,0,1:T(8,128)(2,1)S(1)}, bf16[2,2,32,384]{3,2,0,1:T(8,128)(2,1)S(1)}, u32[]{:S(2)}, u32[]{:S(2)}) collective-permute-start(bf16[2,2,32,384]{3,2,0,1:T(8,128)(2,1)S(1)} %pad_maximum_fusion.2), channel_id=1, source_target_pairs={{0,64},{32,96},{64,0},{96,32},{128,192},{160,224},{192,128},{224,1... | collective-permute-start | bytes 294920 | tf_op jit(solution)/shard_map/ppermute | solution.py:386
  58.4 4.0 %collective-permute-start.3 = (bf16[2,2,2,32,384]{4,3,0,1,2:T(8,128)(2,1)S(1)}, bf16[2,2,2,32,384]{4,3,0,1,2:T(8,128)(2,1)}, u32[]{:S(2)}, u32[]{:S(2)}) collective-permute-start(bf16[2,2,2,32,384]{4,3,0,1,2:T(8,128)(2,1)S(1)} %pad_maximum_fusion.1), channel_id=1, source_target_pairs={{0,32},{32,0},{64,96},{96,64},{128,160},{160,128},{192,224},{224,1... | collective-permute-start | bytes 589832 | tf_op jit(solution)/shard_map/ppermute | solution.py:386
  62.4 26.5 %copy-start.2 = (bf16[4,256,256]{2,1,0:T(8,128)(2,1)S(1)}, bf16[4,256,256]{2,1,0:T(8,128)(2,1)}, u32[]{:S(2)}) copy-start(bf16[4,256,256]{2,1,0:T(8,128)(2,1)} %get-tuple-element.23.pick_ref) | copy-start | bytes 1572868
  88.9 1.2 copy-start.1
  102.1 3.3 %collective-permute-start.4 = (bf16[2,2,2,32,384]{4,3,0,1,2:T(8,128)(2,1)S(1)}, bf16[2,2,2,32,384]{4,3,0,1,2:T(8,128)(2,1)S(1)}, u32[]{:S(2)}, u32[]{:S(2)}) collective-permute-start(bf16[2,2,2,32,384]{4,3,0,1,2:T(8,128)(2,1)S(1)} %fusion), channel_id=1, source_target_pairs={{0,32},{32,0},{64,96},{96,64},{128,160},{160,128},{192,224},{224,1... | collective-permute-start | bytes 589832 | tf_op jit(solution)/shard_map/ppermute | solution.py:386
  105.5 6.7 %collective-permute-start.5 = (bf16[2,2,32,384]{3,2,0,1:T(8,128)(2,1)S(1)}, bf16[2,2,32,384]{3,2,0,1:T(8,128)(2,1)S(1)}, u32[]{:S(2)}, u32[]{:S(2)}) collective-permute-start(bf16[2,2,32,384]{3,2,0,1:T(8,128)(2,1)S(1)} %fusion.1), channel_id=1, source_target_pairs={{0,64},{32,96},{64,0},{96,32},{128,192},{160,224},{192,128},{224,1... | collective-permute-start | bytes 294920 | tf_op jit(solution)/shard_map/ppermute | solution.py:386
  112.3 6.9 %collective-permute-start.6 = (bf16[2,32,384]{2,1,0:T(8,128)(2,1)S(1)}, bf16[2,32,384]{2,1,0:T(8,128)(2,1)S(1)}, u32[]{:S(2)}, u32[]{:S(2)}) collective-permute-start(bf16[2,32,384]{2,1,0:T(8,128)(2,1)S(1)} %fusion.2), channel_id=1, source_target_pairs={{0,128},{32,160},{64,192},{96,224},{128,0},{160,32},{192,64},{224,... | collective-permute-start | bytes 147464 | tf_op jit(solution)/shard_map/ppermute | solution.py:386
  119.2 10.2 %collective-permute-start.7 = (bf16[32,384]{1,0:T(8,128)(2,1)S(1)}, bf16[32,384]{1,0:T(8,128)(2,1)S(1)}, u32[]{:S(2)}, u32[]{:S(2)}) collective-permute-start(bf16[32,384]{1,0:T(8,128)(2,1)S(1)} %fusion.3), channel_id=1, source_target_pairs={{0,256},{32,288},{64,320},{96,352},{128,384},{160,416},{192,448},{... | collective-permute-start | bytes 73736 | tf_op jit(solution)/shard_map/ppermute | solution.py:386
  129.4 10.1 %collective-permute-start.8 = (f32[8,384]{1,0:T(8,128)S(1)}, f32[8,384]{1,0:T(8,128)S(1)}, u32[]{:S(2)}, u32[]{:S(2)}) collective-permute-start(f32[8,384]{1,0:T(8,128)S(1)} %get-tuple-element.33), channel_id=1, source_target_pairs={{0,1},{1,0},{2,3},{3,2},{4,5},{5,4},{6,7},{7,6},{8,9},{9,8},{10,11... | collective-permute-start | bytes 36872 | tf_op jit(solution)/shard_map/ppermute | solution.py:386
  133.3 7.1 %collective-permute-start.9 = (f32[8,384]{1,0:T(8,128)S(1)}, f32[8,384]{1,0:T(8,128)S(1)}, u32[]{:S(2)}, u32[]{:S(2)}) collective-permute-start(f32[8,384]{1,0:T(8,128)S(1)} %get-tuple-element.34), channel_id=1, source_target_pairs={{0,2},{1,3},{2,0},{3,1},{4,6},{5,7},{6,4},{7,5},{8,10},{9,11},{10,... | collective-permute-start | bytes 36872 | tf_op jit(solution)/shard_map/ppermute | solution.py:386
  137.6 5.6 %collective-permute-start.10 = (f32[8,384]{1,0:T(8,128)S(1)}, f32[8,384]{1,0:T(8,128)S(1)}, u32[]{:S(2)}, u32[]{:S(2)}) collective-permute-start(f32[8,384]{1,0:T(8,128)S(1)} %get-tuple-element.35), channel_id=1, source_target_pairs={{0,3},{1,2},{2,1},{3,0},{4,7},{5,6},{6,5},{7,4},{8,11},{9,10},{10,... | collective-permute-start | bytes 36872 | tf_op jit(solution)/shard_map/ppermute | solution.py:386
  153.8 57.9 %copy-start.4 = (s32[128]{0:T(128)S(1)}, s32[128]{0:T(128)}, u32[]{:S(2)}) copy-start(s32[128]{0:T(128)} %param.15) | copy-start | bytes 1540
  153.8 57.9 %all-to-all-start.2 = ((bf16[32,288,128]{2,1,0:T(8,128)(2,1)}), bf16[32,288,128]{2,1,0:T(8,128)(2,1)S(1)}, u32[]{:S(2)}, u32[]{:S(2)}) async-start(bf16[32,288,128]{2,1,0:T(8,128)(2,1)} %get-tuple-element.25), calls=%async_computation.2 | async-start | bytes 4718592 | tf_op jit(solution)/shard_map/all_to_all | solution.py:381

commit v6 on v5

--- a/solution.py
+++ b/solution.py
@@ -26,7 +26,7 @@
 TEXT_ROWS = 32
 BODY_ROWS = UNITS * BLOCK
 MSG_ROWS = BODY_ROWS + TEXT_ROWS
-STEP = 2
+STEP = 4
 
 
 def iota(shape, dim):
@@ -204,7 +204,8 @@
 
 
 def attend_kernel(
-    z_ref, bias_ref, pick_ref, in_ref, tail_ref, w_ref, out_ref, wg_ref, acc_ref, text_ref, w3_ref, cond_ref
+    z_ref, mask_ref, pick_ref, in_ref, tail_ref, w_ref, out_ref, wg_ref,
+    acc_ref, text_ref, w3_ref, cond_ref, bias_ref, bias_sem,
 ):
     i = pl.program_id(0)
     n = SLOTS
@@ -213,6 +214,8 @@
 
     @pl.when(i == 0)
     def _():
+        copy = pltpu.make_async_copy(mask_ref, bias_ref, bias_sem)
+        copy.start()
         for c in range(2):
             tiles = tail_ref[:, c * 2 * BUCKET : (c + 1) * 2 * BUCKET, :].astype(F32)
             tiles = tiles.reshape(PEERS, 2, BUCKET, LANES)
@@ -225,57 +228,67 @@
         for h in range(HPD):
             w3_ref[h] = w_ref[:, h * LANES : (h + 1) * LANES]
         acc_ref[...] = jnp.zeros_like(acc_ref)
+        copy.wait()
 
     scale = LANES ** (-0.5)
 
     @pl.when(i < UNITS // STEP)
     def _():
-        for u in range(STEP):
+        units = range(STEP)
+        heads, owners = [], []
+        for u in units:
             unit = unit0 + i * STEP + u
             owner = unit // HPD
-            h = unit - owner * HPD
-            t = owner - owner0
-
-            def pair_of(pair):
-                off = u * BLOCK + pair * 2 * BUCKET
-                both = in_ref[:, off : off + 2 * BUCKET, :].astype(F32).reshape(PEERS, 2, BUCKET, LANES)
-                return both[:, 0].reshape(n, LANES), both[:, 1].reshape(n, LANES)
-
-            def put(pair, a, b):
-                off = u * BLOCK + pair * 2 * BUCKET
-                out_ref[:, off : off + 2 * BUCKET, :] = jnp.concatenate(
-                    [a.reshape(PEERS, BUCKET, LANES), b.reshape(PEERS, BUCKET, LANES)], axis=1
-                ).astype(BF16)
-
-            q, k = pair_of(0)
-            v, g = pair_of(1)
-            q, k, g = q.astype(BF16), k.astype(BF16), g.astype(BF16)
-            v = (v + dot(cond_ref[t], w3_ref[h])).astype(BF16)
-            s = dot_nt(q, k) * scale + bias_ref[t]
+            heads.append(unit - owner * HPD)
+            owners.append(owner - owner0)
+
+        def pair_of(u, pair):
+            off = u * BLOCK + pair * 2 * BUCKET
+            both = in_ref[:, off : off + 2 * BUCKET, :].astype(F32).reshape(PEERS, 2, BUCKET, LANES)
+            return both[:, 0].reshape(n, LANES), both[:, 1].reshape(n, LANES)
+
+        def put(u, pair, a, b):
+            off = u * BLOCK + pair * 2 * BUCKET
+            out_ref[:, off : off + 2 * BUCKET, :] = jnp.concatenate(
+                [a.reshape(PEERS, BUCKET, LANES), b.reshape(PEERS, BUCKET, LANES)], axis=1
+            ).astype(BF16)
+
+        qk = [[x.astype(BF16) for x in pair_of(u, 0)] for u in units]
+        scores = [dot_nt(q, k) for q, k in qk]
+        vg = []
+        for u in units:
+            v, g = pair_of(u, 1)
+            extra = dot(cond_ref[owners[u]], w3_ref[heads[u]])
+            vg.append(((v + extra).astype(BF16), g.astype(BF16)))
+        prob_grads = [dot_nt(g, v) for v, g in vg]
+        probs = []
+        for u in units:
+            s = scores[u] * scale + bias_ref[owners[u]]
             e = jnp.exp(s - jnp.max(s, axis=1, keepdims=True))
-            p = e * (1.0 / jnp.sum(e, axis=1, keepdims=True))
-            w = p.astype(BF16)
-            out = dot(w, v)
-            value_grad = dot_tn(w, g)
-            pg = dot_nt(g, v)
+            probs.append(e * (1.0 / jnp.sum(e, axis=1, keepdims=True)))
+        weights = [p.astype(BF16) for p in probs]
+        score_grads = []
+        for p, pg in zip(probs, prob_grads):
             centre = jnp.sum(p * pg, axis=1, keepdims=True)
-            sg = (p * (pg - centre)).astype(BF16)
-            query_grad = dot(sg, k) * scale
-            key_grad = dot_tn(sg, q) * scale
-            put(0, out, query_grad)
-            put(1, key_grad, value_grad)
-            acc_ref[h] += dot_tn(pick_ref[t], value_grad.astype(BF16))
+            score_grads.append((p * (pg - centre)).astype(BF16))
+        for u in units:
+            (q, k), (v, g) = qk[u], vg[u]
+            out = dot(weights[u], v)
+            value_grad = dot_tn(weights[u], g)
+            query_grad = dot(score_grads[u], k) * scale
+            key_grad = dot_tn(score_grads[u], q) * scale
+            put(u, 0, out, query_grad)
+            put(u, 1, key_grad, value_grad)
+            acc_ref[heads[u]] += dot_tn(pick_ref[owners[u]], value_grad.astype(BF16))
 
     @pl.when(i == UNITS // STEP)
     def _():
         text = text_ref[...]
         tg = jnp.zeros((GTEXT, TEXT), F32)
         for h in range(HPD):
-            acc = acc_ref[h]
-            high = acc.astype(BF16)
-            low = (acc - high.astype(F32)).astype(BF16)
-            tg = tg + dot_nt(high, w3_ref[h]) + dot_nt(low, w3_ref[h])
-            wg_ref[:, h * LANES : (h + 1) * LANES] = dot_tn(text, high) + dot_tn(text, low)
+            acc = acc_ref[h].astype(BF16)
+            tg = tg + dot_nt(acc, w3_ref[h])
+            wg_ref[:, h * LANES : (h + 1) * LANES] = dot_tn(text, acc)
         tg = tg.reshape(PEERS, BUCKET, TEXT)
         for c in range(2):
             both = jnp.concatenate(
@@ -295,7 +308,7 @@
             num_scalar_prefetch=1,
             grid=(UNITS // STEP + 1,),
             in_specs=[
-                full((NEAR, SLOTS, SLOTS)),
+                pl.BlockSpec(memory_space=pltpu.HBM),
                 full((NEAR, SLOTS, GTEXT)),
                 pl.BlockSpec((PEERS, STEP * BLOCK, LANES), lambda i, z: (0, jnp.minimum(i, last), 0)),
                 pl.BlockSpec((PEERS, TEXT_ROWS, LANES), lambda i, z: (0, BODY_ROWS // TEXT_ROWS, 0)),
@@ -307,6 +320,8 @@
                 pltpu.VMEM((GTEXT, TEXT), BF16),
                 pltpu.VMEM((HPD, TEXT, LANES), BF16),
                 pltpu.VMEM((NEAR, SLOTS, TEXT), BF16),
+                pltpu.VMEM((NEAR, SLOTS, SLOTS), F32),
+                pltpu.SemaphoreType.DMA,
             ],
         ),
         out_shape=[
@@ -315,7 +330,7 @@
         ],
         compiler_params=pltpu.CompilerParams(vmem_limit_bytes=28 << 20),
         name="attend",
-    )(zi, bias, pick, got, got, w)
+    )(zi, pltpu.with_memory_space_constraint(bias, pltpu.HBM), pick, got, got, w)
 
 
 def unpack_kernel(msg_ref, dest_ref, in_ref, o_ref, q_ref, k_ref, v_ref, tg_ref, sel_ref):

time: 216 us -> 211 us (0.977)
  Pallas kernels: 23.2 us -> 19.9 us
    pallas_call x1, Pallas kernels: 10.7 us -> 7.3 us  [attend(): pl.pallas_call(attend_kernel, grid_spec=pltpu.PrefetchScalarGridSpec(num_...]
where the time goes in v6:
time: 211 us; the launch traced here: 210 us
  waiting for transfers between devices  95.5 us (45%)
  starting transfers between devices  58.5 us (28%)
  blocking collectives  33 us (16%)
  Pallas kernels  19.9 us (9%)
    all_to_all x2, waiting for transfers between devices, exchange(): return lax.all_to_all(x, 'seq', split_axis=0, concat_axis=0, tiled=True)  75.7 us
    ppermute x11, starting transfers between devices, swap(): return lax.ppermute(x, axis, [(j, j ^ bit) for j in range(size)])  45.9 us
    all_to_all x1, blocking collectives, exchange(): return lax.all_to_all(x, 'seq', split_axis=0, concat_axis=0, tiled=True)  22.4 us
    ppermute x11, waiting for transfers between devices, swap(): return lax.ppermute(x, axis, [(j, j ^ bit) for j in range(size)])  19.7 us
    all_to_all x2, starting transfers between devices, exchange(): return lax.all_to_all(x, 'seq', split_axis=0, concat_axis=0, tiled=True)  12.5 us
    all_to_all x1, blocking collectives, reduce_weight(): lax.all_to_all(lines, 'seq', 0, 0, axis_index_groups=groups, tiled=True)  10.6 us
    pallas_call x1, Pallas kernels, attend(): pl.pallas_call(attend_kernel, grid_spec=pltpu.PrefetchScalarGridSpec(num_...  7.3 us
    pallas_call x1, Pallas kernels, pack(): pl.pallas_call(pack_kernel, grid=(NX,), in_specs=[full((PEERS * 8, LANES)...  5.05 us
  transfers between devices with their start and end apart: 13, of which 11 were waited for; matrix products, arithmetic and copies ran while one was open for 1% of the time, Pallas kernels for 1%

profile of v6, /device:TPU:2, one launch (start us, length us, event | category | flops | bytes accessed | tf_op | source)
XLA Modules:
  0.0 210.4 jit_solution(3747825450712640866)
XLA Ops:
  0.6 1.4 prep.1
  2.0 22.4 %all_to_all.20 = f32[32,8,128]{2,1,0:T(8,128)} all-to-all(f32[32,8,128]{2,1,0:T(8,128)} %bitcast.59), channel_id=1, replica_groups=mesh['dp'=16,'seq'=32] {'seq'}, dimensions={0} | all-to-all | bytes 262144 | tf_op jit(solution)/shard_map/all_to_all | solution.py:396
  24.5 5.0 %pack.1 = (bf16[8,4,288,128]{3,2,1,0:T(8,128)(2,1)}, f32[24,128]{1,0:T(8,128)}) custom-call(f32[256,128]{1,0:T(8,128)} %bitcast.50, s32[1,128]{1,0:T(1,128)} %bitcast.55, bf16[8,512]{1,0:T(8,128)(2,1)} %text_ref.1, bf16[128,1536]{1,0:T(8,128)(2,1)} %q_ref.1, bf16[128,1536]{1,0:T(8,128)(2,1)} %k_ref.1, bf16[128,1536]{1,0:T(8,128)(2,1)} %v_ref.1, ...), custom_call_target="tpu_custom_call" | custom-call | tf_op jit(solution)/shard_map/pack/pallas_call | solution.py:142
  29.5 5.7 %all-to-all-start.1 = ((bf16[32,288,128]{2,1,0:T(8,128)(2,1)}), bf16[32,288,128]{2,1,0:T(8,128)(2,1)S(1)}, u32[]{:S(2)}, u32[]{:S(2)}) async-start(bf16[32,288,128]{2,1,0:T(8,128)(2,1)} %bitcast.57), calls=%async_computation.1 | async-start | bytes 4718592 | tf_op jit(solution)/shard_map/all_to_all | solution.py:396
  35.3 7.7 %collective-permute-start = (bf16[32,384]{1,0:T(8,128)(2,1)S(1)}, bf16[32,384]{1,0:T(8,128)(2,1)S(1)}, u32[]{:S(2)}, u32[]{:S(2)}) collective-permute-start(bf16[32,384]{1,0:T(8,128)(2,1)S(1)} %bitcast.62), channel_id=1, source_target_pairs={{0,256},{32,288},{64,320},{96,352},{128,384},{160,416},{192,448},{... | collective-permute-start | bytes 73736 | tf_op jit(solution)/shard_map/ppermute | solution.py:401
  43.0 1.9 collective-permute-done
  44.9 4.5 %collective-permute-start.1 = (bf16[2,32,384]{2,1,0:T(8,128)(2,1)S(1)}, bf16[2,32,384]{2,1,0:T(8,128)(2,1)S(1)}, u32[]{:S(2)}, u32[]{:S(2)}) collective-permute-start(bf16[2,32,384]{2,1,0:T(8,128)(2,1)S(1)} %pad_maximum_fusion.3), channel_id=1, source_target_pairs={{0,128},{32,160},{64,192},{96,224},{128,0},{160,32},{192,64},{224,... | collective-permute-start | bytes 147464 | tf_op jit(solution)/shard_map/ppermute | solution.py:401
  49.5 2.3 %collective-permute-done.1 = bf16[2,32,384]{2,1,0:T(8,128)(2,1)S(1)} collective-permute-done((bf16[2,32,384]{2,1,0:T(8,128)(2,1)S(1)}, bf16[2,32,384]{2,1,0:T(8,128)(2,1)S(1)}, u32[]{:S(2)}, u32[]{:S(2)}) %collective-permute-start.1) | collective-permute-done | bytes 49184 | tf_op jit(solution)/shard_map/ppermute | solution.py:401
  51.9 3.5 %collective-permute-start.2 = (bf16[2,2,32,384]{3,2,0,1:T(8,128)(2,1)S(1)}, bf16[2,2,32,384]{3,2,0,1:T(8,128)(2,1)S(1)}, u32[]{:S(2)}, u32[]{:S(2)}) collective-permute-start(bf16[2,2,32,384]{3,2,0,1:T(8,128)(2,1)S(1)} %pad_maximum_fusion.2), channel_id=1, source_target_pairs={{0,64},{32,96},{64,0},{96,32},{128,192},{160,224},{192,128},{224,1... | collective-permute-start | bytes 294920 | tf_op jit(solution)/shard_map/ppermute | solution.py:401
  55.4 3.0 %collective-permute-done.2 = bf16[2,2,32,384]{3,2,0,1:T(8,128)(2,1)S(1)} collective-permute-done((bf16[2,2,32,384]{3,2,0,1:T(8,128)(2,1)S(1)}, bf16[2,2,32,384]{3,2,0,1:T(8,128)(2,1)S(1)}, u32[]{:S(2)}, u32[]{:S(2)}) %collective-permute-start.2) | collective-permute-done | bytes 98336 | tf_op jit(solution)/shard_map/ppermute | solution.py:401
  58.4 1.9 collective-permute-start.3
  60.4 2.1 setup.1
  62.5 1.0 select_bitcast_fusion.1
  63.6 25.3 %all-to-all-done.1.in_ref.tail_ref = bf16[32,288,128]{2,1,0:T(8,128)(2,1)S(1)} async-done(((bf16[32,288,128]{2,1,0:T(8,128)(2,1)}), bf16[32,288,128]{2,1,0:T(8,128)(2,1)S(1)}, u32[]{:S(2)}, u32[]{:S(2)}) %all-to-all-start.1) | async-done | bytes 2359328 | tf_op jit(solution)/shard_map/all_to_all | solution.py:396
  89.0 7.3 %attend.1 = (bf16[32,288,128]{2,1,0:T(8,128)(2,1)}, f32[512,384]{1,0:T(8,128)}) custom-call(s32[1]{0:T(128)} %bitcast.5.z_ref, f32[4,256,256]{2,1,0:T(8,128)} %get-tuple-element.22.mask_ref, bf16[4,256,256]{2,1,0:T(8,128)(2,1)S(1)} %copy-done.1, bf16[32,288,128]{2,1,0:T(8,128)(2,1)S(1)} %all-to-all-done.1.in_ref.tail_ref, ...), custom_call_target="tpu_custom_call" | custom-call | tf_op jit(solution)/shard_map/attend/pallas_call | solution.py:305
  96.3 1.2 fusion.4
  97.5 1.9 collective-permute-start.4
  99.4 1.4 collective-permute-done.4
  100.9 3.5 %collective-permute-start.5 = (bf16[2,2,32,384]{3,2,0,1:T(8,128)(2,1)S(1)}, bf16[2,2,32,384]{3,2,0,1:T(8,128)(2,1)S(1)}, u32[]{:S(2)}, u32[]{:S(2)}) collective-permute-start(bf16[2,2,32,384]{3,2,0,1:T(8,128)(2,1)S(1)} %fusion.1), channel_id=1, source_target_pairs={{0,64},{32,96},{64,0},{96,32},{128,192},{160,224},{192,128},{224,1... | collective-permute-start | bytes 294920 | tf_op jit(solution)/shard_map/ppermute | solution.py:401
  104.4 3.2 %collective-permute-done.5 = bf16[2,2,32,384]{3,2,0,1:T(8,128)(2,1)S(1)} collective-permute-done((bf16[2,2,32,384]{3,2,0,1:T(8,128)(2,1)S(1)}, bf16[2,2,32,384]{3,2,0,1:T(8,128)(2,1)S(1)}, u32[]{:S(2)}, u32[]{:S(2)}) %collective-permute-start.5) | collective-permute-done | bytes 98336 | tf_op jit(solution)/shard_map/ppermute | solution.py:401
  107.7 4.5 %collective-permute-start.6 = (bf16[2,32,384]{2,1,0:T(8,128)(2,1)S(1)}, bf16[2,32,384]{2,1,0:T(8,128)(2,1)S(1)}, u32[]{:S(2)}, u32[]{:S(2)}) collective-permute-start(bf16[2,32,384]{2,1,0:T(8,128)(2,1)S(1)} %fusion.2), channel_id=1, source_target_pairs={{0,128},{32,160},{64,192},{96,224},{128,0},{160,32},{192,64},{224,... | collective-permute-start | bytes 147464 | tf_op jit(solution)/shard_map/ppermute | solution.py:401
  112.2 2.4 %collective-permute-done.6 = bf16[2,32,384]{2,1,0:T(8,128)(2,1)S(1)} collective-permute-done((bf16[2,32,384]{2,1,0:T(8,128)(2,1)S(1)}, bf16[2,32,384]{2,1,0:T(8,128)(2,1)S(1)}, u32[]{:S(2)}, u32[]{:S(2)}) %collective-permute-start.6) | collective-permute-done | bytes 49184 | tf_op jit(solution)/shard_map/ppermute | solution.py:401
  114.6 8.3 %collective-permute-start.7 = (bf16[32,384]{1,0:T(8,128)(2,1)S(1)}, bf16[32,384]{1,0:T(8,128)(2,1)S(1)}, u32[]{:S(2)}, u32[]{:S(2)}) collective-permute-start(bf16[32,384]{1,0:T(8,128)(2,1)S(1)} %fusion.3), channel_id=1, source_target_pairs={{0,256},{32,288},{64,320},{96,352},{128,384},{160,416},{192,448},{... | collective-permute-start | bytes 73736 | tf_op jit(solution)/shard_map/ppermute | solution.py:401
  122.9 1.9 collective-permute-done.7.got_ref
  124.9 3.9 %collective-permute-start.8 = (f32[8,384]{1,0:T(8,128)S(1)}, f32[8,384]{1,0:T(8,128)S(1)}, u32[]{:S(2)}, u32[]{:S(2)}) collective-permute-start(f32[8,384]{1,0:T(8,128)S(1)} %get-tuple-element.33), channel_id=1, source_target_pairs={{0,1},{1,0},{2,3},{3,2},{4,5},{5,4},{6,7},{7,6},{8,9},{9,8},{10,11... | collective-permute-start | bytes 36872 | tf_op jit(solution)/shard_map/ppermute | solution.py:401
  128.7 4.3 %collective-permute-start.9 = (f32[8,384]{1,0:T(8,128)S(1)}, f32[8,384]{1,0:T(8,128)S(1)}, u32[]{:S(2)}, u32[]{:S(2)}) collective-permute-start(f32[8,384]{1,0:T(8,128)S(1)} %get-tuple-element.34), channel_id=1, source_target_pairs={{0,2},{1,3},{2,0},{3,1},{4,6},{5,7},{6,4},{7,5},{8,10},{9,11},{10,... | collective-permute-start | bytes 36872 | tf_op jit(solution)/shard_map/ppermute | solution.py:401
  133.0 1.9 collective-permute-start.10
  135.8 2.8 %collective-permute-done.10.refs_3_ = f32[8,384]{1,0:T(8,128)S(1)} collective-permute-done((f32[8,384]{1,0:T(8,128)S(1)}, f32[8,384]{1,0:T(8,128)S(1)}, u32[]{:S(2)}, u32[]{:S(2)}) %collective-permute-start.10) | collective-permute-done | bytes 12320 | tf_op jit(solution)/shard_map/ppermute | solution.py:401
  138.6 10.6 %all_to_all.21.in_ref = f32[8,4,384]{2,1,0:T(4,128)S(1)} all-to-all(f32[8,4,384]{2,1,0:T(4,128)S(1)} %shard_map.137), channel_id=1, replica_groups={{0,4,8,12,16,20,24,28},{1,5,9,13,17,21,25,29},{2,6,10,14,18,22,26,30},{..., dimensions={0} | all-to-all | bytes 98304 | tf_op jit(solution)/shard_map/all_to_all | solution.py:466
  149.2 6.8 %all-to-all-start.2 = ((bf16[32,288,128]{2,1,0:T(8,128)(2,1)}), bf16[32,288,128]{2,1,0:T(8,128)(2,1)S(1)}, u32[]{:S(2)}, u32[]{:S(2)}) async-start(bf16[32,288,128]{2,1,0:T(8,128)(2,1)} %get-tuple-element.25), calls=%async_computation.2 | async-start | bytes 4718592 | tf_op jit(solution)/shard_map/all_to_all | solution.py:396
  156.7 50.4 %all-to-all-done.2 = bf16[32,288,128]{2,1,0:T(8,128)(2,1)S(1)} async-done(((bf16[32,288,128]{2,1,0:T(8,128)(2,1)}), bf16[32,288,128]{2,1,0:T(8,128)(2,1)S(1)}, u32[]{:S(2)}, u32[]{:S(2)}) %all-to-all-start.2) | async-done | bytes 2359328 | tf_op jit(solution)/shard_map/all_to_all | solution.py:396
  207.1 3.3 %unpack.1 = (bf16[128,1536]{1,0:T(8,128)(2,1)}, bf16[128,1536]{1,0:T(8,128)(2,1)}, bf16[128,1536]{1,0:T(8,128)(2,1)}, bf16[128,1536]{1,0:T(8,128)(2,1)}, f32[8,512]{1,0:T(8,128)}) custom-call(f32[256,128]{1,0:T(8,128)S(1)} %bitcast.52, s32[1,128]{1,0:T(1,128)S(1)} %bitcast.56, bf16[8,4,288,128]{3,2,1,0:T(8,128)(2,1)S(1)} %bitcast.49), custom_call_target="tpu_custom_call" | custom-call | tf_op jit(solution)/shard_map/unpack/pallas_call | solution.py:379
  (32 shorter events, 2.0 us)
Async XLA Ops:
  29.5 5.7 %copy-start = (f32[32,8,128]{2,1,0:T(8,128)S(1)}, f32[32,8,128]{2,1,0:T(8,128)}, u32[]{:S(2)}) copy-start(f32[32,8,128]{2,1,0:T(8,128)} %all_to_all.20) | copy-start | bytes 393220
  29.5 30.9 %copy-start.2 = (f32[24,128]{1,0:T(8,128)S(1)}, f32[24,128]{1,0:T(8,128)}, u32[]{:S(2)}) copy-start(f32[24,128]{1,0:T(8,128)} %get-tuple-element.21.own_ref) | copy-start | bytes 36868
  29.5 59.4 %all-to-all-start.1 = ((bf16[32,288,128]{2,1,0:T(8,128)(2,1)}), bf16[32,288,128]{2,1,0:T(8,128)(2,1)S(1)}, u32[]{:S(2)}, u32[]{:S(2)}) async-start(bf16[32,288,128]{2,1,0:T(8,128)(2,1)} %bitcast.57), calls=%async_computation.1 | async-start | bytes 4718592 | tf_op jit(solution)/shard_map/all_to_all | solution.py:396
  35.3 9.6 %collective-permute-start = (bf16[32,384]{1,0:T(8,128)(2,1)S(1)}, bf16[32,384]{1,0:T(8,128)(2,1)S(1)}, u32[]{:S(2)}, u32[]{:S(2)}) collective-permute-start(bf16[32,384]{1,0:T(8,128)(2,1)S(1)} %bitcast.62), channel_id=1, source_target_pairs={{0,256},{32,288},{64,320},{96,352},{128,384},{160,416},{192,448},{... | collective-permute-start | bytes 73736 | tf_op jit(solution)/shard_map/ppermute | solution.py:401
  44.9 6.9 %collective-permute-start.1 = (bf16[2,32,384]{2,1,0:T(8,128)(2,1)S(1)}, bf16[2,32,384]{2,1,0:T(8,128)(2,1)S(1)}, u32[]{:S(2)}, u32[]{:S(2)}) collective-permute-start(bf16[2,32,384]{2,1,0:T(8,128)(2,1)S(1)} %pad_maximum_fusion.3), channel_id=1, source_target_pairs={{0,128},{32,160},{64,192},{96,224},{128,0},{160,32},{192,64},{224,... | collective-permute-start | bytes 147464 | tf_op jit(solution)/shard_map/ppermute | solution.py:401
  51.9 6.5 %collective-permute-start.2 = (bf16[2,2,32,384]{3,2,0,1:T(8,128)(2,1)S(1)}, bf16[2,2,32,384]{3,2,0,1:T(8,128)(2,1)S(1)}, u32[]{:S(2)}, u32[]{:S(2)}) collective-permute-start(bf16[2,2,32,384]{3,2,0,1:T(8,128)(2,1)S(1)} %pad_maximum_fusion.2), channel_id=1, source_target_pairs={{0,64},{32,96},{64,0},{96,32},{128,192},{160,224},{192,128},{224,1... | collective-permute-start | bytes 294920 | tf_op jit(solution)/shard_map/ppermute | solution.py:401
  58.4 4.0 %collective-permute-start.3 = (bf16[2,2,2,32,384]{4,3,0,1,2:T(8,128)(2,1)S(1)}, bf16[2,2,2,32,384]{4,3,0,1,2:T(8,128)(2,1)}, u32[]{:S(2)}, u32[]{:S(2)}) collective-permute-start(bf16[2,2,2,32,384]{4,3,0,1,2:T(8,128)(2,1)S(1)} %pad_maximum_fusion.1), channel_id=1, source_target_pairs={{0,32},{32,0},{64,96},{96,64},{128,160},{160,128},{192,224},{224,1... | collective-permute-start | bytes 589832 | tf_op jit(solution)/shard_map/ppermute | solution.py:401
  62.5 26.5 %copy-start.1 = (bf16[4,256,256]{2,1,0:T(8,128)(2,1)S(1)}, bf16[4,256,256]{2,1,0:T(8,128)(2,1)}, u32[]{:S(2)}) copy-start(bf16[4,256,256]{2,1,0:T(8,128)(2,1)} %get-tuple-element.23.pick_ref) | copy-start | bytes 1572868
  97.5 3.3 %collective-permute-start.4 = (bf16[2,2,2,32,384]{4,3,0,1,2:T(8,128)(2,1)S(1)}, bf16[2,2,2,32,384]{4,3,0,1,2:T(8,128)(2,1)S(1)}, u32[]{:S(2)}, u32[]{:S(2)}) collective-permute-start(bf16[2,2,2,32,384]{4,3,0,1,2:T(8,128)(2,1)S(1)} %fusion), channel_id=1, source_target_pairs={{0,32},{32,0},{64,96},{96,64},{128,160},{160,128},{192,224},{224,1... | collective-permute-start | bytes 589832 | tf_op jit(solution)/shard_map/ppermute | solution.py:401
  100.9 6.7 %collective-permute-start.5 = (bf16[2,2,32,384]{3,2,0,1:T(8,128)(2,1)S(1)}, bf16[2,2,32,384]{3,2,0,1:T(8,128)(2,1)S(1)}, u32[]{:S(2)}, u32[]{:S(2)}) collective-permute-start(bf16[2,2,32,384]{3,2,0,1:T(8,128)(2,1)S(1)} %fusion.1), channel_id=1, source_target_pairs={{0,64},{32,96},{64,0},{96,32},{128,192},{160,224},{192,128},{224,1... | collective-permute-start | bytes 294920 | tf_op jit(solution)/shard_map/ppermute | solution.py:401
  107.7 6.9 %collective-permute-start.6 = (bf16[2,32,384]{2,1,0:T(8,128)(2,1)S(1)}, bf16[2,32,384]{2,1,0:T(8,128)(2,1)S(1)}, u32[]{:S(2)}, u32[]{:S(2)}) collective-permute-start(bf16[2,32,384]{2,1,0:T(8,128)(2,1)S(1)} %fusion.2), channel_id=1, source_target_pairs={{0,128},{32,160},{64,192},{96,224},{128,0},{160,32},{192,64},{224,... | collective-permute-start | bytes 147464 | tf_op jit(solution)/shard_map/ppermute | solution.py:401
  114.6 10.2 %collective-permute-start.7 = (bf16[32,384]{1,0:T(8,128)(2,1)S(1)}, bf16[32,384]{1,0:T(8,128)(2,1)S(1)}, u32[]{:S(2)}, u32[]{:S(2)}) collective-permute-start(bf16[32,384]{1,0:T(8,128)(2,1)S(1)} %fusion.3), channel_id=1, source_target_pairs={{0,256},{32,288},{64,320},{96,352},{128,384},{160,416},{192,448},{... | collective-permute-start | bytes 73736 | tf_op jit(solution)/shard_map/ppermute | solution.py:401
  124.9 10.1 %collective-permute-start.8 = (f32[8,384]{1,0:T(8,128)S(1)}, f32[8,384]{1,0:T(8,128)S(1)}, u32[]{:S(2)}, u32[]{:S(2)}) collective-permute-start(f32[8,384]{1,0:T(8,128)S(1)} %get-tuple-element.33), channel_id=1, source_target_pairs={{0,1},{1,0},{2,3},{3,2},{4,5},{5,4},{6,7},{7,6},{8,9},{9,8},{10,11... | collective-permute-start | bytes 36872 | tf_op jit(solution)/shard_map/ppermute | solution.py:401
  128.7 7.1 %collective-permute-start.9 = (f32[8,384]{1,0:T(8,128)S(1)}, f32[8,384]{1,0:T(8,128)S(1)}, u32[]{:S(2)}, u32[]{:S(2)}) collective-permute-start(f32[8,384]{1,0:T(8,128)S(1)} %get-tuple-element.34), channel_id=1, source_target_pairs={{0,2},{1,3},{2,0},{3,1},{4,6},{5,7},{6,4},{7,5},{8,10},{9,11},{10,... | collective-permute-start | bytes 36872 | tf_op jit(solution)/shard_map/ppermute | solution.py:401
  133.0 5.6 %collective-permute-start.10 = (f32[8,384]{1,0:T(8,128)S(1)}, f32[8,384]{1,0:T(8,128)S(1)}, u32[]{:S(2)}, u32[]{:S(2)}) collective-permute-start(f32[8,384]{1,0:T(8,128)S(1)} %get-tuple-element.35), channel_id=1, source_target_pairs={{0,3},{1,2},{2,1},{3,0},{4,7},{5,6},{6,5},{7,4},{8,11},{9,10},{10,... | collective-permute-start | bytes 36872 | tf_op jit(solution)/shard_map/ppermute | solution.py:401
  149.2 57.9 %copy-start.3 = (s32[128]{0:T(128)S(1)}, s32[128]{0:T(128)}, u32[]{:S(2)}) copy-start(s32[128]{0:T(128)} %param.15) | copy-start | bytes 1540
  149.2 57.9 %all-to-all-start.2 = ((bf16[32,288,128]{2,1,0:T(8,128)(2,1)}), bf16[32,288,128]{2,1,0:T(8,128)(2,1)S(1)}, u32[]{:S(2)}, u32[]{:S(2)}) async-start(bf16[32,288,128]{2,1,0:T(8,128)(2,1)} %get-tuple-element.25), calls=%async_computation.2 | async-start | bytes 4718592 | tf_op jit(solution)/shard_map/all_to_all | solution.py:396

commit v7 on v6

--- a/solution.py
+++ b/solution.py
@@ -24,6 +24,7 @@
 GTEXT = 256
 BLOCK = 2 * 2 * BUCKET
 TEXT_ROWS = 32
+TGR = NZ * BUCKET
 BODY_ROWS = UNITS * BLOCK
 MSG_ROWS = BODY_ROWS + TEXT_ROWS
 STEP = 4
@@ -204,7 +205,7 @@
 
 
 def attend_kernel(
-    z_ref, mask_ref, pick_ref, in_ref, tail_ref, w_ref, out_ref, wg_ref,
+    z_ref, mask_ref, pick_ref, in_ref, tail_ref, w_ref, out_ref, wg_ref, tg_ref,
     acc_ref, text_ref, w3_ref, cond_ref, bias_ref, bias_sem,
 ):
     i = pl.program_id(0)
@@ -289,14 +290,9 @@
             acc = acc_ref[h].astype(BF16)
             tg = tg + dot_nt(acc, w3_ref[h])
             wg_ref[:, h * LANES : (h + 1) * LANES] = dot_tn(text, acc)
-        tg = tg.reshape(PEERS, BUCKET, TEXT)
-        for c in range(2):
-            both = jnp.concatenate(
-                [tg[:, :, 2 * c * LANES : (2 * c + 1) * LANES], tg[:, :, (2 * c + 1) * LANES : (2 * c + 2) * LANES]],
-                axis=1,
-            ).astype(BF16)
-            off = c * 2 * BUCKET
-            out_ref[:, off : off + 2 * BUCKET, :] = both
+        tg = tg.reshape(NZ, NX, BUCKET, TEXT)
+        for x in range(NX):
+            tg_ref[x] = tg[:, x].reshape(NZ * BUCKET, TEXT).astype(BF16)
 
 
 def attend(zi, bias, pick, got, w):
@@ -314,7 +310,11 @@
                 pl.BlockSpec((PEERS, TEXT_ROWS, LANES), lambda i, z: (0, BODY_ROWS // TEXT_ROWS, 0)),
                 full((TEXT, COLS)),
             ],
-            out_specs=[pl.BlockSpec((PEERS, STEP * BLOCK, LANES), lambda i, z: (0, i, 0)), full((TEXT, COLS))],
+            out_specs=[
+                pl.BlockSpec((PEERS, STEP * BLOCK, LANES), lambda i, z: (0, jnp.minimum(i, last), 0)),
+                full((TEXT, COLS)),
+                full((NX, NZ * BUCKET, TEXT)),
+            ],
             scratch_shapes=[
                 pltpu.VMEM((HPD, GTEXT, LANES), F32),
                 pltpu.VMEM((GTEXT, TEXT), BF16),
@@ -325,15 +325,16 @@
             ],
         ),
         out_shape=[
-            pltpu.HBM((PEERS, MSG_ROWS, LANES), BF16),
+            pltpu.HBM((PEERS, BODY_ROWS, LANES), BF16),
             pltpu.HBM((TEXT, COLS), F32),
+            pltpu.HBM((NX, NZ * BUCKET, TEXT), BF16),
         ],
         compiler_params=pltpu.CompilerParams(vmem_limit_bytes=28 << 20),
         name="attend",
     )(zi, pltpu.with_memory_space_constraint(bias, pltpu.HBM), pick, got, got, w)
 
 
-def unpack_kernel(msg_ref, dest_ref, in_ref, o_ref, q_ref, k_ref, v_ref, tg_ref, sel_ref):
+def unpack_kernel(msg_ref, dest_ref, in_ref, o_ref, q_ref, k_ref, v_ref, sel_ref):
     x = pl.program_id(0)
 
     @pl.when(x == 0)
@@ -356,21 +357,6 @@
             a_ref[:, span] = dot(sel, a).astype(BF16)
             b_ref[:, span] = dot(sel, b).astype(BF16)
 
-    for c in range(2):
-        off = BODY_ROWS + c * 2 * BUCKET
-        total = jnp.sum(in_ref[:, 0, off : off + 2 * BUCKET, :].astype(F32), axis=0)
-        for half in range(2):
-            span = slice((2 * c + half) * LANES, (2 * c + half + 1) * LANES)
-            piece = total[half * BUCKET : (half + 1) * BUCKET]
-
-            @pl.when(x == 0)
-            def _():
-                tg_ref[:, span] = piece
-
-            @pl.when(x > 0)
-            def _():
-                tg_ref[:, span] += piece
-
 
 def unpack(msg, dest, got):
     full = lambda shape: pl.BlockSpec(shape, lambda x: (0,) * len(shape))
@@ -382,10 +368,10 @@
         in_specs=[
             full((PEERS * 8, LANES)),
             full((1, LANES)),
-            pl.BlockSpec((NZ, 1, MSG_ROWS, LANES), lambda x: (0, x, 0, 0)),
+            pl.BlockSpec((NZ, 1, BODY_ROWS, LANES), lambda x: (0, x, 0, 0)),
         ],
-        out_specs=[cols, cols, cols, cols, full((BUCKET, TEXT))],
-        out_shape=[rows, rows, rows, rows, jax.ShapeDtypeStruct((BUCKET, TEXT), F32)],
+        out_specs=[cols, cols, cols, cols],
+        out_shape=[rows, rows, rows, rows],
         scratch_shapes=[pltpu.VMEM((ROWS, COMPACT * BUCKET), BF16)],
         compiler_params=pltpu.CompilerParams(vmem_limit_bytes=24 << 20),
         name="unpack",
@@ -418,28 +404,46 @@
     return jnp.where(up, one, zero), swap(jnp.where(up, zero, one).astype(kind), axis, bit)
 
 
-def x_split_kernel(x_ref, keep_ref, got_ref, *refs):
-    total_ref = refs[NX]
+def x_split_kernel(x_ref, keep_ref, got_ref, tg_ref, own_ref, mine_ref, *refs):
+    total_ref, piece_ref = refs[NX - 1 :]
     total_ref[...] = keep_ref[...] + got_ref[...].astype(F32)
-    for f, out_ref in enumerate(refs[:NX]):
+    for f in range(NX):
+        target = piece_ref if f else own_ref
         for j in range(NZ):
-            out_ref[pl.ds(j, 1), :] = total_ref[pl.ds(j * NX + (x_ref[0] ^ f), 1), :]
-
-
-def join_kernel(x_ref, *refs):
-    out_ref = refs[NX]
+            target[pl.ds(j, 1), :] = total_ref[pl.ds(j * NX + (x_ref[0] ^ f), 1), :]
+        if f == 0:
+            mine_ref[...] = tg_ref[x_ref[0]]
+        else:
+            send_ref = refs[f - 1]
+            send_ref[:TGR, :] = tg_ref[x_ref[0] ^ f]
+            rows = jnp.concatenate([piece_ref[...], jnp.zeros((NZ, COLS), F32)], axis=0)
+            send_ref[TGR:, :COLS] = rows.astype(BF16)
+            send_ref[TGR:, COLS:] = jnp.zeros((2 * NZ, TEXT - COLS), BF16)
+
+
+def join_kernel(x_ref, own_ref, mine_ref, *refs):
+    got_refs, (out_ref, weight_ref, row_ref) = refs[: NX - 1], refs[NX - 1 :]
+    total = mine_ref[...].astype(F32)
+    weight_ref[0] = own_ref[...]
+    for f, got_ref in enumerate(got_refs, 1):
+        total = total + got_ref[:TGR, :].astype(F32)
+        weight_ref[f] = got_ref[TGR:, :COLS].astype(F32)[:NZ]
+    total = total.reshape(NZ, BUCKET, TEXT)
+    row_ref[...] = jnp.zeros_like(row_ref)
     for z in range(NZ):
         for f in range(NX):
-            out_ref[z, pl.ds(f, 1), :] = refs[f][pl.ds(z, 1), :]
-
-
-def row_sum_kernel(x_ref, in_ref, out_ref, total_ref):
-    total = in_ref[0]
+            row_ref[z, f : f + 1, :COLS] = weight_ref[f, z : z + 1, :]
+        out_ref[z] = jnp.concatenate([total[z], row_ref[z]], axis=0).astype(BF16)
+
+
+def row_sum_kernel(x_ref, in_ref, out_ref, tg_ref, total_ref):
+    total = in_ref[0].astype(F32)
     for z in range(1, NZ):
-        total = total + in_ref[z]
-    total_ref[...] = total
+        total = total + in_ref[z].astype(F32)
+    tg_ref[...] = total[:BUCKET]
+    total_ref[...] = total[BUCKET:]
     for c in range(NX):
-        out_ref[:, c * COLS : (c + 1) * COLS] = total_ref[pl.ds(x_ref[0] ^ c, 1), :]
+        out_ref[:, c * COLS : (c + 1) * COLS] = total_ref[pl.ds(x_ref[0] ^ c, 1), :COLS]
 
 
 def small_call(kernel, outs, scratch, index, *args):
@@ -453,19 +457,21 @@
     )(index, *args)
 
 
-def reduce_weight(wg, xi):
+def reduce_text(wg, tg, xi):
     wg = wg.reshape(2, 2, 2, 2, PEERS, COLS)
     keep, got = halve(wg, "dp", 1, 3, BF16)
     for bit, dim in ((2, 2), (4, 1), (8, 0)):
         keep, got = halve(keep + got.astype(F32), "dp", bit, dim, BF16)
-    piece = ((NZ, COLS), F32)
-    parts = small_call(x_split_kernel, [piece] * NX, [pltpu.VMEM((PEERS, COLS), F32)], xi, keep, got)
-    parts = [parts[0]] + [swap(parts[f], "seq", f) for f in range(1, NX)]
-    lines = small_call(join_kernel, [((NZ, NX, COLS), F32)], [], xi, *parts)[0]
+    outs = [((NZ, COLS), F32), ((TGR, TEXT), BF16)] + [((TGR + 2 * NZ, TEXT), BF16)] * (NX - 1)
+    scratch = [pltpu.VMEM((PEERS, COLS), F32), pltpu.VMEM((NZ, COLS), F32)]
+    own, mine, *sends = small_call(x_split_kernel, outs, scratch, xi, keep, got, tg)
+    parts = [own, mine] + [swap(send, "seq", f) for f, send in enumerate(sends, 1)]
+    scratch = [pltpu.VMEM((NX, NZ, COLS), F32), pltpu.VMEM((NZ, BUCKET, TEXT), F32)]
+    lines = small_call(join_kernel, [((NZ, 2 * BUCKET, TEXT), BF16)], scratch, xi, *parts)[0]
     groups = [[z * NX + x for z in range(NZ)] for x in range(NX)]
     lines = lax.all_to_all(lines, "seq", 0, 0, axis_index_groups=groups, tiled=True)
-    row = [((1, NX * COLS), F32)]
-    return small_call(row_sum_kernel, row, [pltpu.VMEM((NX, COLS), F32)], xi, lines)[0]
+    outs = [((1, NX * COLS), F32), ((BUCKET, TEXT), F32)]
+    return small_call(row_sum_kernel, outs, [pltpu.VMEM((BUCKET, TEXT), F32)], xi, lines)
 
 
 def local(query, key, value, text, cond_weight, cotangent, dest, segment, align):
@@ -481,11 +487,11 @@
     bias, pick = setup(zi, msg, own)
     my_w = msg3[:, 4 : 4 + HPD, :].astype(BF16).reshape(PEERS, COLS)
     full_w = gather_bits(my_w, "dp", (8, 4, 2, 1)).reshape(TEXT, COLS)
-    back, wg = attend(zi, bias, pick, got, full_w)
+    back, wg, tg = attend(zi, bias, pick, got, full_w)
     returned = exchange(back)
-    weight_grad = reduce_weight(wg, xi)
-    attended, query_grad, key_grad, value_grad, text_grad = unpack(
-        msg, dest_row, returned.reshape(NZ, NX, MSG_ROWS, LANES)
+    weight_grad, text_grad = reduce_text(wg, tg, xi)
+    attended, query_grad, key_grad, value_grad = unpack(
+        msg, dest_row, returned.reshape(NZ, NX, BODY_ROWS, LANES)
     )
     return attended, query_grad, key_grad, value_grad, text_grad, weight_grad
 

time: 211 us -> 207 us (0.981)
  the two profiles are of different devices: /device:TPU:2 before, /device:TPU:4 now
where the time goes in v7:
time: 207 us
  waiting for transfers between devices  90.2 us (44%)
  starting transfers between devices  58.8 us (28%)
  blocking collectives  33.9 us (16%)
  Pallas kernels  20 us (10%)
    all_to_all x2, waiting for transfers between devices, exchange(): return lax.all_to_all(x, 'seq', split_axis=0, concat_axis=0, tiled=True)  71.6 us
    ppermute x11, starting transfers between devices, swap(): return lax.ppermute(x, axis, [(j, j ^ bit) for j in range(size)])  45.2 us
    all_to_all x1, blocking collectives, exchange(): return lax.all_to_all(x, 'seq', split_axis=0, concat_axis=0, tiled=True)  22 us
    ppermute x11, waiting for transfers between devices, swap(): return lax.ppermute(x, axis, [(j, j ^ bit) for j in range(size)])  18.6 us
    all_to_all x2, starting transfers between devices, exchange(): return lax.all_to_all(x, 'seq', split_axis=0, concat_axis=0, tiled=True)  13.5 us
    all_to_all x1, blocking collectives, reduce_text(): lax.all_to_all(lines, 'seq', 0, 0, axis_index_groups=groups, tiled=True)  12 us
    pallas_call x1, Pallas kernels, attend(): pl.pallas_call(attend_kernel, grid_spec=pltpu.PrefetchScalarGridSpec(num_...  7.63 us
    pallas_call x1, Pallas kernels, pack(): pl.pallas_call(pack_kernel, grid=(NX,), in_specs=[full((PEERS * 8, LANES)...  5 us
  transfers between devices with their start and end apart: 13, of which 11 were waited for; matrix products, arithmetic and copies ran while one was open for 1% of the time, Pallas kernels for 1%

profile of v7, /device:TPU:4, one launch (start us, length us, event | category | flops | bytes accessed | tf_op | source)
XLA Modules:
  0.0 206.6 jit_solution(16045204062526553906)
XLA Ops:
  0.6 1.4 prep.1
  2.0 22.0 %all_to_all.20 = f32[32,8,128]{2,1,0:T(8,128)} all-to-all(f32[32,8,128]{2,1,0:T(8,128)} %bitcast.59), channel_id=1, replica_groups=mesh['dp'=16,'seq'=32] {'seq'}, dimensions={0} | all-to-all | bytes 262144 | tf_op jit(solution)/shard_map/all_to_all | solution.py:382
  24.0 5.0 %pack.1 = (bf16[8,4,288,128]{3,2,1,0:T(8,128)(2,1)}, f32[24,128]{1,0:T(8,128)}) custom-call(f32[256,128]{1,0:T(8,128)} %bitcast.50, s32[1,128]{1,0:T(1,128)} %bitcast.55, bf16[8,512]{1,0:T(8,128)(2,1)} %text_ref.1, bf16[128,1536]{1,0:T(8,128)(2,1)} %q_ref.1, bf16[128,1536]{1,0:T(8,128)(2,1)} %k_ref.1, bf16[128,1536]{1,0:T(8,128)(2,1)} %v_ref.1, ...), custom_call_target="tpu_custom_call" | custom-call | tf_op jit(solution)/shard_map/pack/pallas_call | solution.py:143
  29.0 6.1 %all-to-all-start.1 = ((bf16[32,288,128]{2,1,0:T(8,128)(2,1)}), bf16[32,288,128]{2,1,0:T(8,128)(2,1)S(1)}, u32[]{:S(2)}, u32[]{:S(2)}) async-start(bf16[32,288,128]{2,1,0:T(8,128)(2,1)} %bitcast.57), calls=%async_computation.1 | async-start | bytes 4718592 | tf_op jit(solution)/shard_map/all_to_all | solution.py:382
  35.2 7.7 %collective-permute-start = (bf16[32,384]{1,0:T(8,128)(2,1)S(1)}, bf16[32,384]{1,0:T(8,128)(2,1)S(1)}, u32[]{:S(2)}, u32[]{:S(2)}) collective-permute-start(bf16[32,384]{1,0:T(8,128)(2,1)S(1)} %bitcast.62), channel_id=1, source_target_pairs={{0,256},{32,288},{64,320},{96,352},{128,384},{160,416},{192,448},{... | collective-permute-start | bytes 73736 | tf_op jit(solution)/shard_map/ppermute | solution.py:387
  43.0 1.9 collective-permute-done
  44.9 4.5 %collective-permute-start.1 = (bf16[2,32,384]{2,1,0:T(8,128)(2,1)S(1)}, bf16[2,32,384]{2,1,0:T(8,128)(2,1)S(1)}, u32[]{:S(2)}, u32[]{:S(2)}) collective-permute-start(bf16[2,32,384]{2,1,0:T(8,128)(2,1)S(1)} %pad_maximum_fusion.3), channel_id=1, source_target_pairs={{0,128},{32,160},{64,192},{96,224},{128,0},{160,32},{192,64},{224,... | collective-permute-start | bytes 147464 | tf_op jit(solution)/shard_map/ppermute | solution.py:387
  49.4 2.3 %collective-permute-done.1 = bf16[2,32,384]{2,1,0:T(8,128)(2,1)S(1)} collective-permute-done((bf16[2,32,384]{2,1,0:T(8,128)(2,1)S(1)}, bf16[2,32,384]{2,1,0:T(8,128)(2,1)S(1)}, u32[]{:S(2)}, u32[]{:S(2)}) %collective-permute-start.1) | collective-permute-done | bytes 49184 | tf_op jit(solution)/shard_map/ppermute | solution.py:387
  51.8 3.5 %collective-permute-start.2 = (bf16[2,2,32,384]{3,2,0,1:T(8,128)(2,1)S(1)}, bf16[2,2,32,384]{3,2,0,1:T(8,128)(2,1)S(1)}, u32[]{:S(2)}, u32[]{:S(2)}) collective-permute-start(bf16[2,2,32,384]{3,2,0,1:T(8,128)(2,1)S(1)} %pad_maximum_fusion.2), channel_id=1, source_target_pairs={{0,64},{32,96},{64,0},{96,32},{128,192},{160,224},{192,128},{224,1... | collective-permute-start | bytes 294920 | tf_op jit(solution)/shard_map/ppermute | solution.py:387
  55.3 3.0 %collective-permute-done.2 = bf16[2,2,32,384]{3,2,0,1:T(8,128)(2,1)S(1)} collective-permute-done((bf16[2,2,32,384]{3,2,0,1:T(8,128)(2,1)S(1)}, bf16[2,2,32,384]{3,2,0,1:T(8,128)(2,1)S(1)}, u32[]{:S(2)}, u32[]{:S(2)}) %collective-permute-start.2) | collective-permute-done | bytes 98336 | tf_op jit(solution)/shard_map/ppermute | solution.py:387
  58.4 1.9 collective-permute-start.3
  60.3 2.1 %setup.1 = (f32[4,256,256]{2,1,0:T(8,128)}, bf16[4,256,256]{2,1,0:T(8,128)(2,1)}) custom-call(s32[1]{0:T(128)} %bitcast.5.z_ref, f32[256,128]{1,0:T(8,128)S(1)} %bitcast.51, f32[24,128]{1,0:T(8,128)S(1)} %copy-done.3), custom_call_target="tpu_custom_call" | custom-call | tf_op jit(solution)/shard_map/setup/pallas_call | solution.py:195
  62.4 1.0 select_bitcast_fusion.1
  63.6 26.7 %all-to-all-done.1.in_ref.tail_ref = bf16[32,288,128]{2,1,0:T(8,128)(2,1)S(1)} async-done(((bf16[32,288,128]{2,1,0:T(8,128)(2,1)}), bf16[32,288,128]{2,1,0:T(8,128)(2,1)S(1)}, u32[]{:S(2)}, u32[]{:S(2)}) %all-to-all-start.1) | async-done | bytes 2359328 | tf_op jit(solution)/shard_map/all_to_all | solution.py:382
  90.3 7.6 %attend.1 = (bf16[32,256,128]{2,1,0:T(8,128)(2,1)}, f32[512,384]{1,0:T(8,128)}, bf16[4,64,512]{2,1,0:T(8,128)(2,1)}) custom-call(s32[1]{0:T(128)} %bitcast.5.z_ref, f32[4,256,256]{2,1,0:T(8,128)} %get-tuple-element.25.mask_ref, bf16[4,256,256]{2,1,0:T(8,128)(2,1)S(1)} %copy-done.1, bf16[32,288,128]{2,1,0:T(8,128)(2,1)S(1)} %all-to-all-done.1.in_ref.tail_ref, ...), custom_call_target="tpu_custom_call" | custom-call | tf_op jit(solution)/shard_map/attend/pallas_call | solution.py:301
  97.9 1.2 fusion.4
  99.2 2.1 collective-permute-start.4
  101.2 1.4 collective-permute-done.4
  102.7 3.5 %collective-permute-start.5 = (bf16[2,2,32,384]{3,2,0,1:T(8,128)(2,1)S(1)}, bf16[2,2,32,384]{3,2,0,1:T(8,128)(2,1)S(1)}, u32[]{:S(2)}, u32[]{:S(2)}) collective-permute-start(bf16[2,2,32,384]{3,2,0,1:T(8,128)(2,1)S(1)} %fusion.1), channel_id=1, source_target_pairs={{0,64},{32,96},{64,0},{96,32},{128,192},{160,224},{192,128},{224,1... | collective-permute-start | bytes 294920 | tf_op jit(solution)/shard_map/ppermute | solution.py:387
  106.2 3.2 %collective-permute-done.5 = bf16[2,2,32,384]{3,2,0,1:T(8,128)(2,1)S(1)} collective-permute-done((bf16[2,2,32,384]{3,2,0,1:T(8,128)(2,1)S(1)}, bf16[2,2,32,384]{3,2,0,1:T(8,128)(2,1)S(1)}, u32[]{:S(2)}, u32[]{:S(2)}) %collective-permute-start.5) | collective-permute-done | bytes 98336 | tf_op jit(solution)/shard_map/ppermute | solution.py:387
  109.5 4.5 %collective-permute-start.6 = (bf16[2,32,384]{2,1,0:T(8,128)(2,1)S(1)}, bf16[2,32,384]{2,1,0:T(8,128)(2,1)S(1)}, u32[]{:S(2)}, u32[]{:S(2)}) collective-permute-start(bf16[2,32,384]{2,1,0:T(8,128)(2,1)S(1)} %fusion.2), channel_id=1, source_target_pairs={{0,128},{32,160},{64,192},{96,224},{128,0},{160,32},{192,64},{224,... | collective-permute-start | bytes 147464 | tf_op jit(solution)/shard_map/ppermute | solution.py:387
  114.0 2.4 %collective-permute-done.6 = bf16[2,32,384]{2,1,0:T(8,128)(2,1)S(1)} collective-permute-done((bf16[2,32,384]{2,1,0:T(8,128)(2,1)S(1)}, bf16[2,32,384]{2,1,0:T(8,128)(2,1)S(1)}, u32[]{:S(2)}, u32[]{:S(2)}) %collective-permute-start.6) | collective-permute-done | bytes 49184 | tf_op jit(solution)/shard_map/ppermute | solution.py:387
  116.4 8.3 %collective-permute-start.7 = (bf16[32,384]{1,0:T(8,128)(2,1)S(1)}, bf16[32,384]{1,0:T(8,128)(2,1)S(1)}, u32[]{:S(2)}, u32[]{:S(2)}) collective-permute-start(bf16[32,384]{1,0:T(8,128)(2,1)S(1)} %fusion.3), channel_id=1, source_target_pairs={{0,256},{32,288},{64,320},{96,352},{128,384},{160,416},{192,448},{... | collective-permute-start | bytes 73736 | tf_op jit(solution)/shard_map/ppermute | solution.py:387
  124.7 1.9 collective-permute-done.7.got_ref
  126.7 3.1 %collective-permute-start.8 = (bf16[80,512]{1,0:T(8,128)(2,1)S(1)}, bf16[80,512]{1,0:T(8,128)(2,1)S(1)}, u32[]{:S(2)}, u32[]{:S(2)}) collective-permute-start(bf16[80,512]{1,0:T(8,128)(2,1)S(1)} %get-tuple-element.37), channel_id=1, source_target_pairs={{0,1},{1,0},{2,3},{3,2},{4,5},{5,4},{6,7},{7,6},{8,9},{9,8},{10,11... | collective-permute-start | bytes 245768 | tf_op jit(solution)/shard_map/ppermute | solution.py:387
  129.8 1.9 collective-permute-start.9
  131.7 4.2 %collective-permute-start.10 = (bf16[80,512]{1,0:T(8,128)(2,1)S(1)}, bf16[80,512]{1,0:T(8,128)(2,1)S(1)}, u32[]{:S(2)}, u32[]{:S(2)}) collective-permute-start(bf16[80,512]{1,0:T(8,128)(2,1)S(1)} %get-tuple-element.39), channel_id=1, source_target_pairs={{0,3},{1,2},{2,1},{3,0},{4,7},{5,6},{6,5},{7,4},{8,11},{9,10},{10,... | collective-permute-start | bytes 245768 | tf_op jit(solution)/shard_map/ppermute | solution.py:387
  135.9 1.7 collective-permute-done.9.refs_1_
  138.6 12.0 %all_to_all.21.in_ref = bf16[8,16,512]{2,1,0:T(8,128)(2,1)S(1)} all-to-all(bf16[8,16,512]{2,1,0:T(8,128)(2,1)S(1)} %shard_map.137), channel_id=1, replica_groups={{0,4,8,12,16,20,24,28},{1,5,9,13,17,21,25,29},{2,6,10,14,18,22,26,30},{..., dimensions={0} | all-to-all | bytes 262144 | tf_op jit(solution)/shard_map/all_to_all | solution.py:472
  150.6 7.4 %all-to-all-start.2 = ((bf16[32,256,128]{2,1,0:T(8,128)(2,1)}), bf16[32,256,128]{2,1,0:T(8,128)(2,1)S(1)}, u32[]{:S(2)}, u32[]{:S(2)}) async-start(bf16[32,256,128]{2,1,0:T(8,128)(2,1)} %get-tuple-element.28), calls=%async_computation.2 | async-start | bytes 4194304 | tf_op jit(solution)/shard_map/all_to_all | solution.py:382
  158.6 44.9 %all-to-all-done.2 = bf16[32,256,128]{2,1,0:T(8,128)(2,1)S(1)} async-done(((bf16[32,256,128]{2,1,0:T(8,128)(2,1)}), bf16[32,256,128]{2,1,0:T(8,128)(2,1)S(1)}, u32[]{:S(2)}, u32[]{:S(2)}) %all-to-all-start.2) | async-done | bytes 2097184 | tf_op jit(solution)/shard_map/all_to_all | solution.py:382
  203.5 3.1 %unpack.1 = (bf16[128,1536]{1,0:T(8,128)(2,1)}, bf16[128,1536]{1,0:T(8,128)(2,1)}, bf16[128,1536]{1,0:T(8,128)(2,1)}, bf16[128,1536]{1,0:T(8,128)(2,1)}) custom-call(f32[256,128]{1,0:T(8,128)S(1)} %bitcast.52, s32[1,128]{1,0:T(1,128)S(1)} %bitcast.56, bf16[8,4,256,128]{3,2,1,0:T(8,128)(2,1)S(1)} %bitcast.49), custom_call_target="tpu_custom_call" | custom-call | tf_op jit(solution)/shard_map/unpack/pallas_call | solution.py:365
  (34 shorter events, 2.1 us)
Async XLA Ops:
  29.0 6.2 %copy-start = (f32[32,8,128]{2,1,0:T(8,128)S(1)}, f32[32,8,128]{2,1,0:T(8,128)}, u32[]{:S(2)}) copy-start(f32[32,8,128]{2,1,0:T(8,128)} %all_to_all.20) | copy-start | bytes 393220
  29.0 31.3 %copy-start.3 = (f32[24,128]{1,0:T(8,128)S(1)}, f32[24,128]{1,0:T(8,128)}, u32[]{:S(2)}) copy-start(f32[24,128]{1,0:T(8,128)} %get-tuple-element.24.own_ref) | copy-start | bytes 36868
  29.0 61.3 %all-to-all-start.1 = ((bf16[32,288,128]{2,1,0:T(8,128)(2,1)}), bf16[32,288,128]{2,1,0:T(8,128)(2,1)S(1)}, u32[]{:S(2)}, u32[]{:S(2)}) async-start(bf16[32,288,128]{2,1,0:T(8,128)(2,1)} %bitcast.57), calls=%async_computation.1 | async-start | bytes 4718592 | tf_op jit(solution)/shard_map/all_to_all | solution.py:382
  35.2 9.6 %collective-permute-start = (bf16[32,384]{1,0:T(8,128)(2,1)S(1)}, bf16[32,384]{1,0:T(8,128)(2,1)S(1)}, u32[]{:S(2)}, u32[]{:S(2)}) collective-permute-start(bf16[32,384]{1,0:T(8,128)(2,1)S(1)} %bitcast.62), channel_id=1, source_target_pairs={{0,256},{32,288},{64,320},{96,352},{128,384},{160,416},{192,448},{... | collective-permute-start | bytes 73736 | tf_op jit(solution)/shard_map/ppermute | solution.py:387
  44.9 6.9 %collective-permute-start.1 = (bf16[2,32,384]{2,1,0:T(8,128)(2,1)S(1)}, bf16[2,32,384]{2,1,0:T(8,128)(2,1)S(1)}, u32[]{:S(2)}, u32[]{:S(2)}) collective-permute-start(bf16[2,32,384]{2,1,0:T(8,128)(2,1)S(1)} %pad_maximum_fusion.3), channel_id=1, source_target_pairs={{0,128},{32,160},{64,192},{96,224},{128,0},{160,32},{192,64},{224,... | collective-permute-start | bytes 147464 | tf_op jit(solution)/shard_map/ppermute | solution.py:387
  51.8 6.5 %collective-permute-start.2 = (bf16[2,2,32,384]{3,2,0,1:T(8,128)(2,1)S(1)}, bf16[2,2,32,384]{3,2,0,1:T(8,128)(2,1)S(1)}, u32[]{:S(2)}, u32[]{:S(2)}) collective-permute-start(bf16[2,2,32,384]{3,2,0,1:T(8,128)(2,1)S(1)} %pad_maximum_fusion.2), channel_id=1, source_target_pairs={{0,64},{32,96},{64,0},{96,32},{128,192},{160,224},{192,128},{224,1... | collective-permute-start | bytes 294920 | tf_op jit(solution)/shard_map/ppermute | solution.py:387
  58.4 4.1 %collective-permute-start.3 = (bf16[2,2,2,32,384]{4,3,0,1,2:T(8,128)(2,1)S(1)}, bf16[2,2,2,32,384]{4,3,0,1,2:T(8,128)(2,1)}, u32[]{:S(2)}, u32[]{:S(2)}) collective-permute-start(bf16[2,2,2,32,384]{4,3,0,1,2:T(8,128)(2,1)S(1)} %pad_maximum_fusion.1), channel_id=1, source_target_pairs={{0,32},{32,0},{64,96},{96,64},{128,160},{160,128},{192,224},{224,1... | collective-permute-start | bytes 589832 | tf_op jit(solution)/shard_map/ppermute | solution.py:387
  62.4 27.9 %copy-start.1 = (bf16[4,256,256]{2,1,0:T(8,128)(2,1)S(1)}, bf16[4,256,256]{2,1,0:T(8,128)(2,1)}, u32[]{:S(2)}) copy-start(bf16[4,256,256]{2,1,0:T(8,128)(2,1)} %get-tuple-element.26.pick_ref) | copy-start | bytes 1572868
  99.1 27.5 %copy-start.2 = (bf16[4,64,512]{2,1,0:T(8,128)(2,1)S(1)}, bf16[4,64,512]{2,1,0:T(8,128)(2,1)}, u32[]{:S(2)}) copy-start(bf16[4,64,512]{2,1,0:T(8,128)(2,1)} %get-tuple-element.34.tg_ref) | copy-start | bytes 786436
  99.2 3.5 %collective-permute-start.4 = (bf16[2,2,2,32,384]{4,3,0,1,2:T(8,128)(2,1)S(1)}, bf16[2,2,2,32,384]{4,3,0,1,2:T(8,128)(2,1)S(1)}, u32[]{:S(2)}, u32[]{:S(2)}) collective-permute-start(bf16[2,2,2,32,384]{4,3,0,1,2:T(8,128)(2,1)S(1)} %fusion), channel_id=1, source_target_pairs={{0,32},{32,0},{64,96},{96,64},{128,160},{160,128},{192,224},{224,1... | collective-permute-start | bytes 589832 | tf_op jit(solution)/shard_map/ppermute | solution.py:387
  102.7 6.7 %collective-permute-start.5 = (bf16[2,2,32,384]{3,2,0,1:T(8,128)(2,1)S(1)}, bf16[2,2,32,384]{3,2,0,1:T(8,128)(2,1)S(1)}, u32[]{:S(2)}, u32[]{:S(2)}) collective-permute-start(bf16[2,2,32,384]{3,2,0,1:T(8,128)(2,1)S(1)} %fusion.1), channel_id=1, source_target_pairs={{0,64},{32,96},{64,0},{96,32},{128,192},{160,224},{192,128},{224,1... | collective-permute-start | bytes 294920 | tf_op jit(solution)/shard_map/ppermute | solution.py:387
  109.5 6.9 %collective-permute-start.6 = (bf16[2,32,384]{2,1,0:T(8,128)(2,1)S(1)}, bf16[2,32,384]{2,1,0:T(8,128)(2,1)S(1)}, u32[]{:S(2)}, u32[]{:S(2)}) collective-permute-start(bf16[2,32,384]{2,1,0:T(8,128)(2,1)S(1)} %fusion.2), channel_id=1, source_target_pairs={{0,128},{32,160},{64,192},{96,224},{128,0},{160,32},{192,64},{224,... | collective-permute-start | bytes 147464 | tf_op jit(solution)/shard_map/ppermute | solution.py:387
  116.4 10.2 %collective-permute-start.7 = (bf16[32,384]{1,0:T(8,128)(2,1)S(1)}, bf16[32,384]{1,0:T(8,128)(2,1)S(1)}, u32[]{:S(2)}, u32[]{:S(2)}) collective-permute-start(bf16[32,384]{1,0:T(8,128)(2,1)S(1)} %fusion.3), channel_id=1, source_target_pairs={{0,256},{32,288},{64,320},{96,352},{128,384},{160,416},{192,448},{... | collective-permute-start | bytes 73736 | tf_op jit(solution)/shard_map/ppermute | solution.py:387
  126.7 9.2 %collective-permute-start.8 = (bf16[80,512]{1,0:T(8,128)(2,1)S(1)}, bf16[80,512]{1,0:T(8,128)(2,1)S(1)}, u32[]{:S(2)}, u32[]{:S(2)}) collective-permute-start(bf16[80,512]{1,0:T(8,128)(2,1)S(1)} %get-tuple-element.37), channel_id=1, source_target_pairs={{0,1},{1,0},{2,3},{3,2},{4,5},{5,4},{6,7},{7,6},{8,9},{9,8},{10,11... | collective-permute-start | bytes 245768 | tf_op jit(solution)/shard_map/ppermute | solution.py:387
  129.8 7.9 %collective-permute-start.9 = (bf16[80,512]{1,0:T(8,128)(2,1)S(1)}, bf16[80,512]{1,0:T(8,128)(2,1)S(1)}, u32[]{:S(2)}, u32[]{:S(2)}) collective-permute-start(bf16[80,512]{1,0:T(8,128)(2,1)S(1)} %get-tuple-element.38), channel_id=1, source_target_pairs={{0,2},{1,3},{2,0},{3,1},{4,6},{5,7},{6,4},{7,5},{8,10},{9,11},{10,... | collective-permute-start | bytes 245768 | tf_op jit(solution)/shard_map/ppermute | solution.py:387
  131.7 6.8 %collective-permute-start.10 = (bf16[80,512]{1,0:T(8,128)(2,1)S(1)}, bf16[80,512]{1,0:T(8,128)(2,1)S(1)}, u32[]{:S(2)}, u32[]{:S(2)}) collective-permute-start(bf16[80,512]{1,0:T(8,128)(2,1)S(1)} %get-tuple-element.39), channel_id=1, source_target_pairs={{0,3},{1,2},{2,1},{3,0},{4,7},{5,6},{6,5},{7,4},{8,11},{9,10},{10,... | collective-permute-start | bytes 245768 | tf_op jit(solution)/shard_map/ppermute | solution.py:387
  138.6 64.9 %copy-start.4 = (s32[128]{0:T(128)S(1)}, s32[128]{0:T(128)}, u32[]{:S(2)}) copy-start(s32[128]{0:T(128)} %param.15) | copy-start | bytes 1540
  150.6 52.9 %all-to-all-start.2 = ((bf16[32,256,128]{2,1,0:T(8,128)(2,1)}), bf16[32,256,128]{2,1,0:T(8,128)(2,1)S(1)}, u32[]{:S(2)}, u32[]{:S(2)}) async-start(bf16[32,256,128]{2,1,0:T(8,128)(2,1)} %get-tuple-element.28), calls=%async_computation.2 | async-start | bytes 4194304 | tf_op jit(solution)/shard_map/all_to_all | solution.py:382
